TPU v7x, 256 devices: a whole 4x4x8 slice. The times are simulated.
256 devices in a mesh: req: 32 (over z, y), mdl: 8 (over x, core).
Axes of the slice: x: 4, y: 4, z: 8, core: 2. Of those that a mesh axis runs over, the one named last changes fastest.
Arguments:
- stream: bfloat16 [24576, 1792], P('req'), may hold values from -6 to 6
- attention_projection_weight: bfloat16 [3, 1792, 1792], P(None, 'mdl'), may hold values from -0.125 to 0.125
- head_output_weight: bfloat16 [1792, 1792], P('mdl'), may hold values from -0.125 to 0.125
- adapter_down_maps: bfloat16 [64, 1792, 16], P('mdl'), may hold values from -0.125 to 0.125
- adapter_up_maps: bfloat16 [2, 1792, 1024], P(None, 'mdl'), may hold values from -1.5 to 1.5
- tenant_adapter_scale: float32 [4], replicated, may hold values from 0.5 to 2
- feedforward_norm_gain: bfloat16 [1792], replicated, may hold values from 0.099609375 to 1.8984375
- feedforward_weight: bfloat16 [3, 1792, 4864], P(None, 'req', 'mdl'), may hold values from -0.125 to 0.125
- prefix_cache_store: bfloat16 [1024, 2, 1792, 128], P('req', None, 'mdl'), may hold values from -140 to 140
- token_adapter_index: int32 [24576], P('req'), may hold values from 0 to 63
- request_token_lengths: int32 [32, 24], P('req'), may hold values from 1 to 192, 768 in all within a row
- request_tenant_index: int32 [768], P('req'), may hold values from 0 to 3
- last_page_holder: int32 [768, 1], replicated, may hold values from 0 to 31; in each aligned block of 24 rows (0 to 23, 24 to 47, ...) at most 2 rows name the same one
- holder_page_slot: int32 [768], replicated, may hold values from 0 to 31
- page_filled_rows: int32 [768], replicated, may hold values from 64 to 128
Outputs:
- layer_out: bfloat16 [24576, 1792], P(('req', 'mdl'))
Inputs may be any that keep to these rules, and one draw needn't show every extreme that they name: `last_page_holder`: within the rows of one index of req (aligned blocks of 24 rows) no holder is named more than 2 times, and one holder exactly 2 times in some blocks. `request_token_lengths`: each row sums to 768; its longest request has exactly 192 tokens.
All inputs are finite; a program needn't handle non-finite values.
Results may differ from a plain program's by a relative error of at most 0.025.
Values may be sent and summed in bfloat16 or wider, within the bound.
A program may use at most 128 MiB of HBM per device.

v0:
```python
import math

import jax
import jax.numpy as jnp
from jax import lax
from jax.sharding import PartitionSpec as P

HEAD_SIZE = 112
WINDOW = 64


def window_cols(one_page, fill_rows):
    return lax.dynamic_slice_in_dim(one_page, fill_rows - WINDOW, WINDOW, 2)


def per_device(
    stream,
    attention_projection_weight,
    head_output_weight,
    adapter_down_maps,
    adapter_up_maps,
    tenant_adapter_scale,
    feedforward_norm_gain,
    feedforward_weight,
    prefix_cache_store,
    token_adapter_index,
    request_token_lengths,
    request_tenant_index,
    last_page_holder,
    holder_page_slot,
    page_filled_rows,
):
    tok_count, model_width = stream.shape
    head_column_set = attention_projection_weight.shape[1]
    head_local = head_column_set // HEAD_SIZE
    req_per_dev = request_token_lengths.shape[1]
    rank_total_width = adapter_down_maps.shape[2]
    adapter_number = adapter_up_maps.shape[2] // rank_total_width
    req_devices = lax.axis_size("req")
    req_index = lax.axis_index("req")
    mdl_index = lax.axis_index("mdl")
    row_share = tok_count // lax.axis_size("mdl")
    cap_slots = max(2, (req_per_dev + req_devices - 1) // req_devices + 1)
    projected_rows = jnp.einsum(
        "td,kcd->ktc", stream, attention_projection_weight, preferred_element_type=jnp.float32
    )
    all_onehot = (
        token_adapter_index[:, None] == jnp.arange(adapter_number, dtype=jnp.int32)[None, :]
    )
    holder_count = adapter_down_maps.shape[0]
    holder_rank_rows = jnp.einsum(
        "qf,kfn->qkn", stream, adapter_down_maps, preferred_element_type=jnp.float32
    )
    held_onehot = (
        token_adapter_index[:, None]
        == (mdl_index * holder_count + jnp.arange(holder_count, dtype=jnp.int32))[None, :]
    )
    rank_part = jnp.sum(holder_rank_rows * held_onehot.astype(jnp.float32)[:, :, None], axis=1)
    rank_feat = lax.psum(rank_part.astype(jnp.bfloat16), "mdl")
    broadcast_result = (
        all_onehot.astype(jnp.bfloat16)[:, :, None] * rank_feat[:, None, :]
    ).reshape(tok_count, adapter_number * rank_total_width)
    adapter_column_set = jnp.einsum(
        "iu,pdu->ipd", broadcast_result, adapter_up_maps, preferred_element_type=jnp.float32
    )
    positions = jnp.arange(tok_count, dtype=jnp.int32)
    lengths_row = request_token_lengths[0]
    starts = jnp.cumsum(lengths_row) - lengths_row
    member = (positions[:, None] >= starts[None, :]) & (
        positions[:, None] < (starts + lengths_row)[None, :]
    )
    member_int = member.astype(jnp.int32)
    request_of = jnp.sum(member_int * jnp.arange(req_per_dev, dtype=jnp.int32)[None, :], axis=1)
    relative = positions - jnp.sum(member_int * starts[None, :], axis=1)
    tenant_hot = (
        request_tenant_index[:, None]
        == jnp.arange(tenant_adapter_scale.shape[0], dtype=jnp.int32)[None, :]
    ).astype(jnp.float32)
    request_scale = jnp.sum(tenant_hot * tenant_adapter_scale[None, :], axis=1)
    per_token_scale = jnp.sum(member.astype(jnp.float32) * request_scale[None, :], axis=1)[:, None]
    query_rows = (projected_rows[0] + per_token_scale * adapter_column_set[:, 0]).astype(
        jnp.bfloat16
    )
    key_rows = projected_rows[1].astype(jnp.bfloat16)
    value_row_block = (projected_rows[2] + per_token_scale * adapter_column_set[:, 1]).astype(
        jnp.bfloat16
    )
    owner_column = last_page_holder[:, 0]
    owner_table = owner_column.reshape(req_devices, req_per_dev)
    slot_table = holder_page_slot.reshape(req_devices, req_per_dev)
    owned = (owner_table == req_index).astype(jnp.int32)
    owned_rank = jnp.cumsum(owned, axis=1) - 1
    picked = owned[:, None, :] * (
        owned_rank[:, None, :] == jnp.arange(cap_slots, dtype=jnp.int32)[None, :, None]
    ).astype(jnp.int32)
    send_slot = jnp.sum(picked * slot_table[:, None, :], axis=2)
    my_owner = lax.dynamic_slice_in_dim(owner_column, req_index * req_per_dev, req_per_dev, 0)
    my_fill = lax.dynamic_slice_in_dim(page_filled_rows, req_index * req_per_dev, req_per_dev, 0)
    order_ids = jnp.arange(req_per_dev, dtype=jnp.int32)
    earlier = (my_owner[:, None] == my_owner[None, :]) & (order_ids[:, None] > order_ids[None, :])
    flat_pick = my_owner * cap_slots + jnp.sum(earlier.astype(jnp.int32), axis=1)
    source_pages = jnp.take(prefix_cache_store, send_slot, axis=0)
    page_inner = prefix_cache_store.shape[1:]
    arrived = lax.all_to_all(source_pages, "req", split_axis=0, concat_axis=0, tiled=True)
    chosen = jnp.take(arrived.reshape((req_devices * cap_slots,) + page_inner), flat_pick, axis=0)
    prefix_cols = jax.vmap(window_cols)(chosen, my_fill)
    prefix = jnp.transpose(prefix_cols, (0, 3, 1, 2))
    key_all = jnp.concatenate(
        [key_rows, prefix[:, :, 0].reshape(req_per_dev * WINDOW, head_column_set)], axis=0
    )
    value_all = jnp.concatenate(
        [value_row_block, prefix[:, :, 1].reshape(req_per_dev * WINDOW, head_column_set)], axis=0
    )
    distance = positions[:, None] - positions[None, :]
    local_ok = (request_of[:, None] == request_of[None, :]) & (distance >= 0) & (distance <= WINDOW)
    key_request = jnp.repeat(jnp.arange(req_per_dev, dtype=jnp.int32), WINDOW)
    key_offset = jnp.tile(jnp.arange(WINDOW, dtype=jnp.int32), req_per_dev)
    prefix_ok = (request_of[:, None] == key_request[None, :]) & (
        key_offset[None, :] >= relative[:, None]
    )
    allowed = jnp.concatenate([local_ok, prefix_ok], axis=1)
    query_heads = query_rows.reshape(tok_count, head_local, HEAD_SIZE)
    key_heads = key_all.reshape(-1, head_local, HEAD_SIZE)
    value_heads = value_all.reshape(-1, head_local, HEAD_SIZE)
    scores = jnp.einsum(
        "thd,shd->hts", query_heads, key_heads, preferred_element_type=jnp.float32
    ) * (1.0 / math.sqrt(HEAD_SIZE))
    masked = jnp.where(allowed[None], scores, -1e30)
    row_max = jnp.max(masked, axis=-1, keepdims=True)
    exp_scores = jnp.exp(masked - row_max)
    weights = (exp_scores / jnp.sum(exp_scores, axis=-1, keepdims=True)).astype(jnp.bfloat16)
    mixed = (
        jnp.einsum("hts,shd->thd", weights, value_heads, preferred_element_type=jnp.float32)
        .astype(jnp.bfloat16)
        .reshape(tok_count, head_column_set)
    )
    attn_part = (
        jnp.dot(mixed, head_output_weight, preferred_element_type=jnp.float32)
        .astype(jnp.bfloat16)
        .astype(jnp.float32)
    )
    gain_wide = feedforward_norm_gain.astype(jnp.float32)[None, :]
    attn_full = lax.psum(attn_part.astype(jnp.bfloat16), "mdl").astype(jnp.float32)
    resid_full = (stream.astype(jnp.float32) + attn_full).astype(jnp.bfloat16)
    resid_wide = resid_full.astype(jnp.float32)
    mean_sq = jnp.mean(resid_wide * resid_wide, axis=1, keepdims=True)
    normed = (resid_wide * lax.rsqrt(mean_sq + 1e-06) * gain_wide).astype(jnp.bfloat16)
    resid_mine = lax.dynamic_slice_in_dim(resid_full, mdl_index * row_share, row_share, 0)
    full_mlp = lax.all_gather(feedforward_weight, "req", axis=1, tiled=True)
    gate_part = jnp.dot(normed, full_mlp[0], preferred_element_type=jnp.float32)
    up_part = jnp.dot(normed, full_mlp[1], preferred_element_type=jnp.float32)
    hidden = (jax.nn.silu(gate_part) * up_part).astype(jnp.bfloat16)
    mlp_part = (
        jnp.einsum("tf,df->td", hidden, full_mlp[2], preferred_element_type=jnp.float32)
        .astype(jnp.bfloat16)
        .astype(jnp.float32)
    )
    mlp_mine = lax.psum_scatter(
        mlp_part.astype(jnp.bfloat16), "mdl", scatter_dimension=0, tiled=True
    ).astype(jnp.float32)
    return (resid_mine.astype(jnp.float32) + mlp_mine).astype(jnp.bfloat16)


def solution(mesh):
    return jax.shard_map(
        per_device,
        mesh=mesh,
        in_specs=(
            P("req", None),
            P(None, "mdl", None),
            P("mdl", None),
            P("mdl", None, None),
            P(None, "mdl", None),
            P(),
            P(),
            P(None, "req", "mdl"),
            P("req", None, "mdl", None),
            P("req"),
            P("req", None),
            P("req"),
            P(),
            P(),
            P(),
        ),
        out_specs=P(("req", "mdl"), None),
        check_vma=False,
    )
```

profile of v0, /device:TPU:8, one launch (start us, length us, event | category | flops | bytes accessed | tf_op | source)
XLA Modules:
  0.0 413.7 jit_solution(9208175052067111481)
XLA Ops:
  7.4 0.8 fusion.34
  8.4 0.2 reduce_window_sum.18
  8.6 0.8 mul.153
  9.5 0.1 copy.34
  9.6 0.1 reshape.179
  9.8 0.1 copy.33
  9.9 6.5 %gather_fusion = bf16[64,2,224,128]{3,2,1,0:T(8,128)(2,1)} fusion(bf16[32,2,224,128]{3,2,1,0:T(8,128)(2,1)} %param.23, s32[1024]{0:T(1024)S(1)} %pad_clamp_fusion.1), kind=kCustom, calls=%fused_computation | custom fusion | bytes 14680320 | tf_op jit(solution)/shard_map/jit(_take)/gather | solution.py:102
  16.4 6.9 %broadcast_select_fusion = bf16[32,2,2,224,128]{4,3,2,1,0:T(8,128)(2,1)} fusion(bf16[32,2,2,224,128]{4,3,2,1,0:T(8,128)(2,1)} %bitcast.74, pred[32,2]{1,0:T(8,128)(4,1)S(1)} %copy.33), kind=kLoop, calls=%fused_computation.8 | loop fusion | flops 3670016 | bytes 14680128 | tf_op jit(solution)/shard_map/jit(_take)/select_n | solution.py:102
  23.2 11.9 %all-to-all-start = ((bf16[32,2,2,224,128]{4,3,2,1,0:T(8,128)(2,1)}), bf16[32,2,2,224,128]{4,3,2,1,0:T(8,128)(2,1)}, u32[]{:S(2)}, u32[]{:S(2)}) async-start(bf16[32,2,2,224,128]{4,3,2,1,0:T(8,128)(2,1)} %broadcast_select_fusion), calls=%async_computation | async-start | bytes 14680064 | tf_op jit(solution)/shard_map/all_to_all | solution.py:104
  35.3 0.1 reduce
  35.6 3.9 fusion.17
  39.5 1.3 copy-done.2
  41.0 2.8 fusion.50
  43.8 26.7 %psum.14 = bf16[768,16]{0,1:T(8,128)(2,1)S(1)} all-reduce(bf16[768,16]{0,1:T(8,128)(2,1)S(1)} %multiply_reduce_fusion), channel_id=1, replica_groups=mesh['req'=32,'mdl'=8] {'mdl'}, use_global_device_ids=true, to_apply=%region_4.5 | all-reduce | flops 12288 | bytes 49152 | tf_op jit(solution)/shard_map/psum | solution.py:59
  70.5 0.8 fusion.37
  71.3 0.2 convert_reduce_fusion
  71.5 0.8 and_bitcast_fusion
  72.4 0.1 select_reduce_fusion.2
  72.5 0.1 select_reduce_fusion.1
  72.6 0.1 broadcast_multiply_fusion
  72.7 1.4 fusion.47
  74.1 2.1 fusion.51
  76.2 0.1 fusion.48
  76.3 0.3 fusion.14
  76.6 1.0 add_convert_fusion.3
  77.7 1.2 compare_and_fusion
  79.0 1.4 pad_add_fusion
  80.3 118.6 %all-to-all-done = bf16[32,2,2,224,128]{4,3,2,1,0:T(8,128)(2,1)} async-done(((bf16[32,2,2,224,128]{4,3,2,1,0:T(8,128)(2,1)}), bf16[32,2,2,224,128]{4,3,2,1,0:T(8,128)(2,1)}, u32[]{:S(2)}, u32[]{:S(2)}) %all-to-all-start) | async-done | bytes 7340064 | tf_op jit(solution)/shard_map/all_to_all | solution.py:104
  198.9 5.7 %gather_fusion.1 = bf16[24,2,224,128]{3,2,1,0:T(8,128)(2,1)} fusion(bf16[64,2,224,128]{3,2,1,0:T(8,128)(2,1)} %bitcast.16, s32[1024]{0:T(1024)S(1)} %pad_clamp_fusion), kind=kCustom, calls=%fused_computation.1 | custom fusion | bytes 5505120 | tf_op jit(solution)/shard_map/jit(_take)/gather | solution.py:105
  204.6 3.7 broadcast_select_fusion.1
  208.3 8.8 %copy.35 = bf16[24,2,224,128]{2,1,0,3:T(2,128)(2,1)} copy(bf16[24,2,224,128]{3,2,1,0:T(8,128)(2,1)} %broadcast_select_fusion.1) | data formatting | bytes 5505024 | tf_op jit(solution)/shard_map/jit(_take)/select_n | solution.py:105
  217.1 8.9 %gather_fusion.2 = bf16[24,2,224,64]{2,1,3,0:T(2,128)(2,1)S(1)} fusion(bf16[24,2,224,128]{2,1,0,3:T(2,128)(2,1)} %copy.35, s32[24]{0:T(128)S(1)} %get-tuple-element.21), kind=kCustom, calls=%fused_computation.2 | custom fusion | bytes 2752896 | tf_op jit(solution)/shard_map/vmap()/gather | solution.py:13
  226.0 6.5 %slice_reduce_fusion.1 = (bf16[24,64,224]{2,1,0:T(8,128)(2,1)S(1)}, bf16[24,64,224]{2,1,0:T(8,128)(2,1)S(1)}) fusion(bf16[24,64,2,224]{3,2,1,0:T(2,128)(2,1)S(1)} %bitcast.75), kind=kLoop, calls=%fused_computation.40 | loop fusion | bytes 2752512 | tf_op jit(solution)/shard_map/slice | solution.py:112
  232.5 0.4 concatenate.23
  232.9 0.6 copy.37
  233.5 0.4 concatenate.20
  233.9 0.6 copy.36
  234.5 9.7 %fusion.49 = (f32[2,768]{1,0:T(2,128)S(1)}, f32[2,768,2304]{2,1,0:T(8,128)}) fusion(pred[768,2304]{1,0:T(8,128)(4,1)} %pad_add_fusion, bf16[768,2,112]{0,2,1:T(8,128)(2,1)S(1)} %copy-done.6, bf16[1536,2,112]{0,2,1:T(8,128)(2,1)S(1)} %copy.37, bf16[768,2,112]{0,2,1:T(8,128)(2,1)S(1)} %bitcast.83), kind=kOutput, calls=%fused_computation.100 | convolution fusion | flops 808945920 | bytes 17307648 | tf_op jit(solution)/shard_map/sub | solution.py:130
  244.2 7.6 %fusion.22 = bf16[2,112,768]{2,1,0:T(8,128)(2,1)S(1)} fusion(f32[2,768,2304]{2,1,0:T(8,128)} %get-tuple-element.20, f32[2,768]{1,0:T(2,128)S(1)} %get-tuple-element.19, bf16[1536,2,112]{0,2,1:T(8,128)(2,1)S(1)} %copy.36, bf16[768,2,112]{0,2,1:T(8,128)(2,1)S(1)} %copy-done.5), kind=kOutput, calls=%fused_computation.41 | convolution fusion | flops 802037760 | bytes 15538176 | tf_op jit(solution)/shard_map/hts,shd->thd/dot_general | solution.py:133
  251.8 2.5 convolution_convert_fusion
  254.4 0.5 all-gather.2.cloned.1.call-update
  255.0 77.6 %all-reduce.3.cloned.1.call-done = bf16[768,1792]{1,0:T(8,128)(2,1)} async-done(((bf16[768,1792]{1,0:T(8,128)(2,1)}), bf16[768,1792]{1,0:T(8,128)(2,1)}) %all-reduce.3.cloned.1.call-update) | async-done | bytes 2752528 | tf_op jit(solution)/shard_map/psum | solution.py:143
  332.6 5.3 %fusion.6 = (f32[768]{0:T(1024)S(1)}, bf16[768,1792]{1,0:T(8,128)(2,1)}) fusion(bf16[768,1792]{1,0:T(8,128)(2,1)} %all-reduce.3.cloned.1.call-done, bf16[768,1792]{1,0:T(8,128)(2,1)} %param.15), kind=kLoop, calls=%fused_computation.16 | loop fusion | flops 9633024 | bytes 8260608 | tf_op jit(solution)/shard_map/reduce_sum | solution.py:146
  338.0 14.1 %all-gather.2.cloned.1.call-done = bf16[3,1792,608]{2,1,0:T(8,128)(2,1)} async-done(((bf16[3,56,608]{2,1,0:T(8,128)(2,1)}), bf16[3,1792,608]{2,1,0:T(8,128)(2,1)}) %all-gather.2.cloned.1.call-update) | async-done | bytes 6537232 | tf_op jit(solution)/shard_map/all_gather | solution.py:149
  352.0 5.8 %fusion.16 = f32[768,608]{0,1:T(8,128)} fusion(bf16[3,1792,608]{2,1,0:T(8,128)(2,1)} %all-gather.2.cloned.1.call-done, bf16[768,1792]{1,0:T(8,128)(2,1)} %get-tuple-element.10, f32[1792]{0:T(1024)S(1)} %convert_element_type.118, f32[768]{0:T(1024)S(1)} %add_rsqrt_fusion), kind=kOutput, calls=%fused_computation.35 | convolution fusion | flops 1679032320 | bytes 6924288 | tf_op jit(solution)/shard_map/dot_general | solution.py:150
  357.9 10.5 %convolution_convert_fusion.1 = bf16[768,1792]{1,0:T(8,128)(2,1)} fusion(bf16[3,1792,608]{2,1,0:T(8,128)(2,1)} %all-gather.2.cloned.1.call-done, f32[768,608]{0,1:T(8,128)} %fusion.16, bf16[768,1792]{1,0:T(8,128)(2,1)} %get-tuple-element.10, f32[1792]{0:T(1024)S(1)} %convert_element_type.118, f32[768]{0:T(1024)S(1)} %add_rsqrt_fusion), kind=kOutput, calls=%fused_computation.22 | convolution fusion | flops 3356737536 | bytes 11970560 | tf_op jit(solution)/shard_map/tf,df->td/dot_general | solution.py:154
  368.5 36.0 %reduce-scatter.2.cloned.1.call-done = bf16[96,1792]{1,0:T(8,128)(2,1)} async-done(((bf16[768,1792]{1,0:T(8,128)(2,1)}), bf16[96,1792]{1,0:T(8,128)(2,1)}) %reduce-scatter.2.cloned.1.call-update) | async-done | bytes 344080 | tf_op jit(solution)/shard_map/reduce_scatter | solution.py:158
  404.4 1.9 add_convert_fusion.1
  (54 shorter events, 1.1 us)
Async XLA Ops:
  7.4 28.2 %copy-start = (bf16[3,224,1792]{2,1,0:T(8,128)(2,1)S(1)}, bf16[3,224,1792]{2,1,0:T(8,128)(2,1)}, u32[]{:S(2)}) copy-start(bf16[3,224,1792]{2,1,0:T(8,128)(2,1)} %param.16) | copy-start | bytes 7225348
  23.2 11.9 %copy-start.9 = (s32[1,24]{1,0:T(1,128)S(1)}, s32[1,24]{1,0:T(1,128)}, u32[]{:S(2)}) copy-start(s32[1,24]{1,0:T(1,128)} %param.25) | copy-start | bytes 292
  23.2 175.7 %all-to-all-start = ((bf16[32,2,2,224,128]{4,3,2,1,0:T(8,128)(2,1)}), bf16[32,2,2,224,128]{4,3,2,1,0:T(8,128)(2,1)}, u32[]{:S(2)}, u32[]{:S(2)}) async-start(bf16[32,2,2,224,128]{4,3,2,1,0:T(8,128)(2,1)} %broadcast_select_fusion), calls=%async_computation | async-start | bytes 14680064 | tf_op jit(solution)/shard_map/all_to_all | solution.py:104
  35.1 297.5 %all-reduce.3.cloned.1.call-start = ((), (), s32[]{:S(2)}) async-start(), calls=%async_computation.2 | async-start | bytes 5505024 | tf_op jit(solution)/shard_map/psum | solution.py:143
  35.6 5.3 %copy-start.7 = (s32[768]{0:T(1024)S(1)}, s32[768]{0:T(1024)}, u32[]{:S(2)}) copy-start(s32[768]{0:T(1024)} %param.24) | copy-start | bytes 9220
  35.6 5.4 %copy-start.4 = (bf16[8,1792,16]{1,2,0:T(8,128)(2,1)S(1)}, bf16[8,1792,16]{1,2,0:T(8,128)(2,1)}, u32[]{:S(2)}) copy-start(bf16[8,1792,16]{1,2,0:T(8,128)(2,1)} %param.18) | copy-start | bytes 1376260
  39.5 1.3 copy-start.2
  40.9 31.4 %copy-start.10 = (f32[4]{0:T(128)S(1)}, f32[4]{0:T(128)}, u32[]{:S(2)}) copy-start(f32[4]{0:T(128)} %param.20) | copy-start | bytes 52
  40.9 31.4 %copy-start.11 = (s32[24]{0:T(128)S(1)}, s32[24]{0:T(128)}, u32[]{:S(2)}) copy-start(s32[24]{0:T(128)} %param.26) | copy-start | bytes 292
  232.9 1.6 copy-start.6
  234.5 9.8 %copy-start.5 = (bf16[768,2,112]{0,2,1:T(8,128)(2,1)S(1)}, bf16[768,2,112]{0,2,1:T(8,128)(2,1)}, u32[]{:S(2)}) copy-start(bf16[768,2,112]{0,2,1:T(8,128)(2,1)} %get-tuple-element.17) | copy-start | bytes 1032196
  244.2 7.6 %copy-start.3 = (bf16[224,1792]{1,0:T(8,128)(2,1)S(1)}, bf16[224,1792]{1,0:T(8,128)(2,1)}, u32[]{:S(2)}) copy-start(bf16[224,1792]{1,0:T(8,128)(2,1)} %param.17) | copy-start | bytes 2408452
  251.8 3.2 copy-start.8
  254.4 97.6 %all-gather.2.cloned.1.call-start = ((), (), s32[]{:S(2)}) async-start(), calls=%async_computation.3 | async-start | bytes 7096320 | tf_op jit(solution)/shard_map/all_gather | solution.py:149
  255.0 149.4 %reduce-scatter.2.cloned.1.call-start = ((), (), s32[]{:S(2)}) async-start(), calls=%async_computation.4 | async-start | bytes 3096576 | tf_op jit(solution)/shard_map/reduce_scatter | solution.py:158
  357.9 48.4 %copy-start.1 = (bf16[3,224,1792]{2,1,0:T(8,128)(2,1)S(1)}, bf16[3,224,1792]{2,1,0:T(8,128)(2,1)}, u32[]{:S(2)}) copy-start(bf16[3,224,1792]{2,1,0:T(8,128)(2,1)} %param.16) | copy-start | bytes 7225348
Sparse Core Ops, SparseCore 0:
  254.5 78.0 all-reduce.2
  368.6 35.7 reduce-scatter.1
Sparse Core Ops, SparseCore 1:
  257.9 94.1 all-gather.1
where the time goes:
time: 415 us; the launch traced here: 414 us
  waiting for transfers between devices  247 us (60%)
  matrix products  45 us (11%)
  local copies, waits for them, and re-layouts  42.8 us (10%)
  blocking collectives  26.7 us (6%)
  other arithmetic  25.3 us (6%)
  between operations  15.2 us (4%)
  starting transfers between devices  12 us (3%)
    all_to_all x1, waiting for transfers between devices, per_device(): lax.all_to_all(source_pages, 'req', split_axis=0, concat_axis=0, tiled=True)  119 us
    psum x1, waiting for transfers between devices, per_device(): lax.psum(attn_part.astype(jnp.bfloat16), 'mdl').astype(jnp.float32)  77.6 us
    reduce_scatter x1, waiting for transfers between devices, per_device(): lax.psum_scatter(mlp_part.astype(jnp.bfloat16), 'mdl', scatter_dimension=...  36 us
    psum x1, blocking collectives, per_device(): rank_feat = lax.psum(rank_part.astype(jnp.bfloat16), 'mdl')  26.7 us
    all_gather x1, waiting for transfers between devices, per_device(): full_mlp = lax.all_gather(feedforward_weight, 'req', axis=1, tiled=True)  14.1 us
    all_to_all x1, starting transfers between devices, per_device(): lax.all_to_all(source_pages, 'req', split_axis=0, concat_axis=0, tiled=True)  11.9 us
    dot_general x1, matrix products, per_device(): jnp.einsum('tf,df->td', hidden, full_mlp[2], preferred_element_type=jnp.f...  10.5 us
    sub x1, matrix products, per_device(): exp_scores = jnp.exp(masked - row_max)  9.74 us
  transfers between devices with their start and end apart: 4, of which 4 were waited for; matrix products, arithmetic and copies ran while one was open for 5% of the time, Pallas kernels for 0%

commit v1 on v0

--- a/solution.py
+++ b/solution.py
@@ -7,10 +7,6 @@
 
 HEAD_SIZE = 112
 WINDOW = 64
-
-
-def window_cols(one_page, fill_rows):
-    return lax.dynamic_slice_in_dim(one_page, fill_rows - WINDOW, WINDOW, 2)
 
 
 def per_device(
@@ -94,17 +90,29 @@
         owned_rank[:, None, :] == jnp.arange(cap_slots, dtype=jnp.int32)[None, :, None]
     ).astype(jnp.int32)
     send_slot = jnp.sum(picked * slot_table[:, None, :], axis=2)
+    fill_table = page_filled_rows.reshape(req_devices, req_per_dev)
+    send_fill = jnp.sum(picked * fill_table[:, None, :], axis=2)
     my_owner = lax.dynamic_slice_in_dim(owner_column, req_index * req_per_dev, req_per_dev, 0)
-    my_fill = lax.dynamic_slice_in_dim(page_filled_rows, req_index * req_per_dev, req_per_dev, 0)
     order_ids = jnp.arange(req_per_dev, dtype=jnp.int32)
     earlier = (my_owner[:, None] == my_owner[None, :]) & (order_ids[:, None] > order_ids[None, :])
     flat_pick = my_owner * cap_slots + jnp.sum(earlier.astype(jnp.int32), axis=1)
-    source_pages = jnp.take(prefix_cache_store, send_slot, axis=0)
-    page_inner = prefix_cache_store.shape[1:]
+    page_inner = prefix_cache_store.shape[1:3]
+
+    def cut_window(slot, fill):
+        return lax.dynamic_slice(
+            prefix_cache_store, (slot, 0, 0, fill - WINDOW), (1,) + page_inner + (WINDOW,)
+        )[0]
+
+    source_pages = jax.vmap(cut_window)(send_slot.reshape(-1), send_fill.reshape(-1))
+    source_pages = source_pages.reshape((req_devices, cap_slots) + page_inner + (WINDOW,))
     arrived = lax.all_to_all(source_pages, "req", split_axis=0, concat_axis=0, tiled=True)
-    chosen = jnp.take(arrived.reshape((req_devices * cap_slots,) + page_inner), flat_pick, axis=0)
-    prefix_cols = jax.vmap(window_cols)(chosen, my_fill)
-    prefix = jnp.transpose(prefix_cols, (0, 3, 1, 2))
+    chosen = jnp.take(
+        arrived.reshape((req_devices * cap_slots,) + page_inner + (WINDOW,)),
+        flat_pick,
+        axis=0,
+        mode="clip",
+    )
+    prefix = jnp.transpose(chosen, (0, 3, 1, 2))
     key_all = jnp.concatenate(
         [key_rows, prefix[:, :, 0].reshape(req_per_dev * WINDOW, head_column_set)], axis=0
     )

time: 415 us -> 326 us (0.79)
  waiting for transfers between devices: 247 us -> 172 us
  other arithmetic: 25.3 us -> 13.9 us
    all_to_all x1, waiting for transfers between devices: 119 us -> 49.7 us  [per_device(): lax.all_to_all(source_pages, 'req', split_axis=0, concat_axis=0, tiled=True)]
    unnamed x24 -> x27, local copies, waits for them, and re-layouts: 1.38 us -> 12.6 us
    select_n x3 -> x0, other arithmetic: 10.6 us -> none  [the longest x2 6.88 us: per_device(): source_pages = jnp.take(prefix_cache_store, send_slot, axis=0)]
    select_n x3 -> x0, local copies, waits for them, and re-layouts: 8.98 us -> none  [the longest x1 8.79 us: per_device(): jnp.take(arrived.reshape((req_devices * cap_slots,) + page_inner), flat_p...]
    slice x1, local copies, waits for them, and re-layouts: 6.48 us -> 0.17 us  [per_device(): prefix[:, :, 1].reshape(req_per_dev * WINDOW, head_column_set)]
    psum x1, waiting for transfers between devices: 77.6 us -> 71.7 us  [per_device(): lax.psum(attn_part.astype(jnp.bfloat16), 'mdl').astype(jnp.float32)]
    all_to_all x0 -> x1, local copies, waits for them, and re-layouts: none -> 5.1 us  [per_device(): lax.all_to_all(source_pages, 'req', split_axis=0, concat_axis=0, tiled=True)]
    gather x3 -> x2, local copies, waits for them, and re-layouts: 21 us -> 17.2 us  [the longest x1 14.4 us: cut_window(): lax.dynamic_slice(prefix_cache_store, (slot, 0, 0, fill - WINDOW), (1,) +...]
  transfers between devices with their start and end apart: 4 -> 4, of which waited for: 4 -> 4; matrix products, arithmetic and copies ran while one was open for 5% -> 6% of each run, Pallas kernels for 0% -> 0%
where the time goes in v1:
time: 326 us
  waiting for transfers between devices  172 us (53%)
  matrix products  43.6 us (13%)
  local copies, waits for them, and re-layouts  42.1 us (13%)
  blocking collectives  26.8 us (8%)
  between operations  15.2 us (5%)
  other arithmetic  13.9 us (4%)
  starting transfers between devices  12.2 us (4%)
    psum x1, waiting for transfers between devices, per_device(): lax.psum(attn_part.astype(jnp.bfloat16), 'mdl').astype(jnp.float32)  71.7 us
    all_to_all x1, waiting for transfers between devices, per_device(): lax.all_to_all(source_pages, 'req', split_axis=0, concat_axis=0, tiled=True)  49.7 us
    reduce_scatter x1, waiting for transfers between devices, per_device(): lax.psum_scatter(mlp_part.astype(jnp.bfloat16), 'mdl', scatter_dimension=...  36 us
    psum x1, blocking collectives, per_device(): rank_feat = lax.psum(rank_part.astype(jnp.bfloat16), 'mdl')  26.8 us
    gather x1, local copies, waits for them, and re-layouts, cut_window(): lax.dynamic_slice(prefix_cache_store, (slot, 0, 0, fill - WINDOW), (1,) +...  14.4 us
    all_gather x1, waiting for transfers between devices, per_device(): full_mlp = lax.all_gather(feedforward_weight, 'req', axis=1, tiled=True)  14.1 us
    unnamed x27, local copies, waits for them, and re-layouts  12.6 us
    all_to_all x1, starting transfers between devices, per_device(): lax.all_to_all(source_pages, 'req', split_axis=0, concat_axis=0, tiled=True)  11.8 us
  transfers between devices with their start and end apart: 4, of which 4 were waited for; matrix products, arithmetic and copies ran while one was open for 6% of the time, Pallas kernels for 0%

profile of v1, /device:TPU:8, one launch (start us, length us, event | category | flops | bytes accessed | tf_op | source)
XLA Modules:
  0.0 325.8 jit_solution(10154584434537367979)
XLA Ops:
  7.4 0.8 fusion.36
  8.4 0.2 reduce_window_sum.18
  8.6 0.8 mul.159
  9.5 0.8 mul.162
  10.5 0.1 add.111
  10.7 0.1 sub.51
  10.9 0.1 reshape.213
  11.0 11.2 %copy.33 = bf16[32,2,224,128]{2,1,0,3:T(2,128)(2,1)} copy(bf16[32,2,224,128]{3,2,1,0:T(8,128)(2,1)} %param.23) | data formatting | bytes 7340032 | tf_op args[8]
  22.2 14.4 %gather_fusion = bf16[64,2,224,64]{2,1,3,0:T(2,128)(2,1)} fusion(bf16[32,2,224,128]{2,1,0,3:T(2,128)(2,1)} %copy.33, s32[64]{0:T(128)S(1)} %fusion.43), kind=kCustom, calls=%fused_computation | custom fusion | bytes 7341056 | tf_op jit(solution)/shard_map/vmap()/gather | solution.py:102
  36.5 11.8 %all-to-all-start = ((bf16[32,2,2,224,64]{3,2,4,1,0:T(2,128)(2,1)}), bf16[32,2,2,224,64]{3,2,4,1,0:T(2,128)(2,1)}, u32[]{:S(2)}, u32[]{:S(2)}) async-start(bf16[32,2,2,224,64]{3,2,4,1,0:T(2,128)(2,1)} %bitcast.72), calls=%async_computation | async-start | bytes 8388608 | tf_op jit(solution)/shard_map/all_to_all | solution.py:108
  48.6 0.1 reduce
  48.8 3.9 %fusion.17 = f32[3,768,224]{1,2,0:T(8,128)S(1)} fusion(bf16[3,224,1792]{2,1,0:T(8,128)(2,1)S(1)} %copy-done, bf16[768,1792]{1,0:T(8,128)(2,1)} %param.15), kind=kOutput, calls=%fused_computation.34 | convolution fusion | flops 1849688064 | bytes 7225344 | tf_op jit(solution)/shard_map/td,kcd->ktc/dot_general | solution.py:40
  52.7 1.4 copy-done.2
  54.3 2.8 fusion.57
  57.1 26.8 %psum.14 = bf16[768,16]{0,1:T(8,128)(2,1)S(1)} all-reduce(bf16[768,16]{0,1:T(8,128)(2,1)S(1)} %multiply_reduce_fusion), channel_id=1, replica_groups=mesh['req'=32,'mdl'=8] {'mdl'}, use_global_device_ids=true, to_apply=%region_4.5 | all-reduce | flops 12288 | bytes 49152 | tf_op jit(solution)/shard_map/psum | solution.py:55
  83.9 0.8 fusion.44
  84.7 0.2 convert_reduce_fusion
  84.9 0.8 fusion.42
  85.7 0.1 select_reduce_fusion.2
  85.8 0.1 select_reduce_fusion.1
  86.0 0.1 broadcast_multiply_fusion
  86.1 1.4 fusion.53
  87.5 0.9 fusion.58
  88.4 0.1 fusion.55
  88.5 0.3 fusion.14
  88.8 1.1 add_convert_fusion.3
  89.9 1.2 compare_and_fusion
  91.2 1.3 pad_add_fusion
  92.5 49.7 %all-to-all-done = bf16[32,2,2,224,64]{3,2,4,1,0:T(2,128)(2,1)} async-done(((bf16[32,2,2,224,64]{3,2,4,1,0:T(2,128)(2,1)}), bf16[32,2,2,224,64]{3,2,4,1,0:T(2,128)(2,1)}, u32[]{:S(2)}, u32[]{:S(2)}) %all-to-all-start) | async-done | bytes 3670048 | tf_op jit(solution)/shard_map/all_to_all | solution.py:108
  142.2 5.1 %copy.34 = bf16[32,2,2,224,64]{3,4,2,1,0:T(8,128)(2,1)} copy(bf16[32,2,2,224,64]{3,2,4,1,0:T(2,128)(2,1)} %all-to-all-done) | data formatting | bytes 7340032 | tf_op jit(solution)/shard_map/all_to_all | solution.py:108
  147.3 2.8 gather_fusion.1
  150.1 0.2 fusion.54
  150.3 0.4 concatenate.26
  150.7 0.6 copy.36
  151.3 0.4 concatenate.23
  151.7 0.6 copy.35
  152.3 9.6 %fusion.56 = (f32[2,768]{1,0:T(2,128)S(1)}, f32[2,768,2304]{2,1,0:T(8,128)}) fusion(pred[768,2304]{1,0:T(8,128)(4,1)} %pad_add_fusion, bf16[768,2,112]{0,2,1:T(8,128)(2,1)S(1)} %copy-done.6, bf16[1536,2,112]{0,2,1:T(8,128)(2,1)S(1)} %copy.36, bf16[768,2,112]{0,2,1:T(8,128)(2,1)S(1)} %bitcast.82), kind=kOutput, calls=%fused_computation.99 | convolution fusion | flops 808945920 | bytes 17307648 | tf_op jit(solution)/shard_map/sub | solution.py:138
  161.9 7.6 %fusion.22 = bf16[2,112,768]{2,1,0:T(8,128)(2,1)S(1)} fusion(f32[2,768,2304]{2,1,0:T(8,128)} %get-tuple-element.22, f32[2,768]{1,0:T(2,128)S(1)} %get-tuple-element.21, bf16[1536,2,112]{0,2,1:T(8,128)(2,1)S(1)} %copy.35, bf16[768,2,112]{0,2,1:T(8,128)(2,1)S(1)} %copy-done.5), kind=kOutput, calls=%fused_computation.36 | convolution fusion | flops 802037760 | bytes 15538176 | tf_op jit(solution)/shard_map/hts,shd->thd/dot_general | solution.py:141
  169.5 2.5 convolution_convert_fusion
  172.1 0.5 all-gather.2.cloned.1.call-update
  172.6 0.3 reduce-scatter.2.cloned.1.call-start
  172.9 71.7 %all-reduce.2.cloned.1.call-done = bf16[768,1792]{1,0:T(8,128)(2,1)} async-done(((bf16[768,1792]{1,0:T(8,128)(2,1)}), bf16[768,1792]{1,0:T(8,128)(2,1)}) %all-reduce.2.cloned.1.call-update) | async-done | bytes 2752528 | tf_op jit(solution)/shard_map/psum | solution.py:151
  244.6 5.3 %fusion.6 = (f32[768]{0:T(1024)S(1)}, bf16[768,1792]{1,0:T(8,128)(2,1)}) fusion(bf16[768,1792]{1,0:T(8,128)(2,1)} %all-reduce.2.cloned.1.call-done, bf16[768,1792]{1,0:T(8,128)(2,1)} %param.15), kind=kLoop, calls=%fused_computation.14 | loop fusion | flops 9633024 | bytes 8260608 | tf_op jit(solution)/shard_map/reduce_sum | solution.py:154
  250.0 14.1 %all-gather.2.cloned.1.call-done = bf16[3,1792,608]{2,1,0:T(8,128)(2,1)} async-done(((bf16[3,56,608]{2,1,0:T(8,128)(2,1)}), bf16[3,1792,608]{2,1,0:T(8,128)(2,1)}) %all-gather.2.cloned.1.call-update) | async-done | bytes 6537232 | tf_op jit(solution)/shard_map/all_gather | solution.py:157
  264.1 5.8 %fusion.16 = f32[768,608]{0,1:T(8,128)} fusion(bf16[3,1792,608]{2,1,0:T(8,128)(2,1)} %all-gather.2.cloned.1.call-done, bf16[768,1792]{1,0:T(8,128)(2,1)} %get-tuple-element.10, f32[1792]{0:T(1024)S(1)} %convert_element_type.118, f32[768]{0:T(1024)S(1)} %add_rsqrt_fusion), kind=kOutput, calls=%fused_computation.32 | convolution fusion | flops 1679032320 | bytes 6924288 | tf_op jit(solution)/shard_map/dot_general | solution.py:158
  269.9 10.5 %convolution_convert_fusion.1 = bf16[768,1792]{1,0:T(8,128)(2,1)} fusion(bf16[3,1792,608]{2,1,0:T(8,128)(2,1)} %all-gather.2.cloned.1.call-done, f32[768,608]{0,1:T(8,128)} %fusion.16, bf16[768,1792]{1,0:T(8,128)(2,1)} %get-tuple-element.10, f32[1792]{0:T(1024)S(1)} %convert_element_type.118, f32[768]{0:T(1024)S(1)} %add_rsqrt_fusion), kind=kOutput, calls=%fused_computation.20 | convolution fusion | flops 3356737536 | bytes 11970560 | tf_op jit(solution)/shard_map/tf,df->td/dot_general | solution.py:162
  280.5 36.0 %reduce-scatter.2.cloned.1.call-done = bf16[96,1792]{1,0:T(8,128)(2,1)} async-done(((bf16[768,1792]{1,0:T(8,128)(2,1)}), bf16[96,1792]{1,0:T(8,128)(2,1)}) %reduce-scatter.2.cloned.1.call-update) | async-done | bytes 344080 | tf_op jit(solution)/shard_map/reduce_scatter | solution.py:166
  316.4 1.9 add_convert_fusion.1
  (58 shorter events, 1.4 us)
Async XLA Ops:
  7.4 41.5 %copy-start = (bf16[3,224,1792]{2,1,0:T(8,128)(2,1)S(1)}, bf16[3,224,1792]{2,1,0:T(8,128)(2,1)}, u32[]{:S(2)}) copy-start(bf16[3,224,1792]{2,1,0:T(8,128)(2,1)} %param.16) | copy-start | bytes 7225348
  36.5 11.9 %copy-start.9 = (s32[1,24]{1,0:T(1,128)S(1)}, s32[1,24]{1,0:T(1,128)}, u32[]{:S(2)}) copy-start(s32[1,24]{1,0:T(1,128)} %param.25) | copy-start | bytes 292
  36.5 105.6 %all-to-all-start = ((bf16[32,2,2,224,64]{3,2,4,1,0:T(2,128)(2,1)}), bf16[32,2,2,224,64]{3,2,4,1,0:T(2,128)(2,1)}, u32[]{:S(2)}, u32[]{:S(2)}) async-start(bf16[32,2,2,224,64]{3,2,4,1,0:T(2,128)(2,1)} %bitcast.72), calls=%async_computation | async-start | bytes 8388608 | tf_op jit(solution)/shard_map/all_to_all | solution.py:108
  48.4 196.3 %all-reduce.2.cloned.1.call-start = ((), (), s32[]{:S(2)}) async-start(), calls=%async_computation.2 | async-start | bytes 5505024 | tf_op jit(solution)/shard_map/psum | solution.py:151
  48.8 5.4 %copy-start.7 = (s32[768]{0:T(1024)S(1)}, s32[768]{0:T(1024)}, u32[]{:S(2)}) copy-start(s32[768]{0:T(1024)} %param.24) | copy-start | bytes 9220
  48.8 5.4 %copy-start.4 = (bf16[8,1792,16]{1,2,0:T(8,128)(2,1)S(1)}, bf16[8,1792,16]{1,2,0:T(8,128)(2,1)}, u32[]{:S(2)}) copy-start(bf16[8,1792,16]{1,2,0:T(8,128)(2,1)} %param.18) | copy-start | bytes 1376260
  52.7 1.4 copy-start.2
  54.2 31.5 %copy-start.11 = (f32[4]{0:T(128)S(1)}, f32[4]{0:T(128)}, u32[]{:S(2)}) copy-start(f32[4]{0:T(128)} %param.20) | copy-start | bytes 52
  54.2 31.5 %copy-start.12 = (s32[24]{0:T(128)S(1)}, s32[24]{0:T(128)}, u32[]{:S(2)}) copy-start(s32[24]{0:T(128)} %param.26) | copy-start | bytes 292
  57.1 30.4 %copy-start.10 = (bf16[2,224,1024]{2,1,0:T(8,128)(2,1)S(1)}, bf16[2,224,1024]{2,1,0:T(8,128)(2,1)}, u32[]{:S(2)}) copy-start(bf16[2,224,1024]{2,1,0:T(8,128)(2,1)} %param.19) | copy-start | bytes 2752516
  150.7 1.6 copy-start.6
  152.3 9.6 %copy-start.5 = (bf16[768,2,112]{0,2,1:T(8,128)(2,1)S(1)}, bf16[768,2,112]{0,2,1:T(8,128)(2,1)}, u32[]{:S(2)}) copy-start(bf16[768,2,112]{0,2,1:T(8,128)(2,1)} %get-tuple-element.17) | copy-start | bytes 1032196
  161.9 7.6 %copy-start.3 = (bf16[224,1792]{1,0:T(8,128)(2,1)S(1)}, bf16[224,1792]{1,0:T(8,128)(2,1)}, u32[]{:S(2)}) copy-start(bf16[224,1792]{1,0:T(8,128)(2,1)} %param.17) | copy-start | bytes 2408452
  169.5 3.4 %copy-start.8 = (bf16[1792]{0:T(1024)(128)(2,1)S(1)}, bf16[1792]{0:T(1024)(128)(2,1)}, u32[]{:S(2)}) copy-start(bf16[1792]{0:T(1024)(128)(2,1)} %param.21) | copy-start | bytes 10756
  172.0 92.0 %all-gather.2.cloned.1.call-start = ((), (), s32[]{:S(2)}) async-start(), calls=%async_computation.3 | async-start | bytes 7096320 | tf_op jit(solution)/shard_map/all_gather | solution.py:157
  172.6 143.8 %reduce-scatter.2.cloned.1.call-start = ((), (), s32[]{:S(2)}) async-start(), calls=%async_computation.4 | async-start | bytes 3096576 | tf_op jit(solution)/shard_map/reduce_scatter | solution.py:166
  269.9 48.4 %copy-start.1 = (bf16[3,224,1792]{2,1,0:T(8,128)(2,1)S(1)}, bf16[3,224,1792]{2,1,0:T(8,128)(2,1)}, u32[]{:S(2)}) copy-start(bf16[3,224,1792]{2,1,0:T(8,128)(2,1)} %param.16) | copy-start | bytes 7225348
Sparse Core Ops, SparseCore 0:
  172.2 72.4 all-reduce.1
  280.6 35.7 reduce-scatter.1
Sparse Core Ops, SparseCore 1:
  175.5 88.5 all-gather.1

commit v2 on v1

--- a/solution.py
+++ b/solution.py
@@ -106,6 +106,8 @@
     source_pages = jax.vmap(cut_window)(send_slot.reshape(-1), send_fill.reshape(-1))
     source_pages = source_pages.reshape((req_devices, cap_slots) + page_inner + (WINDOW,))
     arrived = lax.all_to_all(source_pages, "req", split_axis=0, concat_axis=0, tiled=True)
+    full_mlp = lax.all_gather(feedforward_weight, "req", axis=1, tiled=True)
+    full_mlp, arrived = lax.optimization_barrier((full_mlp, arrived))
     chosen = jnp.take(
         arrived.reshape((req_devices * cap_slots,) + page_inner + (WINDOW,)),
         flat_pick,
@@ -154,7 +156,6 @@
     mean_sq = jnp.mean(resid_wide * resid_wide, axis=1, keepdims=True)
     normed = (resid_wide * lax.rsqrt(mean_sq + 1e-06) * gain_wide).astype(jnp.bfloat16)
     resid_mine = lax.dynamic_slice_in_dim(resid_full, mdl_index * row_share, row_share, 0)
-    full_mlp = lax.all_gather(feedforward_weight, "req", axis=1, tiled=True)
     gate_part = jnp.dot(normed, full_mlp[0], preferred_element_type=jnp.float32)
     up_part = jnp.dot(normed, full_mlp[1], preferred_element_type=jnp.float32)
     hidden = (jax.nn.silu(gate_part) * up_part).astype(jnp.bfloat16)

time: 326 us -> 344 us (1.055)
  waiting for transfers between devices: 172 us -> 191 us
    all_to_all x1, waiting for transfers between devices: 49.7 us -> 81 us  [per_device(): lax.all_to_all(source_pages, 'req', split_axis=0, concat_axis=0, tiled=True)]
    all_gather x1, waiting for transfers between devices: 14.1 us -> 0.01 us  [per_device(): full_mlp = lax.all_gather(feedforward_weight, 'req', axis=1, tiled=True)]
    optimization_barrier x0 -> x1, local copies, waits for them, and re-layouts: none -> 5.1 us  [per_device(): full_mlp, arrived = lax.optimization_barrier((full_mlp, arrived))]
    all_to_all x1 -> x0, local copies, waits for them, and re-layouts: 5.1 us -> none  [per_device(): lax.all_to_all(source_pages, 'req', split_axis=0, concat_axis=0, tiled=True)]
    unnamed x27 -> x29, local copies, waits for them, and re-layouts: 12.6 us -> 14.2 us
  transfers between devices with their start and end apart: 4 -> 4, of which waited for: 4 -> 3; matrix products, arithmetic and copies ran while one was open for 6% -> 13% of each run, Pallas kernels for 0% -> 0%
where the time goes in v2:
time: 344 us; the launch traced here: 343 us
  waiting for transfers between devices  191 us (56%)
  local copies, waits for them, and re-layouts  43.7 us (13%)
  matrix products  42.9 us (12%)
  blocking collectives  26.8 us (8%)
  between operations  13.5 us (4%)
  starting transfers between devices  13.1 us (4%)
  other arithmetic  12.1 us (4%)
    all_to_all x1, waiting for transfers between devices, per_device(): lax.all_to_all(source_pages, 'req', split_axis=0, concat_axis=0, tiled=True)  81 us
    psum x1, waiting for transfers between devices, per_device(): lax.psum(attn_part.astype(jnp.bfloat16), 'mdl').astype(jnp.float32)  72 us
    reduce_scatter x1, waiting for transfers between devices, per_device(): lax.psum_scatter(mlp_part.astype(jnp.bfloat16), 'mdl', scatter_dimension=...  37.4 us
    psum x1, blocking collectives, per_device(): rank_feat = lax.psum(rank_part.astype(jnp.bfloat16), 'mdl')  26.8 us
    gather x1, local copies, waits for them, and re-layouts, cut_window(): lax.dynamic_slice(prefix_cache_store, (slot, 0, 0, fill - WINDOW), (1,) +...  14.5 us
    unnamed x29, local copies, waits for them, and re-layouts  14.2 us
    all_to_all x1, starting transfers between devices, per_device(): lax.all_to_all(source_pages, 'req', split_axis=0, concat_axis=0, tiled=True)  12.8 us
    dot_general x1, matrix products, per_device(): jnp.einsum('tf,df->td', hidden, full_mlp[2], preferred_element_type=jnp.f...  10.6 us
  transfers between devices with their start and end apart: 4, of which 3 were waited for; matrix products, arithmetic and copies ran while one was open for 13% of the time, Pallas kernels for 0%

profile of v2, /device:TPU:8, one launch (start us, length us, event | category | flops | bytes accessed | tf_op | source)
XLA Modules:
  0.0 343.2 jit_solution(13836156589425205847)
XLA Ops:
  6.5 0.7 all-gather.2.cloned.1.call-update
  7.3 0.7 fusion.46
  8.1 0.2 reduce_window_sum.18
  8.4 0.8 mul.159
  9.2 0.8 mul.162
  10.2 0.1 sub.51
  10.4 0.1 reshape.213
  10.6 0.1 add.111
  10.7 11.2 %copy.33 = bf16[32,2,224,128]{2,1,0,3:T(2,128)(2,1)} copy(bf16[32,2,224,128]{3,2,1,0:T(8,128)(2,1)} %param.23) | data formatting | bytes 7340032 | tf_op args[8]
  21.9 14.5 %gather_fusion = bf16[64,2,224,64]{2,1,3,0:T(2,128)(2,1)} fusion(bf16[32,2,224,128]{2,1,0,3:T(2,128)(2,1)} %copy.33, s32[64]{0:T(128)S(1)} %fusion.53), kind=kCustom, calls=%fused_computation | custom fusion | bytes 7341056 | tf_op jit(solution)/shard_map/vmap()/gather | solution.py:102
  36.4 12.8 %all-to-all-start = ((bf16[32,2,2,224,64]{3,2,4,1,0:T(2,128)(2,1)}), bf16[32,2,2,224,64]{3,2,4,1,0:T(2,128)(2,1)}, u32[]{:S(2)}, u32[]{:S(2)}) async-start(bf16[32,2,2,224,64]{3,2,4,1,0:T(2,128)(2,1)} %bitcast.72), calls=%async_computation | async-start | bytes 8388608 | tf_op jit(solution)/shard_map/all_to_all | solution.py:108
  49.4 0.1 reduce
  49.6 3.9 %fusion.23 = f32[3,768,224]{1,2,0:T(8,128)S(1)} fusion(bf16[3,224,1792]{2,1,0:T(8,128)(2,1)S(1)} %copy-done, bf16[768,1792]{1,0:T(8,128)(2,1)} %param.15), kind=kOutput, calls=%fused_computation.37 | convolution fusion | flops 1849688064 | bytes 7225344 | tf_op jit(solution)/shard_map/td,kcd->ktc/dot_general | solution.py:40
  53.6 1.4 copy-done.3
  55.1 2.8 fusion.67
  58.0 26.8 %psum.14 = bf16[768,16]{0,1:T(8,128)(2,1)S(1)} all-reduce(bf16[768,16]{0,1:T(8,128)(2,1)S(1)} %multiply_reduce_fusion), channel_id=1, replica_groups=mesh['req'=32,'mdl'=8] {'mdl'}, use_global_device_ids=true, to_apply=%region_4.5 | all-reduce | flops 12288 | bytes 49152 | tf_op jit(solution)/shard_map/psum | solution.py:55
  84.7 0.8 fusion.54
  85.5 0.2 convert_reduce_fusion
  85.7 0.8 fusion.52
  86.5 0.1 select_reduce_fusion.2
  86.6 0.1 select_reduce_fusion.1
  86.8 0.1 broadcast_multiply_fusion
  86.9 1.4 fusion.63
  88.3 0.9 fusion.68
  89.2 0.1 fusion.65
  89.3 0.3 fusion.14
  89.6 1.1 add_convert_fusion.3
  90.7 1.3 compare_and_fusion
  91.9 1.4 pad_add_fusion
  93.3 81.0 %all-to-all-done = bf16[32,2,2,224,64]{3,2,4,1,0:T(2,128)(2,1)} async-done(((bf16[32,2,2,224,64]{3,2,4,1,0:T(2,128)(2,1)}), bf16[32,2,2,224,64]{3,2,4,1,0:T(2,128)(2,1)}, u32[]{:S(2)}, u32[]{:S(2)}) %all-to-all-start) | async-done | bytes 3670048 | tf_op jit(solution)/shard_map/all_to_all | solution.py:108
  174.3 5.1 %copy.34 = bf16[32,2,2,224,64]{3,4,2,1,0:T(8,128)(2,1)} copy(bf16[32,2,2,224,64]{3,2,4,1,0:T(2,128)(2,1)} %all-to-all-done) | data formatting | bytes 7340032 | tf_op jit(solution)/shard_map/optimization_barrier | solution.py:110
  179.4 2.8 gather_fusion.1
  182.3 0.2 fusion.64
  182.5 0.4 concatenate.23
  182.9 0.6 copy.35
  183.5 0.4 concatenate.26
  183.9 0.6 copy.36
  184.5 9.5 %fusion.66 = (f32[2,768]{1,0:T(2,128)S(1)}, f32[2,768,2304]{2,1,0:T(8,128)}) fusion(pred[768,2304]{1,0:T(8,128)(4,1)} %pad_add_fusion, bf16[768,2,112]{0,2,1:T(8,128)(2,1)S(1)} %copy-done.7, bf16[1536,2,112]{0,2,1:T(8,128)(2,1)S(1)} %copy.36, bf16[768,2,112]{0,2,1:T(8,128)(2,1)S(1)} %bitcast.82), kind=kOutput, calls=%fused_computation.102 | convolution fusion | flops 808945920 | bytes 17307648 | tf_op jit(solution)/shard_map/sub | solution.py:140
  194.1 7.6 %fusion.32 = bf16[2,112,768]{2,1,0:T(8,128)(2,1)S(1)} fusion(f32[2,768,2304]{2,1,0:T(8,128)} %get-tuple-element.26, f32[2,768]{1,0:T(2,128)S(1)} %get-tuple-element.25, bf16[1536,2,112]{0,2,1:T(8,128)(2,1)S(1)} %copy.35, bf16[768,2,112]{0,2,1:T(8,128)(2,1)S(1)} %copy-done.6), kind=kOutput, calls=%fused_computation.39 | convolution fusion | flops 802037760 | bytes 15538176 | tf_op jit(solution)/shard_map/hts,shd->thd/dot_general | solution.py:143
  201.7 2.5 convolution_convert_fusion
  204.2 0.3 reduce-scatter.2.cloned.1.call-start
  204.5 72.0 %all-reduce.2.cloned.1.call-done = bf16[768,1792]{1,0:T(8,128)(2,1)} async-done(((bf16[768,1792]{1,0:T(8,128)(2,1)}), bf16[768,1792]{1,0:T(8,128)(2,1)}) %all-reduce.2.cloned.1.call-update) | async-done | bytes 2752528 | tf_op jit(solution)/shard_map/psum | solution.py:153
  276.5 3.7 %fusion.6 = (f32[768]{0:T(1024)S(1)}, bf16[768,1792]{1,0:T(8,128)(2,1)S(1)}) fusion(bf16[768,1792]{1,0:T(8,128)(2,1)} %all-reduce.2.cloned.1.call-done, bf16[768,1792]{1,0:T(8,128)(2,1)} %param.15), kind=kLoop, calls=%fused_computation.14 | loop fusion | flops 9633024 | bytes 8260608 | tf_op jit(solution)/shard_map/reduce_sum | solution.py:156
  280.2 1.5 copy-done.2
  281.7 5.1 %fusion.18 = f32[768,608]{0,1:T(8,128)} fusion(bf16[3,1792,608]{2,1,0:T(8,128)(2,1)} %all-gather.2.cloned.1.call-done, bf16[768,1792]{1,0:T(8,128)(2,1)S(1)} %get-tuple-element.14, f32[1792]{0:T(1024)S(1)} %convert_element_type.118, f32[768]{0:T(1024)S(1)} %add_rsqrt_fusion), kind=kOutput, calls=%fused_computation.31 | convolution fusion | flops 1679032320 | bytes 6924288 | tf_op jit(solution)/shard_map/dot_general | solution.py:159
  286.8 10.6 %convolution_convert_fusion.1 = bf16[768,1792]{1,0:T(8,128)(2,1)} fusion(bf16[3,1792,608]{2,1,0:T(8,128)(2,1)} %all-gather.2.cloned.1.call-done, f32[768,608]{0,1:T(8,128)} %fusion.18, bf16[768,1792]{1,0:T(8,128)(2,1)} %copy-done.2, f32[1792]{0:T(1024)S(1)} %convert_element_type.118, f32[768]{0:T(1024)S(1)} %add_rsqrt_fusion), kind=kOutput, calls=%fused_computation.20 | convolution fusion | flops 3356737536 | bytes 11970560 | tf_op jit(solution)/shard_map/tf,df->td/dot_general | solution.py:163
  297.4 37.4 %reduce-scatter.2.cloned.1.call-done = bf16[96,1792]{1,0:T(8,128)(2,1)} async-done(((bf16[768,1792]{1,0:T(8,128)(2,1)}), bf16[96,1792]{1,0:T(8,128)(2,1)}) %reduce-scatter.2.cloned.1.call-update) | async-done | bytes 344080 | tf_op jit(solution)/shard_map/reduce_scatter | solution.py:167
  334.8 1.9 add_convert_fusion.1
  (60 shorter events, 1.4 us)
Async XLA Ops:
  6.5 43.1 %copy-start = (bf16[3,224,1792]{2,1,0:T(8,128)(2,1)S(1)}, bf16[3,224,1792]{2,1,0:T(8,128)(2,1)}, u32[]{:S(2)}) copy-start(bf16[3,224,1792]{2,1,0:T(8,128)(2,1)} %param.16) | copy-start | bytes 7225348
  6.5 167.8 %all-gather.2.cloned.1.call-start = ((), (), s32[]{:S(2)}) async-start(), calls=%async_computation.2 | async-start | bytes 7096320 | tf_op jit(solution)/shard_map/all_gather | solution.py:109
  36.4 12.8 %copy-start.10 = (s32[1,24]{1,0:T(1,128)S(1)}, s32[1,24]{1,0:T(1,128)}, u32[]{:S(2)}) copy-start(s32[1,24]{1,0:T(1,128)} %param.25) | copy-start | bytes 292
  36.4 137.9 %all-to-all-start = ((bf16[32,2,2,224,64]{3,2,4,1,0:T(2,128)(2,1)}), bf16[32,2,2,224,64]{3,2,4,1,0:T(2,128)(2,1)}, u32[]{:S(2)}, u32[]{:S(2)}) async-start(bf16[32,2,2,224,64]{3,2,4,1,0:T(2,128)(2,1)} %bitcast.72), calls=%async_computation | async-start | bytes 8388608 | tf_op jit(solution)/shard_map/all_to_all | solution.py:108
  49.2 227.3 %all-reduce.2.cloned.1.call-start = ((), (), s32[]{:S(2)}) async-start(), calls=%async_computation.3 | async-start | bytes 5505024 | tf_op jit(solution)/shard_map/psum | solution.py:153
  49.6 5.4 %copy-start.8 = (s32[768]{0:T(1024)S(1)}, s32[768]{0:T(1024)}, u32[]{:S(2)}) copy-start(s32[768]{0:T(1024)} %param.24) | copy-start | bytes 9220
  49.6 5.4 %copy-start.5 = (bf16[8,1792,16]{1,2,0:T(8,128)(2,1)S(1)}, bf16[8,1792,16]{1,2,0:T(8,128)(2,1)}, u32[]{:S(2)}) copy-start(bf16[8,1792,16]{1,2,0:T(8,128)(2,1)} %param.18) | copy-start | bytes 1376260
  53.6 1.4 copy-start.3
  55.0 31.5 %copy-start.12 = (f32[4]{0:T(128)S(1)}, f32[4]{0:T(128)}, u32[]{:S(2)}) copy-start(f32[4]{0:T(128)} %param.20) | copy-start | bytes 52
  55.0 31.4 %copy-start.13 = (s32[24]{0:T(128)S(1)}, s32[24]{0:T(128)}, u32[]{:S(2)}) copy-start(s32[24]{0:T(128)} %param.26) | copy-start | bytes 292
  57.9 30.4 %copy-start.11 = (bf16[2,224,1024]{2,1,0:T(8,128)(2,1)S(1)}, bf16[2,224,1024]{2,1,0:T(8,128)(2,1)}, u32[]{:S(2)}) copy-start(bf16[2,224,1024]{2,1,0:T(8,128)(2,1)} %param.19) | copy-start | bytes 2752516
  182.9 1.6 copy-start.7
  184.5 9.6 %copy-start.6 = (bf16[768,2,112]{0,2,1:T(8,128)(2,1)S(1)}, bf16[768,2,112]{0,2,1:T(8,128)(2,1)}, u32[]{:S(2)}) copy-start(bf16[768,2,112]{0,2,1:T(8,128)(2,1)} %get-tuple-element.21) | copy-start | bytes 1032196
  194.1 7.6 %copy-start.4 = (bf16[224,1792]{1,0:T(8,128)(2,1)S(1)}, bf16[224,1792]{1,0:T(8,128)(2,1)}, u32[]{:S(2)}) copy-start(bf16[224,1792]{1,0:T(8,128)(2,1)} %param.17) | copy-start | bytes 2408452
  201.6 2.8 copy-start.9
  204.2 130.6 %reduce-scatter.2.cloned.1.call-start = ((), (), s32[]{:S(2)}) async-start(), calls=%async_computation.4 | async-start | bytes 3096576 | tf_op jit(solution)/shard_map/reduce_scatter | solution.py:167
  280.2 1.6 copy-start.2
  286.8 49.9 %copy-start.1 = (bf16[3,224,1792]{2,1,0:T(8,128)(2,1)S(1)}, bf16[3,224,1792]{2,1,0:T(8,128)(2,1)}, u32[]{:S(2)}) copy-start(bf16[3,224,1792]{2,1,0:T(8,128)(2,1)} %param.16) | copy-start | bytes 7225348
Sparse Core Ops, SparseCore 0:
  10.0 159.9 all-gather.1
  204.3 72.1 all-reduce.1
  297.5 37.2 reduce-scatter.1

commit v3 on v1

--- a/solution.py
+++ b/solution.py
@@ -97,22 +97,24 @@
     earlier = (my_owner[:, None] == my_owner[None, :]) & (order_ids[:, None] > order_ids[None, :])
     flat_pick = my_owner * cap_slots + jnp.sum(earlier.astype(jnp.int32), axis=1)
     page_inner = prefix_cache_store.shape[1:3]
-
-    def cut_window(slot, fill):
-        return lax.dynamic_slice(
-            prefix_cache_store, (slot, 0, 0, fill - WINDOW), (1,) + page_inner + (WINDOW,)
-        )[0]
-
-    source_pages = jax.vmap(cut_window)(send_slot.reshape(-1), send_fill.reshape(-1))
-    source_pages = source_pages.reshape((req_devices, cap_slots) + page_inner + (WINDOW,))
+    page_rows = prefix_cache_store.shape[3]
+    pages = jnp.take(prefix_cache_store, send_slot.reshape(-1), axis=0, mode="clip")
+    window_pick = (
+        jnp.arange(page_rows, dtype=jnp.int32)[None, :, None]
+        == (send_fill.reshape(-1)[:, None, None] - WINDOW)
+        + jnp.arange(WINDOW, dtype=jnp.int32)[None, None, :]
+    ).astype(jnp.bfloat16)
+    source_pages = jnp.einsum(
+        "skcr,srj->sjkc", pages, window_pick, preferred_element_type=jnp.float32
+    ).astype(jnp.bfloat16)
+    source_pages = source_pages.reshape((req_devices, cap_slots, WINDOW) + page_inner)
     arrived = lax.all_to_all(source_pages, "req", split_axis=0, concat_axis=0, tiled=True)
-    chosen = jnp.take(
-        arrived.reshape((req_devices * cap_slots,) + page_inner + (WINDOW,)),
+    prefix = jnp.take(
+        arrived.reshape((req_devices * cap_slots, WINDOW) + page_inner),
         flat_pick,
         axis=0,
         mode="clip",
     )
-    prefix = jnp.transpose(chosen, (0, 3, 1, 2))
     key_all = jnp.concatenate(
         [key_rows, prefix[:, :, 0].reshape(req_per_dev * WINDOW, head_column_set)], axis=0
     )

time: 326 us -> 315 us (0.966)
  local copies, waits for them, and re-layouts: 42.1 us -> 17.7 us
  matrix products: 43.6 us -> 56.8 us
    dot_general x0 -> x1, matrix products: none -> 13.2 us  [per_device(): jnp.einsum('skcr,srj->sjkc', pages, window_pick, preferred_element_type=j...]
    unnamed x27 -> x26, local copies, waits for them, and re-layouts: 12.6 us -> 1.37 us
    gather x2, local copies, waits for them, and re-layouts: 17.2 us -> 9.34 us  [the longest x1 6.51 us: per_device(): jnp.take(prefix_cache_store, send_slot.reshape(-1), axis=0, mode='clip')]
    all_to_all x1 -> x0, local copies, waits for them, and re-layouts: 5.1 us -> none  [per_device(): lax.all_to_all(source_pages, 'req', split_axis=0, concat_axis=0, tiled=True)]
  transfers between devices with their start and end apart: 4 -> 4, of which waited for: 4 -> 4; matrix products, arithmetic and copies ran while one was open for 6% -> 7% of each run, Pallas kernels for 0% -> 0%
where the time goes in v3:
time: 315 us
  waiting for transfers between devices  172 us (55%)
  matrix products  56.8 us (18%)
  blocking collectives  26.8 us (9%)
  local copies, waits for them, and re-layouts  17.7 us (6%)
  between operations  15.2 us (5%)
  other arithmetic  14 us (4%)
  starting transfers between devices  12.2 us (4%)
    psum x1, waiting for transfers between devices, per_device(): lax.psum(attn_part.astype(jnp.bfloat16), 'mdl').astype(jnp.float32)  71.7 us
    all_to_all x1, waiting for transfers between devices, per_device(): lax.all_to_all(source_pages, 'req', split_axis=0, concat_axis=0, tiled=True)  49.7 us
    reduce_scatter x1, waiting for transfers between devices, per_device(): lax.psum_scatter(mlp_part.astype(jnp.bfloat16), 'mdl', scatter_dimension=...  36 us
    psum x1, blocking collectives, per_device(): rank_feat = lax.psum(rank_part.astype(jnp.bfloat16), 'mdl')  26.8 us
    all_gather x1, waiting for transfers between devices, per_device(): full_mlp = lax.all_gather(feedforward_weight, 'req', axis=1, tiled=True)  14.1 us
    dot_general x1, matrix products, per_device(): jnp.einsum('skcr,srj->sjkc', pages, window_pick, preferred_element_type=j...  13.2 us
    all_to_all x1, starting transfers between devices, per_device(): lax.all_to_all(source_pages, 'req', split_axis=0, concat_axis=0, tiled=True)  11.9 us
    dot_general x1, matrix products, per_device(): jnp.einsum('tf,df->td', hidden, full_mlp[2], preferred_element_type=jnp.f...  10.5 us
  transfers between devices with their start and end apart: 4, of which 4 were waited for; matrix products, arithmetic and copies ran while one was open for 7% of the time, Pallas kernels for 0%

profile of v3, /device:TPU:8, one launch (start us, length us, event | category | flops | bytes accessed | tf_op | source)
XLA Modules:
  0.0 314.7 jit_solution(2396669354189061754)
XLA Ops:
  7.4 0.8 fusion.39
  8.4 0.2 reduce_window_sum.18
  8.6 0.8 mul.159
  9.5 0.8 mul.162
  10.4 0.1 copy.28
  10.5 0.1 reshape.194
  10.6 0.1 copy.26
  10.7 0.1 sub.51
  10.9 6.5 %gather_fusion = bf16[64,2,224,128]{3,2,1,0:T(8,128)(2,1)} fusion(bf16[32,2,224,128]{3,2,1,0:T(8,128)(2,1)} %param.23, s32[1024]{0:T(1024)S(1)} %pad_clamp_fusion.1), kind=kCustom, calls=%fused_computation | custom fusion | bytes 14680320 | tf_op jit(solution)/shard_map/jit(_take)/gather | solution.py:101
  17.4 13.2 %convolution_convert_fusion.2 = bf16[64,64,2,224]{3,1,2,0:T(8,128)(2,1)} fusion(bf16[64,2,224,128]{3,2,1,0:T(8,128)(2,1)} %gather_fusion, s32[64,64]{1,0:T(8,128)S(1)} %iota_add_fusion), kind=kOutput, calls=%fused_computation.23 | convolution fusion | flops 472121344 | bytes 11026432 | tf_op jit(solution)/shard_map/skcr,srj->sjkc/dot_general | solution.py:107
  30.5 11.9 %all-to-all-start = ((bf16[32,2,64,2,224]{4,2,3,1,0:T(8,128)(2,1)}), bf16[32,2,64,2,224]{4,2,3,1,0:T(8,128)(2,1)}, u32[]{:S(2)}, u32[]{:S(2)}) async-start(bf16[32,2,64,2,224]{4,2,3,1,0:T(8,128)(2,1)} %bitcast.75), calls=%async_computation | async-start | bytes 8388608 | tf_op jit(solution)/shard_map/all_to_all | solution.py:111
  42.6 0.1 reduce
  42.9 3.9 %fusion.19 = f32[3,768,224]{1,2,0:T(8,128)S(1)} fusion(bf16[3,224,1792]{2,1,0:T(8,128)(2,1)S(1)} %copy-done, bf16[768,1792]{1,0:T(8,128)(2,1)} %param.15), kind=kOutput, calls=%fused_computation.37 | convolution fusion | flops 1849688064 | bytes 7225344 | tf_op jit(solution)/shard_map/td,kcd->ktc/dot_general | solution.py:40
  46.8 1.3 copy-done.2
  48.3 2.8 fusion.55
  51.2 26.8 %psum.14 = bf16[768,16]{0,1:T(8,128)(2,1)S(1)} all-reduce(bf16[768,16]{0,1:T(8,128)(2,1)S(1)} %multiply_reduce_fusion), channel_id=1, replica_groups=mesh['req'=32,'mdl'=8] {'mdl'}, use_global_device_ids=true, to_apply=%region_4.5 | all-reduce | flops 12288 | bytes 49152 | tf_op jit(solution)/shard_map/psum | solution.py:55
  78.0 0.8 fusion.42
  78.7 0.2 convert_reduce_fusion
  78.9 0.8 fusion.41
  79.8 0.1 select_reduce_fusion.2
  79.9 0.1 select_reduce_fusion.1
  80.0 0.1 broadcast_multiply_fusion
  80.1 1.4 fusion.51
  81.6 0.9 fusion.56
  82.5 0.1 fusion.53
  82.6 0.3 fusion.14
  82.9 1.0 add_convert_fusion.3
  83.9 1.2 compare_and_fusion
  85.2 1.3 pad_add_fusion
  86.5 49.7 %all-to-all-done = bf16[32,2,64,2,224]{4,2,3,1,0:T(8,128)(2,1)} async-done(((bf16[32,2,64,2,224]{4,2,3,1,0:T(8,128)(2,1)}), bf16[32,2,64,2,224]{4,2,3,1,0:T(8,128)(2,1)}, u32[]{:S(2)}, u32[]{:S(2)}) %all-to-all-start) | async-done | bytes 3670048 | tf_op jit(solution)/shard_map/all_to_all | solution.py:111
  136.2 2.8 gather_fusion.1
  139.1 0.2 fusion.52
  139.2 0.4 concatenate.18
  139.7 0.6 copy.30
  140.3 0.4 concatenate.15
  140.7 0.6 copy.29
  141.3 9.6 %fusion.54 = (f32[2,768]{1,0:T(2,128)S(1)}, f32[2,768,2304]{2,1,0:T(8,128)}) fusion(pred[768,2304]{1,0:T(8,128)(4,1)} %pad_add_fusion, bf16[768,2,112]{0,2,1:T(8,128)(2,1)S(1)} %copy-done.6, bf16[1536,2,112]{0,2,1:T(8,128)(2,1)S(1)} %copy.30, bf16[768,2,112]{0,2,1:T(8,128)(2,1)S(1)} %bitcast.83), kind=kOutput, calls=%fused_computation.97 | convolution fusion | flops 808945920 | bytes 17307648 | tf_op jit(solution)/shard_map/sub | solution.py:140
  150.9 7.6 %fusion.24 = bf16[2,112,768]{2,1,0:T(8,128)(2,1)S(1)} fusion(f32[2,768,2304]{2,1,0:T(8,128)} %get-tuple-element.20, f32[2,768]{1,0:T(2,128)S(1)} %get-tuple-element.19, bf16[1536,2,112]{0,2,1:T(8,128)(2,1)S(1)} %copy.29, bf16[768,2,112]{0,2,1:T(8,128)(2,1)S(1)} %copy-done.5), kind=kOutput, calls=%fused_computation.39 | convolution fusion | flops 802037760 | bytes 15538176 | tf_op jit(solution)/shard_map/hts,shd->thd/dot_general | solution.py:143
  158.4 2.5 convolution_convert_fusion
  161.1 0.5 all-gather.2.cloned.1.call-update
  161.6 0.3 reduce-scatter.2.cloned.1.call-start
  161.9 71.7 %all-reduce.2.cloned.1.call-done = bf16[768,1792]{1,0:T(8,128)(2,1)} async-done(((bf16[768,1792]{1,0:T(8,128)(2,1)}), bf16[768,1792]{1,0:T(8,128)(2,1)}) %all-reduce.2.cloned.1.call-update) | async-done | bytes 2752528 | tf_op jit(solution)/shard_map/psum | solution.py:153
  233.6 5.3 %fusion.6 = (f32[768]{0:T(1024)S(1)}, bf16[768,1792]{1,0:T(8,128)(2,1)}) fusion(bf16[768,1792]{1,0:T(8,128)(2,1)} %all-reduce.2.cloned.1.call-done, bf16[768,1792]{1,0:T(8,128)(2,1)} %param.15), kind=kLoop, calls=%fused_computation.14 | loop fusion | flops 9633024 | bytes 8260608 | tf_op jit(solution)/shard_map/reduce_sum | solution.py:156
  238.9 14.1 %all-gather.2.cloned.1.call-done = bf16[3,1792,608]{2,1,0:T(8,128)(2,1)} async-done(((bf16[3,56,608]{2,1,0:T(8,128)(2,1)}), bf16[3,1792,608]{2,1,0:T(8,128)(2,1)}) %all-gather.2.cloned.1.call-update) | async-done | bytes 6537232 | tf_op jit(solution)/shard_map/all_gather | solution.py:159
  253.0 5.8 %fusion.16 = f32[768,608]{0,1:T(8,128)} fusion(bf16[3,1792,608]{2,1,0:T(8,128)(2,1)} %all-gather.2.cloned.1.call-done, bf16[768,1792]{1,0:T(8,128)(2,1)} %get-tuple-element.10, f32[1792]{0:T(1024)S(1)} %convert_element_type.123, f32[768]{0:T(1024)S(1)} %add_rsqrt_fusion), kind=kOutput, calls=%fused_computation.33 | convolution fusion | flops 1679032320 | bytes 6924288 | tf_op jit(solution)/shard_map/dot_general | solution.py:160
  258.9 10.5 %convolution_convert_fusion.1 = bf16[768,1792]{1,0:T(8,128)(2,1)} fusion(bf16[3,1792,608]{2,1,0:T(8,128)(2,1)} %all-gather.2.cloned.1.call-done, f32[768,608]{0,1:T(8,128)} %fusion.16, bf16[768,1792]{1,0:T(8,128)(2,1)} %get-tuple-element.10, f32[1792]{0:T(1024)S(1)} %convert_element_type.123, f32[768]{0:T(1024)S(1)} %add_rsqrt_fusion), kind=kOutput, calls=%fused_computation.20 | convolution fusion | flops 3356737536 | bytes 11970560 | tf_op jit(solution)/shard_map/tf,df->td/dot_general | solution.py:164
  269.4 36.0 %reduce-scatter.2.cloned.1.call-done = bf16[96,1792]{1,0:T(8,128)(2,1)} async-done(((bf16[768,1792]{1,0:T(8,128)(2,1)}), bf16[96,1792]{1,0:T(8,128)(2,1)}) %reduce-scatter.2.cloned.1.call-update) | async-done | bytes 344080 | tf_op jit(solution)/shard_map/reduce_scatter | solution.py:168
  305.4 1.9 add_convert_fusion.1
  (56 shorter events, 1.2 us)
Async XLA Ops:
  7.4 35.5 %copy-start = (bf16[3,224,1792]{2,1,0:T(8,128)(2,1)S(1)}, bf16[3,224,1792]{2,1,0:T(8,128)(2,1)}, u32[]{:S(2)}) copy-start(bf16[3,224,1792]{2,1,0:T(8,128)(2,1)} %param.16) | copy-start | bytes 7225348
  30.5 11.9 %copy-start.9 = (s32[1,24]{1,0:T(1,128)S(1)}, s32[1,24]{1,0:T(1,128)}, u32[]{:S(2)}) copy-start(s32[1,24]{1,0:T(1,128)} %param.25) | copy-start | bytes 292
  30.5 105.7 %all-to-all-start = ((bf16[32,2,64,2,224]{4,2,3,1,0:T(8,128)(2,1)}), bf16[32,2,64,2,224]{4,2,3,1,0:T(8,128)(2,1)}, u32[]{:S(2)}, u32[]{:S(2)}) async-start(bf16[32,2,64,2,224]{4,2,3,1,0:T(8,128)(2,1)} %bitcast.75), calls=%async_computation | async-start | bytes 8388608 | tf_op jit(solution)/shard_map/all_to_all | solution.py:111
  42.4 191.2 %all-reduce.2.cloned.1.call-start = ((), (), s32[]{:S(2)}) async-start(), calls=%async_computation.2 | async-start | bytes 5505024 | tf_op jit(solution)/shard_map/psum | solution.py:153
  42.9 5.3 %copy-start.7 = (s32[768]{0:T(1024)S(1)}, s32[768]{0:T(1024)}, u32[]{:S(2)}) copy-start(s32[768]{0:T(1024)} %param.24) | copy-start | bytes 9220
  42.9 5.4 %copy-start.4 = (bf16[8,1792,16]{1,2,0:T(8,128)(2,1)S(1)}, bf16[8,1792,16]{1,2,0:T(8,128)(2,1)}, u32[]{:S(2)}) copy-start(bf16[8,1792,16]{1,2,0:T(8,128)(2,1)} %param.18) | copy-start | bytes 1376260
  46.8 1.3 copy-start.2
  48.2 31.5 %copy-start.11 = (f32[4]{0:T(128)S(1)}, f32[4]{0:T(128)}, u32[]{:S(2)}) copy-start(f32[4]{0:T(128)} %param.20) | copy-start | bytes 52
  48.2 31.5 %copy-start.12 = (s32[24]{0:T(128)S(1)}, s32[24]{0:T(128)}, u32[]{:S(2)}) copy-start(s32[24]{0:T(128)} %param.26) | copy-start | bytes 292
  51.1 30.4 %copy-start.10 = (bf16[2,224,1024]{2,1,0:T(8,128)(2,1)S(1)}, bf16[2,224,1024]{2,1,0:T(8,128)(2,1)}, u32[]{:S(2)}) copy-start(bf16[2,224,1024]{2,1,0:T(8,128)(2,1)} %param.19) | copy-start | bytes 2752516
  139.6 1.6 copy-start.6
  141.3 9.6 %copy-start.5 = (bf16[768,2,112]{0,2,1:T(8,128)(2,1)S(1)}, bf16[768,2,112]{0,2,1:T(8,128)(2,1)}, u32[]{:S(2)}) copy-start(bf16[768,2,112]{0,2,1:T(8,128)(2,1)} %get-tuple-element.17) | copy-start | bytes 1032196
  150.9 7.6 %copy-start.3 = (bf16[224,1792]{1,0:T(8,128)(2,1)S(1)}, bf16[224,1792]{1,0:T(8,128)(2,1)}, u32[]{:S(2)}) copy-start(bf16[224,1792]{1,0:T(8,128)(2,1)} %param.17) | copy-start | bytes 2408452
  158.4 3.4 %copy-start.8 = (bf16[1792]{0:T(1024)(128)(2,1)S(1)}, bf16[1792]{0:T(1024)(128)(2,1)}, u32[]{:S(2)}) copy-start(bf16[1792]{0:T(1024)(128)(2,1)} %param.21) | copy-start | bytes 10756
  161.0 92.0 %all-gather.2.cloned.1.call-start = ((), (), s32[]{:S(2)}) async-start(), calls=%async_computation.3 | async-start | bytes 7096320 | tf_op jit(solution)/shard_map/all_gather | solution.py:159
  161.6 143.8 %reduce-scatter.2.cloned.1.call-start = ((), (), s32[]{:S(2)}) async-start(), calls=%async_computation.4 | async-start | bytes 3096576 | tf_op jit(solution)/shard_map/reduce_scatter | solution.py:168
  258.9 48.4 %copy-start.1 = (bf16[3,224,1792]{2,1,0:T(8,128)(2,1)S(1)}, bf16[3,224,1792]{2,1,0:T(8,128)(2,1)}, u32[]{:S(2)}) copy-start(bf16[3,224,1792]{2,1,0:T(8,128)(2,1)} %param.16) | copy-start | bytes 7225348
Sparse Core Ops, SparseCore 0:
  161.1 72.4 all-reduce.1
  269.5 35.7 reduce-scatter.1
Sparse Core Ops, SparseCore 1:
  164.5 88.5 all-gather.1

commit v4 on v3

--- a/solution.py
+++ b/solution.py
@@ -3,10 +3,44 @@
 import jax
 import jax.numpy as jnp
 from jax import lax
+from jax.experimental import pallas as pl
+from jax.experimental.pallas import tpu as pltpu
 from jax.sharding import PartitionSpec as P
 
 HEAD_SIZE = 112
 WINDOW = 64
+
+
+def window_kernel(slot_ref, fill_ref, page_ref, out_ref):
+    start = fill_ref[pl.program_id(0)] - WINDOW
+    page_rows = page_ref.shape[-1]
+    page = page_ref[0].reshape(-1, page_rows)
+    row_ids = lax.broadcasted_iota(jnp.int32, (WINDOW, page_rows), 1)
+    out_ids = lax.broadcasted_iota(jnp.int32, (WINDOW, page_rows), 0)
+    pick = (row_ids == out_ids + start).astype(page.dtype)
+    picked = lax.dot_general(
+        pick, page, (((1,), (1,)), ((), ())), preferred_element_type=jnp.float32
+    )
+    out_ref[0] = picked.astype(out_ref.dtype)
+
+
+def cut_windows(store, slots, fills):
+    count = slots.shape[0]
+    inner = store.shape[1] * store.shape[2]
+    return pl.pallas_call(
+        window_kernel,
+        grid_spec=pltpu.PrefetchScalarGridSpec(
+            num_scalar_prefetch=2,
+            grid=(count,),
+            in_specs=[
+                pl.BlockSpec(
+                    (1,) + store.shape[1:], lambda i, slot_ref, fill_ref: (slot_ref[i], 0, 0, 0)
+                )
+            ],
+            out_specs=pl.BlockSpec((1, WINDOW, inner), lambda i, slot_ref, fill_ref: (i, 0, 0)),
+        ),
+        out_shape=jax.ShapeDtypeStruct((count, WINDOW, inner), store.dtype),
+    )(slots, fills, store)
 
 
 def per_device(
@@ -98,15 +132,11 @@
     flat_pick = my_owner * cap_slots + jnp.sum(earlier.astype(jnp.int32), axis=1)
     page_inner = prefix_cache_store.shape[1:3]
     page_rows = prefix_cache_store.shape[3]
-    pages = jnp.take(prefix_cache_store, send_slot.reshape(-1), axis=0, mode="clip")
-    window_pick = (
-        jnp.arange(page_rows, dtype=jnp.int32)[None, :, None]
-        == (send_fill.reshape(-1)[:, None, None] - WINDOW)
-        + jnp.arange(WINDOW, dtype=jnp.int32)[None, None, :]
-    ).astype(jnp.bfloat16)
-    source_pages = jnp.einsum(
-        "skcr,srj->sjkc", pages, window_pick, preferred_element_type=jnp.float32
-    ).astype(jnp.bfloat16)
+    source_pages = cut_windows(
+        prefix_cache_store,
+        jnp.clip(send_slot.reshape(-1), 0, prefix_cache_store.shape[0] - 1),
+        send_fill.reshape(-1),
+    )
     source_pages = source_pages.reshape((req_devices, cap_slots, WINDOW) + page_inner)
     arrived = lax.all_to_all(source_pages, "req", split_axis=0, concat_axis=0, tiled=True)
     prefix = jnp.take(

time: 315 us -> 347 us (1.10)
  Pallas kernels: 0 us -> 35.5 us
  matrix products: 56.8 us -> 43.6 us
  local copies, waits for them, and re-layouts: 17.7 us -> 25 us
    pallas_call x0 -> x1, Pallas kernels: none -> 35.5 us  [cut_windows(): pl.pallas_call(window_kernel, grid_spec=pltpu.PrefetchScalarGridSpec(num_...]
    dot_general x1 -> x0, matrix products: 13.2 us -> none  [per_device(): jnp.einsum('skcr,srj->sjkc', pages, window_pick, preferred_element_type=j...]
    reshape x1 -> x3, local copies, waits for them, and re-layouts: 0.09 us -> 8.31 us  [the longest x1 7.6 us: per_device(): source_pages.reshape((req_devices, cap_slots, WINDOW) + page_inner)]
    gather x1 -> x0, local copies, waits for them, and re-layouts: 6.51 us -> none  [per_device(): jnp.take(prefix_cache_store, send_slot.reshape(-1), axis=0, mode='clip')]
    all_to_all x0 -> x1, local copies, waits for them, and re-layouts: none -> 5.1 us  [per_device(): lax.all_to_all(source_pages, 'req', split_axis=0, concat_axis=0, tiled=True)]
  transfers between devices with their start and end apart: 4 -> 4, of which waited for: 4 -> 4; matrix products, arithmetic and copies ran while one was open for 7% -> 6% of each run, Pallas kernels for 0% -> 0%
where the time goes in v4:
time: 347 us; the launch traced here: 345 us
  waiting for transfers between devices  172 us (50%)
  matrix products  43.6 us (13%)
  Pallas kernels  35.5 us (10%)
  blocking collectives  26.8 us (8%)
  local copies, waits for them, and re-layouts  25 us (7%)
  between operations  15.2 us (4%)
  other arithmetic  13.9 us (4%)
  starting transfers between devices  13.1 us (4%)
    psum x1, waiting for transfers between devices, per_device(): lax.psum(attn_part.astype(jnp.bfloat16), 'mdl').astype(jnp.float32)  71.7 us
    all_to_all x1, waiting for transfers between devices, per_device(): lax.all_to_all(source_pages, 'req', split_axis=0, concat_axis=0, tiled=True)  49.7 us
    reduce_scatter x1, waiting for transfers between devices, per_device(): lax.psum_scatter(mlp_part.astype(jnp.bfloat16), 'mdl', scatter_dimension=...  36 us
    pallas_call x1, Pallas kernels, cut_windows(): pl.pallas_call(window_kernel, grid_spec=pltpu.PrefetchScalarGridSpec(num_...  35.5 us
    psum x1, blocking collectives, per_device(): rank_feat = lax.psum(rank_part.astype(jnp.bfloat16), 'mdl')  26.8 us
    all_gather x1, waiting for transfers between devices, per_device(): full_mlp = lax.all_gather(feedforward_weight, 'req', axis=1, tiled=True)  14.1 us
    all_to_all x1, starting transfers between devices, per_device(): lax.all_to_all(source_pages, 'req', split_axis=0, concat_axis=0, tiled=True)  12.7 us
    dot_general x1, matrix products, per_device(): jnp.einsum('tf,df->td', hidden, full_mlp[2], preferred_element_type=jnp.f...  10.5 us
  transfers between devices with their start and end apart: 4, of which 4 were waited for; matrix products, arithmetic and copies ran while one was open for 6% of the time, Pallas kernels for 0%

profile of v4, /device:TPU:8, one launch (start us, length us, event | category | flops | bytes accessed | tf_op | source)
XLA Modules:
  0.0 345.0 jit_solution(12429306949122452322)
XLA Ops:
  7.4 0.8 fusion.36
  8.4 0.2 reduce_window_sum.18
  8.6 0.8 mul.159
  9.5 0.8 mul.162
  10.4 0.1 copy.27
  10.5 0.6 min.12.slot_ref
  11.2 0.6 reshape.162.fill_ref
  11.8 35.5 %shard_map.145 = bf16[64,64,448]{2,1,0:T(8,128)(2,1)} custom-call(s32[64]{0:T(128)} %min.12.slot_ref, s32[64]{0:T(128)} %reshape.162.fill_ref, bf16[32,2,224,128]{3,2,1,0:T(8,128)(2,1)} %page_ref.1), custom_call_target="tpu_custom_call" | custom-call | tf_op jit(solution)/shard_map/pallas_call | solution.py:30
  47.3 7.6 %reshape.163 = bf16[32,2,64,2,224]{4,3,2,1,0:T(2,128)(2,1)} reshape(bf16[64,64,448]{2,1,0:T(8,128)(2,1)} %shard_map.145) | data formatting | bytes 7340032 | tf_op jit(solution)/shard_map/reshape | solution.py:140
  54.9 12.7 %all-to-all-start = ((bf16[32,2,64,2,224]{4,3,2,1,0:T(2,128)(2,1)}), bf16[32,2,64,2,224]{4,3,2,1,0:T(2,128)(2,1)}, u32[]{:S(2)}, u32[]{:S(2)}) async-start(bf16[32,2,64,2,224]{4,3,2,1,0:T(2,128)(2,1)} %reshape.163), calls=%async_computation | async-start | bytes 8388608 | tf_op jit(solution)/shard_map/all_to_all | solution.py:141
  67.8 0.1 reduce
  68.1 3.9 %fusion.17 = f32[3,768,224]{1,2,0:T(8,128)S(1)} fusion(bf16[3,224,1792]{2,1,0:T(8,128)(2,1)S(1)} %copy-done, bf16[768,1792]{1,0:T(8,128)(2,1)} %param.15), kind=kOutput, calls=%fused_computation.33 | convolution fusion | flops 1849688064 | bytes 7225344 | tf_op jit(solution)/shard_map/td,kcd->ktc/dot_general | solution.py:74
  72.0 1.4 copy-done.2
  73.5 2.8 fusion.52
  76.4 26.8 %psum.14 = bf16[768,16]{0,1:T(8,128)(2,1)S(1)} all-reduce(bf16[768,16]{0,1:T(8,128)(2,1)S(1)} %multiply_reduce_fusion), channel_id=1, replica_groups=mesh['req'=32,'mdl'=8] {'mdl'}, use_global_device_ids=true, to_apply=%region_4.5 | all-reduce | flops 12288 | bytes 49152 | tf_op jit(solution)/shard_map/psum | solution.py:89
  103.2 0.8 fusion.39
  104.0 0.2 convert_reduce_fusion
  104.1 0.8 fusion.38
  105.0 0.1 select_reduce_fusion.2
  105.1 0.1 select_reduce_fusion.1
  105.3 0.1 broadcast_multiply_fusion
  105.4 1.4 fusion.48
  106.8 0.9 fusion.53
  107.7 0.1 fusion.50
  107.8 0.3 fusion.14
  108.1 1.1 add_convert_fusion.3
  109.2 1.2 compare_and_fusion
  110.4 1.3 pad_add_fusion
  111.8 49.7 %all-to-all-done = bf16[32,2,64,2,224]{4,3,2,1,0:T(2,128)(2,1)} async-done(((bf16[32,2,64,2,224]{4,3,2,1,0:T(2,128)(2,1)}), bf16[32,2,64,2,224]{4,3,2,1,0:T(2,128)(2,1)}, u32[]{:S(2)}, u32[]{:S(2)}) %all-to-all-start) | async-done | bytes 3670048 | tf_op jit(solution)/shard_map/all_to_all | solution.py:141
  161.4 5.1 %copy.30 = bf16[32,2,64,2,224]{4,2,3,1,0:T(8,128)(2,1)} copy(bf16[32,2,64,2,224]{4,3,2,1,0:T(2,128)(2,1)} %all-to-all-done) | data formatting | bytes 7340032 | tf_op jit(solution)/shard_map/all_to_all | solution.py:141
  166.5 2.8 gather_fusion
  169.4 0.2 fusion.49
  169.6 0.4 concatenate.18
  170.0 0.6 copy.32
  170.6 0.4 concatenate.15
  171.0 0.6 copy.31
  171.6 9.6 %fusion.51 = (f32[2,768]{1,0:T(2,128)S(1)}, f32[2,768,2304]{2,1,0:T(8,128)}) fusion(pred[768,2304]{1,0:T(8,128)(4,1)} %pad_add_fusion, bf16[768,2,112]{0,2,1:T(8,128)(2,1)S(1)} %copy-done.6, bf16[1536,2,112]{0,2,1:T(8,128)(2,1)S(1)} %copy.32, bf16[768,2,112]{0,2,1:T(8,128)(2,1)S(1)} %bitcast.76), kind=kOutput, calls=%fused_computation.90 | convolution fusion | flops 808945920 | bytes 17307648 | tf_op jit(solution)/shard_map/sub | solution.py:170
  181.2 7.6 %fusion.22 = bf16[2,112,768]{2,1,0:T(8,128)(2,1)S(1)} fusion(f32[2,768,2304]{2,1,0:T(8,128)} %get-tuple-element.20, f32[2,768]{1,0:T(2,128)S(1)} %get-tuple-element.19, bf16[1536,2,112]{0,2,1:T(8,128)(2,1)S(1)} %copy.31, bf16[768,2,112]{0,2,1:T(8,128)(2,1)S(1)} %copy-done.5), kind=kOutput, calls=%fused_computation.35 | convolution fusion | flops 802037760 | bytes 15538176 | tf_op jit(solution)/shard_map/hts,shd->thd/dot_general | solution.py:173
  188.7 2.5 convolution_convert_fusion
  191.4 0.5 all-gather.2.cloned.1.call-update
  191.9 0.3 reduce-scatter.2.cloned.1.call-start
  192.2 71.7 %all-reduce.2.cloned.1.call-done = bf16[768,1792]{1,0:T(8,128)(2,1)} async-done(((bf16[768,1792]{1,0:T(8,128)(2,1)}), bf16[768,1792]{1,0:T(8,128)(2,1)}) %all-reduce.2.cloned.1.call-update) | async-done | bytes 2752528 | tf_op jit(solution)/shard_map/psum | solution.py:183
  263.9 5.3 %fusion.6 = (f32[768]{0:T(1024)S(1)}, bf16[768,1792]{1,0:T(8,128)(2,1)}) fusion(bf16[768,1792]{1,0:T(8,128)(2,1)} %all-reduce.2.cloned.1.call-done, bf16[768,1792]{1,0:T(8,128)(2,1)} %param.15), kind=kLoop, calls=%fused_computation.13 | loop fusion | flops 9633024 | bytes 8260608 | tf_op jit(solution)/shard_map/reduce_sum | solution.py:186
  269.2 14.1 %all-gather.2.cloned.1.call-done = bf16[3,1792,608]{2,1,0:T(8,128)(2,1)} async-done(((bf16[3,56,608]{2,1,0:T(8,128)(2,1)}), bf16[3,1792,608]{2,1,0:T(8,128)(2,1)}) %all-gather.2.cloned.1.call-update) | async-done | bytes 6537232 | tf_op jit(solution)/shard_map/all_gather | solution.py:189
  283.3 5.8 %fusion.16 = f32[768,608]{0,1:T(8,128)} fusion(bf16[3,1792,608]{2,1,0:T(8,128)(2,1)} %all-gather.2.cloned.1.call-done, bf16[768,1792]{1,0:T(8,128)(2,1)} %get-tuple-element.10, f32[1792]{0:T(1024)S(1)} %convert_element_type.118, f32[768]{0:T(1024)S(1)} %add_rsqrt_fusion), kind=kOutput, calls=%fused_computation.31 | convolution fusion | flops 1679032320 | bytes 6924288 | tf_op jit(solution)/shard_map/dot_general | solution.py:190
  289.2 10.5 %convolution_convert_fusion.1 = bf16[768,1792]{1,0:T(8,128)(2,1)} fusion(bf16[3,1792,608]{2,1,0:T(8,128)(2,1)} %all-gather.2.cloned.1.call-done, f32[768,608]{0,1:T(8,128)} %fusion.16, bf16[768,1792]{1,0:T(8,128)(2,1)} %get-tuple-element.10, f32[1792]{0:T(1024)S(1)} %convert_element_type.118, f32[768]{0:T(1024)S(1)} %add_rsqrt_fusion), kind=kOutput, calls=%fused_computation.19 | convolution fusion | flops 3356737536 | bytes 11970560 | tf_op jit(solution)/shard_map/tf,df->td/dot_general | solution.py:194
  299.7 36.0 %reduce-scatter.2.cloned.1.call-done = bf16[96,1792]{1,0:T(8,128)(2,1)} async-done(((bf16[768,1792]{1,0:T(8,128)(2,1)}), bf16[96,1792]{1,0:T(8,128)(2,1)}) %reduce-scatter.2.cloned.1.call-update) | async-done | bytes 344080 | tf_op jit(solution)/shard_map/reduce_scatter | solution.py:198
  335.7 1.9 add_convert_fusion.1
  (55 shorter events, 1.2 us)
Async XLA Ops:
  7.4 60.7 %copy-start = (bf16[3,224,1792]{2,1,0:T(8,128)(2,1)S(1)}, bf16[3,224,1792]{2,1,0:T(8,128)(2,1)}, u32[]{:S(2)}) copy-start(bf16[3,224,1792]{2,1,0:T(8,128)(2,1)} %param.16) | copy-start | bytes 7225348
  54.9 12.8 %copy-start.9 = (s32[1,24]{1,0:T(1,128)S(1)}, s32[1,24]{1,0:T(1,128)}, u32[]{:S(2)}) copy-start(s32[1,24]{1,0:T(1,128)} %param.25) | copy-start | bytes 292
  54.9 106.6 %all-to-all-start = ((bf16[32,2,64,2,224]{4,3,2,1,0:T(2,128)(2,1)}), bf16[32,2,64,2,224]{4,3,2,1,0:T(2,128)(2,1)}, u32[]{:S(2)}, u32[]{:S(2)}) async-start(bf16[32,2,64,2,224]{4,3,2,1,0:T(2,128)(2,1)} %reshape.163), calls=%async_computation | async-start | bytes 8388608 | tf_op jit(solution)/shard_map/all_to_all | solution.py:141
  67.6 196.2 %all-reduce.2.cloned.1.call-start = ((), (), s32[]{:S(2)}) async-start(), calls=%async_computation.2 | async-start | bytes 5505024 | tf_op jit(solution)/shard_map/psum | solution.py:183
  68.1 5.4 %copy-start.7 = (s32[768]{0:T(1024)S(1)}, s32[768]{0:T(1024)}, u32[]{:S(2)}) copy-start(s32[768]{0:T(1024)} %param.24) | copy-start | bytes 9220
  68.1 5.4 %copy-start.4 = (bf16[8,1792,16]{1,2,0:T(8,128)(2,1)S(1)}, bf16[8,1792,16]{1,2,0:T(8,128)(2,1)}, u32[]{:S(2)}) copy-start(bf16[8,1792,16]{1,2,0:T(8,128)(2,1)} %param.18) | copy-start | bytes 1376260
  72.0 1.4 copy-start.2
  73.4 31.5 %copy-start.11 = (f32[4]{0:T(128)S(1)}, f32[4]{0:T(128)}, u32[]{:S(2)}) copy-start(f32[4]{0:T(128)} %param.20) | copy-start | bytes 52
  73.4 31.5 %copy-start.12 = (s32[24]{0:T(128)S(1)}, s32[24]{0:T(128)}, u32[]{:S(2)}) copy-start(s32[24]{0:T(128)} %param.26) | copy-start | bytes 292
  76.4 30.4 %copy-start.10 = (bf16[2,224,1024]{2,1,0:T(8,128)(2,1)S(1)}, bf16[2,224,1024]{2,1,0:T(8,128)(2,1)}, u32[]{:S(2)}) copy-start(bf16[2,224,1024]{2,1,0:T(8,128)(2,1)} %param.19) | copy-start | bytes 2752516
  170.0 1.6 copy-start.6
  171.6 9.6 %copy-start.5 = (bf16[768,2,112]{0,2,1:T(8,128)(2,1)S(1)}, bf16[768,2,112]{0,2,1:T(8,128)(2,1)}, u32[]{:S(2)}) copy-start(bf16[768,2,112]{0,2,1:T(8,128)(2,1)} %get-tuple-element.17) | copy-start | bytes 1032196
  181.2 7.6 %copy-start.3 = (bf16[224,1792]{1,0:T(8,128)(2,1)S(1)}, bf16[224,1792]{1,0:T(8,128)(2,1)}, u32[]{:S(2)}) copy-start(bf16[224,1792]{1,0:T(8,128)(2,1)} %param.17) | copy-start | bytes 2408452
  188.7 3.4 copy-start.8
  191.3 92.0 %all-gather.2.cloned.1.call-start = ((), (), s32[]{:S(2)}) async-start(), calls=%async_computation.3 | async-start | bytes 7096320 | tf_op jit(solution)/shard_map/all_gather | solution.py:189
  191.9 143.8 %reduce-scatter.2.cloned.1.call-start = ((), (), s32[]{:S(2)}) async-start(), calls=%async_computation.4 | async-start | bytes 3096576 | tf_op jit(solution)/shard_map/reduce_scatter | solution.py:198
  289.2 48.4 %copy-start.1 = (bf16[3,224,1792]{2,1,0:T(8,128)(2,1)S(1)}, bf16[3,224,1792]{2,1,0:T(8,128)(2,1)}, u32[]{:S(2)}) copy-start(bf16[3,224,1792]{2,1,0:T(8,128)(2,1)} %param.16) | copy-start | bytes 7225348
Sparse Core Ops, SparseCore 0:
  191.4 72.4 all-reduce.1
  299.8 35.7 reduce-scatter.1
Sparse Core Ops, SparseCore 1:
  194.8 88.5 all-gather.1

commit v5 on v4

--- a/solution.py
+++ b/solution.py
@@ -11,35 +11,49 @@
 WINDOW = 64
 
 
-def window_kernel(slot_ref, fill_ref, page_ref, out_ref):
-    start = fill_ref[pl.program_id(0)] - WINDOW
-    page_rows = page_ref.shape[-1]
-    page = page_ref[0].reshape(-1, page_rows)
+def window_kernel(slot_ref, fill_ref, store_ref, out_ref, held, sems):
+    count = out_ref.shape[0]
+
+    def fetch(i):
+        return pltpu.make_async_copy(store_ref.at[slot_ref[i]], held.at[i], sems.at[i])
+
+    def start(i, carry):
+        fetch(i).start()
+        return carry
+
+    lax.fori_loop(0, count, start, 0)
+    page_rows = held.shape[-1]
     row_ids = lax.broadcasted_iota(jnp.int32, (WINDOW, page_rows), 1)
     out_ids = lax.broadcasted_iota(jnp.int32, (WINDOW, page_rows), 0)
-    pick = (row_ids == out_ids + start).astype(page.dtype)
-    picked = lax.dot_general(
-        pick, page, (((1,), (1,)), ((), ())), preferred_element_type=jnp.float32
-    )
-    out_ref[0] = picked.astype(out_ref.dtype)
+
+    def pick_rows(i, carry):
+        fetch(i).wait()
+        pick = (row_ids == out_ids + (fill_ref[i] - WINDOW)).astype(held.dtype)
+        for part in range(held.shape[1]):
+            out_ref[i, part] = lax.dot_general(
+                pick, held[i, part], (((1,), (1,)), ((), ())), preferred_element_type=jnp.float32
+            ).astype(out_ref.dtype)
+        return carry
+
+    lax.fori_loop(0, count, pick_rows, 0)
 
 
 def cut_windows(store, slots, fills):
     count = slots.shape[0]
-    inner = store.shape[1] * store.shape[2]
+    parts, width, page_rows = store.shape[1:]
     return pl.pallas_call(
         window_kernel,
         grid_spec=pltpu.PrefetchScalarGridSpec(
             num_scalar_prefetch=2,
-            grid=(count,),
-            in_specs=[
-                pl.BlockSpec(
-                    (1,) + store.shape[1:], lambda i, slot_ref, fill_ref: (slot_ref[i], 0, 0, 0)
-                )
+            grid=(1,),
+            in_specs=[pl.BlockSpec(memory_space=pl.ANY)],
+            out_specs=pl.BlockSpec(memory_space=pltpu.VMEM),
+            scratch_shapes=[
+                pltpu.VMEM((count, parts, width, page_rows), store.dtype),
+                pltpu.SemaphoreType.DMA((count,)),
             ],
-            out_specs=pl.BlockSpec((1, WINDOW, inner), lambda i, slot_ref, fill_ref: (i, 0, 0)),
         ),
-        out_shape=jax.ShapeDtypeStruct((count, WINDOW, inner), store.dtype),
+        out_shape=jax.ShapeDtypeStruct((count, parts, WINDOW, width), store.dtype),
     )(slots, fills, store)
 
 
@@ -137,19 +151,19 @@
         jnp.clip(send_slot.reshape(-1), 0, prefix_cache_store.shape[0] - 1),
         send_fill.reshape(-1),
     )
-    source_pages = source_pages.reshape((req_devices, cap_slots, WINDOW) + page_inner)
+    source_pages = source_pages.reshape((req_devices, cap_slots, 2, WINDOW, head_column_set))
     arrived = lax.all_to_all(source_pages, "req", split_axis=0, concat_axis=0, tiled=True)
     prefix = jnp.take(
-        arrived.reshape((req_devices * cap_slots, WINDOW) + page_inner),
+        arrived.reshape((req_devices * cap_slots, 2, WINDOW, head_column_set)),
         flat_pick,
         axis=0,
         mode="clip",
     )
     key_all = jnp.concatenate(
-        [key_rows, prefix[:, :, 0].reshape(req_per_dev * WINDOW, head_column_set)], axis=0
+        [key_rows, prefix[:, 0].reshape(req_per_dev * WINDOW, head_column_set)], axis=0
     )
     value_all = jnp.concatenate(
-        [value_row_block, prefix[:, :, 1].reshape(req_per_dev * WINDOW, head_column_set)], axis=0
+        [value_row_block, prefix[:, 1].reshape(req_per_dev * WINDOW, head_column_set)], axis=0
     )
     distance = positions[:, None] - positions[None, :]
     local_ok = (request_of[:, None] == request_of[None, :]) & (distance >= 0) & (distance <= WINDOW)

time: 347 us -> 313 us (0.902)
  Pallas kernels: 35.5 us -> 16.5 us
  local copies, waits for them, and re-layouts: 25 us -> 12.3 us
    pallas_call x1, Pallas kernels: 35.5 us -> 16.5 us  [cut_windows(): pl.pallas_call(window_kernel, grid_spec=pltpu.PrefetchScalarGridSpec(num_...]
    reshape x2 -> x1, local copies, waits for them, and re-layouts: 7.69 us -> 0.09 us  [the longest x1 7.6 us: per_device(): source_pages.reshape((req_devices, cap_slots, WINDOW) + page_inner)]
    all_to_all x1 -> x0, local copies, waits for them, and re-layouts: 5.1 us -> none  [per_device(): lax.all_to_all(source_pages, 'req', split_axis=0, concat_axis=0, tiled=True)]
  transfers between devices with their start and end apart: 4 -> 4, of which waited for: 4 -> 4; matrix products, arithmetic and copies ran while one was open for 6% -> 7% of each run, Pallas kernels for 0% -> 0%
where the time goes in v5:
time: 313 us; the launch traced here: 312 us
  waiting for transfers between devices  172 us (55%)
  matrix products  43.6 us (14%)
  blocking collectives  26.8 us (9%)
  Pallas kernels  16.5 us (5%)
  between operations  15.2 us (5%)
  other arithmetic  13.9 us (4%)
  local copies, waits for them, and re-layouts  12.3 us (4%)
  starting transfers between devices  12.1 us (4%)
    psum x1, waiting for transfers between devices, per_device(): lax.psum(attn_part.astype(jnp.bfloat16), 'mdl').astype(jnp.float32)  71.7 us
    all_to_all x1, waiting for transfers between devices, per_device(): lax.all_to_all(source_pages, 'req', split_axis=0, concat_axis=0, tiled=True)  49.6 us
    reduce_scatter x1, waiting for transfers between devices, per_device(): lax.psum_scatter(mlp_part.astype(jnp.bfloat16), 'mdl', scatter_dimension=...  36 us
    psum x1, blocking collectives, per_device(): rank_feat = lax.psum(rank_part.astype(jnp.bfloat16), 'mdl')  26.8 us
    pallas_call x1, Pallas kernels, cut_windows(): pl.pallas_call(window_kernel, grid_spec=pltpu.PrefetchScalarGridSpec(num_...  16.5 us
    all_gather x1, waiting for transfers between devices, per_device(): full_mlp = lax.all_gather(feedforward_weight, 'req', axis=1, tiled=True)  14.1 us
    all_to_all x1, starting transfers between devices, per_device(): lax.all_to_all(source_pages, 'req', split_axis=0, concat_axis=0, tiled=True)  11.8 us
    dot_general x1, matrix products, per_device(): jnp.einsum('tf,df->td', hidden, full_mlp[2], preferred_element_type=jnp.f...  10.5 us
  transfers between devices with their start and end apart: 4, of which 4 were waited for; matrix products, arithmetic and copies ran while one was open for 7% of the time, Pallas kernels for 0%

profile of v5, /device:TPU:8, one launch (start us, length us, event | category | flops | bytes accessed | tf_op | source)
XLA Modules:
  0.0 312.3 jit_solution(3980463654520604639)
XLA Ops:
  7.4 0.8 fusion.36
  8.4 0.2 reduce_window_sum.18
  8.6 0.8 mul.159
  9.5 0.8 mul.162
  10.4 0.1 copy.26
  10.5 0.6 min.12.slot_ref
  11.1 0.1 copy.28
  11.2 0.6 reshape.162.fill_ref
  11.8 16.5 %shard_map.145 = bf16[64,2,64,224]{3,2,1,0:T(8,128)(2,1)} custom-call(s32[64]{0:T(128)} %min.12.slot_ref, s32[64]{0:T(128)} %reshape.162.fill_ref, bf16[32,2,224,128]{3,2,1,0:T(8,128)(2,1)} %store_ref.1), custom_call_target="tpu_custom_call" | custom-call | tf_op jit(solution)/shard_map/pallas_call | solution.py:44
  28.3 11.8 %all-to-all-start = ((bf16[32,2,2,64,224]{4,3,2,1,0:T(8,128)(2,1)}), bf16[32,2,2,64,224]{4,3,2,1,0:T(8,128)(2,1)}, u32[]{:S(2)}, u32[]{:S(2)}) async-start(bf16[32,2,2,64,224]{4,3,2,1,0:T(8,128)(2,1)} %bitcast.65), calls=%async_computation | async-start | bytes 8388608 | tf_op jit(solution)/shard_map/all_to_all | solution.py:155
  40.1 0.1 copy.21
  40.3 0.1 reduce
  40.5 3.9 %fusion.17 = f32[3,768,224]{1,2,0:T(8,128)S(1)} fusion(bf16[3,224,1792]{2,1,0:T(8,128)(2,1)S(1)} %copy-done, bf16[768,1792]{1,0:T(8,128)(2,1)} %param.15), kind=kOutput, calls=%fused_computation.33 | convolution fusion | flops 1849688064 | bytes 7225344 | tf_op jit(solution)/shard_map/td,kcd->ktc/dot_general | solution.py:88
  44.4 1.4 copy-done.2
  46.0 2.8 fusion.52
  48.8 26.8 %psum.14 = bf16[768,16]{0,1:T(8,128)(2,1)S(1)} all-reduce(bf16[768,16]{0,1:T(8,128)(2,1)S(1)} %multiply_reduce_fusion), channel_id=1, replica_groups=mesh['req'=32,'mdl'=8] {'mdl'}, use_global_device_ids=true, to_apply=%region_4.5 | all-reduce | flops 12288 | bytes 49152 | tf_op jit(solution)/shard_map/psum | solution.py:103
  75.6 0.8 fusion.39
  76.4 0.2 convert_reduce_fusion
  76.6 0.8 fusion.38
  77.4 0.1 select_reduce_fusion.2
  77.5 0.1 select_reduce_fusion.1
  77.7 0.1 broadcast_multiply_fusion
  77.8 1.4 fusion.48
  79.2 0.9 fusion.53
  80.1 0.1 fusion.50
  80.2 0.3 fusion.14
  80.5 1.1 add_convert_fusion.3
  81.6 1.2 compare_and_fusion
  82.9 1.3 pad_add_fusion
  84.2 49.6 %all-to-all-done = bf16[32,2,2,64,224]{4,3,2,1,0:T(8,128)(2,1)} async-done(((bf16[32,2,2,64,224]{4,3,2,1,0:T(8,128)(2,1)}), bf16[32,2,2,64,224]{4,3,2,1,0:T(8,128)(2,1)}, u32[]{:S(2)}, u32[]{:S(2)}) %all-to-all-start) | async-done | bytes 3670048 | tf_op jit(solution)/shard_map/all_to_all | solution.py:155
  133.8 2.8 gather_fusion
  136.7 0.2 fusion.49
  136.8 0.4 concatenate.18
  137.3 0.6 copy.30
  137.9 0.4 concatenate.15
  138.3 0.6 copy.29
  138.9 9.6 %fusion.51 = (f32[2,768]{1,0:T(2,128)S(1)}, f32[2,768,2304]{2,1,0:T(8,128)}) fusion(pred[768,2304]{1,0:T(8,128)(4,1)} %pad_add_fusion, bf16[768,2,112]{0,2,1:T(8,128)(2,1)S(1)} %copy-done.6, bf16[1536,2,112]{0,2,1:T(8,128)(2,1)S(1)} %copy.30, bf16[768,2,112]{0,2,1:T(8,128)(2,1)S(1)} %bitcast.73), kind=kOutput, calls=%fused_computation.90 | convolution fusion | flops 808945920 | bytes 17307648 | tf_op jit(solution)/shard_map/sub | solution.py:184
  148.5 7.6 %fusion.22 = bf16[2,112,768]{2,1,0:T(8,128)(2,1)S(1)} fusion(f32[2,768,2304]{2,1,0:T(8,128)} %get-tuple-element.20, f32[2,768]{1,0:T(2,128)S(1)} %get-tuple-element.19, bf16[1536,2,112]{0,2,1:T(8,128)(2,1)S(1)} %copy.29, bf16[768,2,112]{0,2,1:T(8,128)(2,1)S(1)} %copy-done.5), kind=kOutput, calls=%fused_computation.35 | convolution fusion | flops 802037760 | bytes 15538176 | tf_op jit(solution)/shard_map/hts,shd->thd/dot_general | solution.py:187
  156.1 2.5 convolution_convert_fusion
  158.7 0.5 all-gather.2.cloned.1.call-update
  159.2 0.3 reduce-scatter.2.cloned.1.call-start
  159.5 71.7 %all-reduce.2.cloned.1.call-done = bf16[768,1792]{1,0:T(8,128)(2,1)} async-done(((bf16[768,1792]{1,0:T(8,128)(2,1)}), bf16[768,1792]{1,0:T(8,128)(2,1)}) %all-reduce.2.cloned.1.call-update) | async-done | bytes 2752528 | tf_op jit(solution)/shard_map/psum | solution.py:197
  231.2 5.3 %fusion.6 = (f32[768]{0:T(1024)S(1)}, bf16[768,1792]{1,0:T(8,128)(2,1)}) fusion(bf16[768,1792]{1,0:T(8,128)(2,1)} %all-reduce.2.cloned.1.call-done, bf16[768,1792]{1,0:T(8,128)(2,1)} %param.15), kind=kLoop, calls=%fused_computation.13 | loop fusion | flops 9633024 | bytes 8260608 | tf_op jit(solution)/shard_map/reduce_sum | solution.py:200
  236.6 14.1 %all-gather.2.cloned.1.call-done = bf16[3,1792,608]{2,1,0:T(8,128)(2,1)} async-done(((bf16[3,56,608]{2,1,0:T(8,128)(2,1)}), bf16[3,1792,608]{2,1,0:T(8,128)(2,1)}) %all-gather.2.cloned.1.call-update) | async-done | bytes 6537232 | tf_op jit(solution)/shard_map/all_gather | solution.py:203
  250.6 5.8 %fusion.16 = f32[768,608]{0,1:T(8,128)} fusion(bf16[3,1792,608]{2,1,0:T(8,128)(2,1)} %all-gather.2.cloned.1.call-done, bf16[768,1792]{1,0:T(8,128)(2,1)} %get-tuple-element.10, f32[1792]{0:T(1024)S(1)} %convert_element_type.118, f32[768]{0:T(1024)S(1)} %add_rsqrt_fusion), kind=kOutput, calls=%fused_computation.31 | convolution fusion | flops 1679032320 | bytes 6924288 | tf_op jit(solution)/shard_map/dot_general | solution.py:204
  256.5 10.5 %convolution_convert_fusion.1 = bf16[768,1792]{1,0:T(8,128)(2,1)} fusion(bf16[3,1792,608]{2,1,0:T(8,128)(2,1)} %all-gather.2.cloned.1.call-done, f32[768,608]{0,1:T(8,128)} %fusion.16, bf16[768,1792]{1,0:T(8,128)(2,1)} %get-tuple-element.10, f32[1792]{0:T(1024)S(1)} %convert_element_type.118, f32[768]{0:T(1024)S(1)} %add_rsqrt_fusion), kind=kOutput, calls=%fused_computation.19 | convolution fusion | flops 3356737536 | bytes 11970560 | tf_op jit(solution)/shard_map/tf,df->td/dot_general | solution.py:208
  267.1 36.0 %reduce-scatter.2.cloned.1.call-done = bf16[96,1792]{1,0:T(8,128)(2,1)} async-done(((bf16[768,1792]{1,0:T(8,128)(2,1)}), bf16[96,1792]{1,0:T(8,128)(2,1)}) %reduce-scatter.2.cloned.1.call-update) | async-done | bytes 344080 | tf_op jit(solution)/shard_map/reduce_scatter | solution.py:212
  303.0 1.9 add_convert_fusion.1
  (53 shorter events, 1.1 us)
Async XLA Ops:
  7.4 33.2 %copy-start = (bf16[3,224,1792]{2,1,0:T(8,128)(2,1)S(1)}, bf16[3,224,1792]{2,1,0:T(8,128)(2,1)}, u32[]{:S(2)}) copy-start(bf16[3,224,1792]{2,1,0:T(8,128)(2,1)} %param.16) | copy-start | bytes 7225348
  28.3 11.8 %copy-start.9 = (s32[1,24]{1,0:T(1,128)S(1)}, s32[1,24]{1,0:T(1,128)}, u32[]{:S(2)}) copy-start(s32[1,24]{1,0:T(1,128)} %param.25) | copy-start | bytes 292
  28.3 105.5 %all-to-all-start = ((bf16[32,2,2,64,224]{4,3,2,1,0:T(8,128)(2,1)}), bf16[32,2,2,64,224]{4,3,2,1,0:T(8,128)(2,1)}, u32[]{:S(2)}, u32[]{:S(2)}) async-start(bf16[32,2,2,64,224]{4,3,2,1,0:T(8,128)(2,1)} %bitcast.65), calls=%async_computation | async-start | bytes 8388608 | tf_op jit(solution)/shard_map/all_to_all | solution.py:155
  40.1 191.1 %all-reduce.2.cloned.1.call-start = ((), (), s32[]{:S(2)}) async-start(), calls=%async_computation.2 | async-start | bytes 5505024 | tf_op jit(solution)/shard_map/psum | solution.py:197
  40.5 5.4 %copy-start.7 = (s32[768]{0:T(1024)S(1)}, s32[768]{0:T(1024)}, u32[]{:S(2)}) copy-start(s32[768]{0:T(1024)} %param.24) | copy-start | bytes 9220
  40.5 5.4 %copy-start.4 = (bf16[8,1792,16]{1,2,0:T(8,128)(2,1)S(1)}, bf16[8,1792,16]{1,2,0:T(8,128)(2,1)}, u32[]{:S(2)}) copy-start(bf16[8,1792,16]{1,2,0:T(8,128)(2,1)} %param.18) | copy-start | bytes 1376260
  44.4 1.4 copy-start.2
  45.9 31.5 %copy-start.11 = (f32[4]{0:T(128)S(1)}, f32[4]{0:T(128)}, u32[]{:S(2)}) copy-start(f32[4]{0:T(128)} %param.20) | copy-start | bytes 52
  45.9 31.5 %copy-start.12 = (s32[24]{0:T(128)S(1)}, s32[24]{0:T(128)}, u32[]{:S(2)}) copy-start(s32[24]{0:T(128)} %param.26) | copy-start | bytes 292
  48.8 30.4 %copy-start.10 = (bf16[2,224,1024]{2,1,0:T(8,128)(2,1)S(1)}, bf16[2,224,1024]{2,1,0:T(8,128)(2,1)}, u32[]{:S(2)}) copy-start(bf16[2,224,1024]{2,1,0:T(8,128)(2,1)} %param.19) | copy-start | bytes 2752516
  137.3 1.6 copy-start.6
  138.9 9.6 %copy-start.5 = (bf16[768,2,112]{0,2,1:T(8,128)(2,1)S(1)}, bf16[768,2,112]{0,2,1:T(8,128)(2,1)}, u32[]{:S(2)}) copy-start(bf16[768,2,112]{0,2,1:T(8,128)(2,1)} %get-tuple-element.17) | copy-start | bytes 1032196
  148.5 7.6 %copy-start.3 = (bf16[224,1792]{1,0:T(8,128)(2,1)S(1)}, bf16[224,1792]{1,0:T(8,128)(2,1)}, u32[]{:S(2)}) copy-start(bf16[224,1792]{1,0:T(8,128)(2,1)} %param.17) | copy-start | bytes 2408452
  156.0 3.4 %copy-start.8 = (bf16[1792]{0:T(1024)(128)(2,1)S(1)}, bf16[1792]{0:T(1024)(128)(2,1)}, u32[]{:S(2)}) copy-start(bf16[1792]{0:T(1024)(128)(2,1)} %param.21) | copy-start | bytes 10756
  158.6 92.0 %all-gather.2.cloned.1.call-start = ((), (), s32[]{:S(2)}) async-start(), calls=%async_computation.3 | async-start | bytes 7096320 | tf_op jit(solution)/shard_map/all_gather | solution.py:203
  159.2 143.8 %reduce-scatter.2.cloned.1.call-start = ((), (), s32[]{:S(2)}) async-start(), calls=%async_computation.4 | async-start | bytes 3096576 | tf_op jit(solution)/shard_map/reduce_scatter | solution.py:212
  256.5 48.4 %copy-start.1 = (bf16[3,224,1792]{2,1,0:T(8,128)(2,1)S(1)}, bf16[3,224,1792]{2,1,0:T(8,128)(2,1)}, u32[]{:S(2)}) copy-start(bf16[3,224,1792]{2,1,0:T(8,128)(2,1)} %param.16) | copy-start | bytes 7225348
Sparse Core Ops, SparseCore 0:
  158.7 72.4 all-reduce.1
  267.2 35.7 reduce-scatter.1
Sparse Core Ops, SparseCore 1:
  162.1 88.5 all-gather.1

commit v6 on v5

--- a/solution.py
+++ b/solution.py
@@ -55,6 +55,62 @@
         ),
         out_shape=jax.ShapeDtypeStruct((count, parts, WINDOW, width), store.dtype),
     )(slots, fills, store)
+
+
+def exchange_kernel(sent, out_ref, got, send_sems, recv_sems):
+    peers = lax.axis_size("req")
+    cap = sent.shape[0] // peers
+    me = lax.axis_index("req")
+    mine = lax.axis_index("mdl")
+    barrier = pltpu.get_barrier_semaphore()
+
+    def greet(k, carry):
+        peer = lax.rem(me + k, peers)
+        pl.semaphore_signal(barrier, inc=1, device_id=(peer, mine), device_id_type=pl.DeviceIdType.MESH)
+        return carry
+
+    lax.fori_loop(1, peers, greet, 0)
+    pl.semaphore_wait(barrier, peers - 1)
+
+    def send(k):
+        peer = lax.rem(me + k, peers)
+        return pltpu.make_async_remote_copy(
+            src_ref=sent.at[pl.ds(peer * cap, cap)],
+            dst_ref=got.at[pl.ds(me * cap, cap)],
+            send_sem=send_sems.at[k],
+            recv_sem=recv_sems.at[k],
+            device_id=(peer, mine),
+            device_id_type=pl.DeviceIdType.MESH,
+        )
+
+    def start_send(k, carry):
+        send(k).start()
+        return carry
+
+    lax.fori_loop(1, peers, start_send, 0)
+    got[pl.ds(me * cap, cap)] = sent[pl.ds(me * cap, cap)]
+
+    def finish(k, carry):
+        send(k).wait()
+        return carry
+
+    lax.fori_loop(1, peers, finish, 0)
+    out_ref[...] = got[...]
+
+
+def exchange_windows(windows, peers):
+    return pl.pallas_call(
+        exchange_kernel,
+        in_specs=[pl.BlockSpec(memory_space=pltpu.VMEM)],
+        out_specs=pl.BlockSpec(memory_space=pltpu.VMEM),
+        scratch_shapes=[
+            pltpu.VMEM(windows.shape, windows.dtype),
+            pltpu.SemaphoreType.DMA((peers,)),
+            pltpu.SemaphoreType.DMA((peers,)),
+        ],
+        out_shape=jax.ShapeDtypeStruct(windows.shape, windows.dtype),
+        compiler_params=pltpu.CompilerParams(collective_id=0, has_side_effects=True),
+    )(windows)
 
 
 def per_device(
@@ -146,13 +202,12 @@
     flat_pick = my_owner * cap_slots + jnp.sum(earlier.astype(jnp.int32), axis=1)
     page_inner = prefix_cache_store.shape[1:3]
     page_rows = prefix_cache_store.shape[3]
-    source_pages = cut_windows(
+    windows = cut_windows(
         prefix_cache_store,
         jnp.clip(send_slot.reshape(-1), 0, prefix_cache_store.shape[0] - 1),
         send_fill.reshape(-1),
     )
-    source_pages = source_pages.reshape((req_devices, cap_slots, 2, WINDOW, head_column_set))
-    arrived = lax.all_to_all(source_pages, "req", split_axis=0, concat_axis=0, tiled=True)
+    arrived = exchange_windows(windows, req_devices)
     prefix = jnp.take(
         arrived.reshape((req_devices * cap_slots, 2, WINDOW, head_column_set)),
         flat_pick,

time: 313 us -> 373 us (1.19)
  Pallas kernels: 16.5 us -> 121 us
  waiting for transfers between devices: 172 us -> 135 us
  starting transfers between devices: 12.1 us -> 0.31 us
    pallas_call x0 -> x1, Pallas kernels: none -> 105 us  [exchange_windows(): pl.pallas_call(exchange_kernel, in_specs=[pl.BlockSpec(memory_space=pltpu...]
    all_to_all x1 -> x0, waiting for transfers between devices: 49.6 us -> none  [per_device(): lax.all_to_all(source_pages, 'req', split_axis=0, concat_axis=0, tiled=True)]
    psum x1, waiting for transfers between devices: 71.7 us -> 84.5 us  [per_device(): lax.psum(attn_part.astype(jnp.bfloat16), 'mdl').astype(jnp.float32)]
    all_to_all x1 -> x0, starting transfers between devices: 11.8 us -> none  [per_device(): lax.all_to_all(source_pages, 'req', split_axis=0, concat_axis=0, tiled=True)]
  transfers between devices with their start and end apart: 4 -> 3, of which waited for: 4 -> 3; matrix products, arithmetic and copies ran while one was open for 7% -> 1% of each run, Pallas kernels for 0% -> 0%
where the time goes in v6:
time: 373 us; the launch traced here: 372 us
  waiting for transfers between devices  135 us (36%)
  Pallas kernels  121 us (32%)
  matrix products  47.3 us (13%)
  blocking collectives  24.8 us (7%)
  between operations  15.2 us (4%)
  local copies, waits for them, and re-layouts  14.1 us (4%)
  other arithmetic  14.1 us (4%)
    pallas_call x1, Pallas kernels, exchange_windows(): pl.pallas_call(exchange_kernel, in_specs=[pl.BlockSpec(memory_space=pltpu...  105 us
    psum x1, waiting for transfers between devices, per_device(): lax.psum(attn_part.astype(jnp.bfloat16), 'mdl').astype(jnp.float32)  84.5 us
    reduce_scatter x1, waiting for transfers between devices, per_device(): lax.psum_scatter(mlp_part.astype(jnp.bfloat16), 'mdl', scatter_dimension=...  36 us
    psum x1, blocking collectives, per_device(): rank_feat = lax.psum(rank_part.astype(jnp.bfloat16), 'mdl')  24.8 us
    pallas_call x1, Pallas kernels, cut_windows(): pl.pallas_call(window_kernel, grid_spec=pltpu.PrefetchScalarGridSpec(num_...  16.5 us
    all_gather x1, waiting for transfers between devices, per_device(): full_mlp = lax.all_gather(feedforward_weight, 'req', axis=1, tiled=True)  14.1 us
    sub x1, matrix products, per_device(): exp_scores = jnp.exp(masked - row_max)  12.1 us
    dot_general x1, matrix products, per_device(): jnp.einsum('tf,df->td', hidden, full_mlp[2], preferred_element_type=jnp.f...  10.5 us
  transfers between devices with their start and end apart: 3, of which 3 were waited for; matrix products, arithmetic and copies ran while one was open for 1% of the time, Pallas kernels for 0%

profile of v6, /device:TPU:8, one launch (start us, length us, event | category | flops | bytes accessed | tf_op | source)
XLA Modules:
  0.0 372.2 jit_solution(2946023521041700107)
XLA Ops:
  7.4 1.7 copy-done
  9.0 3.8 %fusion.17 = f32[3,768,224]{1,2,0:T(8,128)S(1)} fusion(bf16[3,224,1792]{2,1,0:T(8,128)(2,1)S(1)} %copy-done, bf16[768,1792]{1,0:T(8,128)(2,1)} %param.15), kind=kOutput, calls=%fused_computation.33 | convolution fusion | flops 1849688064 | bytes 7225344 | tf_op jit(solution)/shard_map/td,kcd->ktc/dot_general | solution.py:144
  12.9 1.3 fusion.48
  14.3 0.1 reshape.158
  14.4 0.2 reduce_window_sum.18
  14.7 0.2 convert_reduce_fusion
  14.9 0.1 fusion.38
  15.0 0.1 mul.159
  15.2 0.1 mul.162
  15.4 0.1 copy.28
  15.5 0.6 min.12.slot_ref
  16.1 0.1 copy.30
  16.2 0.6 reshape.156.fill_ref
  16.8 16.5 %shard_map.145.sent = bf16[64,2,64,224]{3,2,1,0:T(8,128)(2,1)} custom-call(s32[64]{0:T(128)} %min.12.slot_ref, s32[64]{0:T(128)} %reshape.156.fill_ref, bf16[32,2,224,128]{3,2,1,0:T(8,128)(2,1)} %store_ref.1), custom_call_target="tpu_custom_call" | custom-call | tf_op jit(solution)/shard_map/pallas_call | solution.py:44
  33.3 104.8 %shard_map.146 = bf16[64,2,64,224]{3,2,1,0:T(8,128)(2,1)} custom-call(bf16[64,2,64,224]{3,2,1,0:T(8,128)(2,1)} %shard_map.145.sent), custom_call_target="tpu_custom_call" | custom-call | tf_op jit(solution)/shard_map/pallas_call | solution.py:102
  138.1 2.8 gather_fusion
  141.0 0.2 fusion.49
  141.2 0.4 concatenate.18
  141.6 1.8 copy.32
  143.4 0.1 copy.23
  143.5 0.1 reduce
  143.7 0.1 select_reduce_fusion.1
  143.9 1.1 fusion.14
  145.1 0.1 select_reduce_fusion.3
  145.2 0.1 select_reduce_fusion.2
  145.4 2.8 fusion.52
  148.2 24.8 %psum.14 = bf16[768,16]{0,1:T(8,128)(2,1)S(1)} all-reduce(bf16[768,16]{0,1:T(8,128)(2,1)S(1)} %multiply_reduce_fusion), channel_id=1, replica_groups=mesh['req'=32,'mdl'=8] {'mdl'}, use_global_device_ids=true, to_apply=%region_4.5 | all-reduce | flops 12288 | bytes 49152 | tf_op jit(solution)/shard_map/psum | solution.py:159
  173.1 0.1 broadcast_multiply_fusion
  173.2 2.1 fusion.53
  175.3 1.2 fusion.50
  176.5 0.4 concatenate.15
  176.9 1.8 copy.31
  178.7 1.2 compare_and_fusion
  180.0 2.4 pad_add_fusion
  182.4 0.9 add_convert_fusion.3
  183.3 0.2 copy-done.7
  183.4 12.1 %fusion.51 = (f32[2,768]{1,0:T(2,128)S(1)}, f32[2,768,2304]{2,1,0:T(8,128)}) fusion(pred[768,2304]{1,0:T(8,128)(4,1)} %pad_add_fusion, bf16[768,2,112]{0,2,1:T(8,128)(2,1)} %get-tuple-element.18, bf16[1536,2,112]{0,2,1:T(8,128)(2,1)S(1)} %copy-done.7, bf16[768,2,112]{0,2,1:T(8,128)(2,1)S(1)} %bitcast.70), kind=kOutput, calls=%fused_computation.90 | convolution fusion | flops 808945920 | bytes 17307648 | tf_op jit(solution)/shard_map/sub | solution.py:239
  195.6 7.6 %fusion.22 = bf16[2,112,768]{2,1,0:T(8,128)(2,1)S(1)} fusion(f32[2,768,2304]{2,1,0:T(8,128)} %get-tuple-element.20, f32[2,768]{1,0:T(2,128)S(1)} %get-tuple-element.19, bf16[1536,2,112]{0,2,1:T(8,128)(2,1)S(1)} %copy-done.8, bf16[768,2,112]{0,2,1:T(8,128)(2,1)S(1)} %get-tuple-element.17), kind=kOutput, calls=%fused_computation.35 | convolution fusion | flops 802037760 | bytes 15538176 | tf_op jit(solution)/shard_map/hts,shd->thd/dot_general | solution.py:242
  203.2 2.5 convolution_convert_fusion
  205.8 0.5 all-gather.2.cloned.1.call-update
  206.3 0.3 reduce-scatter.2.cloned.1.call-start
  206.6 84.5 %all-reduce.2.cloned.1.call-done = bf16[768,1792]{1,0:T(8,128)(2,1)} async-done(((bf16[768,1792]{1,0:T(8,128)(2,1)}), bf16[768,1792]{1,0:T(8,128)(2,1)}) %all-reduce.2.cloned.1.call-update) | async-done | bytes 2752528 | tf_op jit(solution)/shard_map/psum | solution.py:252
  291.1 5.3 %fusion.6 = (f32[768]{0:T(1024)S(1)}, bf16[768,1792]{1,0:T(8,128)(2,1)}) fusion(bf16[768,1792]{1,0:T(8,128)(2,1)} %all-reduce.2.cloned.1.call-done, bf16[768,1792]{1,0:T(8,128)(2,1)} %param.15), kind=kLoop, calls=%fused_computation.13 | loop fusion | flops 9633024 | bytes 8260608 | tf_op jit(solution)/shard_map/reduce_sum | solution.py:255
  296.4 14.1 %all-gather.2.cloned.1.call-done = bf16[3,1792,608]{2,1,0:T(8,128)(2,1)} async-done(((bf16[3,56,608]{2,1,0:T(8,128)(2,1)}), bf16[3,1792,608]{2,1,0:T(8,128)(2,1)}) %all-gather.2.cloned.1.call-update) | async-done | bytes 6537232 | tf_op jit(solution)/shard_map/all_gather | solution.py:258
  310.5 5.8 %fusion.16 = f32[768,608]{0,1:T(8,128)} fusion(bf16[3,1792,608]{2,1,0:T(8,128)(2,1)} %all-gather.2.cloned.1.call-done, bf16[768,1792]{1,0:T(8,128)(2,1)} %get-tuple-element.10, f32[1792]{0:T(1024)S(1)} %convert_element_type.118, f32[768]{0:T(1024)S(1)} %add_rsqrt_fusion), kind=kOutput, calls=%fused_computation.31 | convolution fusion | flops 1679032320 | bytes 6924288 | tf_op jit(solution)/shard_map/dot_general | solution.py:259
  316.3 10.5 %convolution_convert_fusion.1 = bf16[768,1792]{1,0:T(8,128)(2,1)} fusion(bf16[3,1792,608]{2,1,0:T(8,128)(2,1)} %all-gather.2.cloned.1.call-done, f32[768,608]{0,1:T(8,128)} %fusion.16, bf16[768,1792]{1,0:T(8,128)(2,1)} %get-tuple-element.10, f32[1792]{0:T(1024)S(1)} %convert_element_type.118, f32[768]{0:T(1024)S(1)} %add_rsqrt_fusion), kind=kOutput, calls=%fused_computation.19 | convolution fusion | flops 3356737536 | bytes 11970560 | tf_op jit(solution)/shard_map/tf,df->td/dot_general | solution.py:263
  326.9 36.0 %reduce-scatter.2.cloned.1.call-done = bf16[96,1792]{1,0:T(8,128)(2,1)} async-done(((bf16[768,1792]{1,0:T(8,128)(2,1)}), bf16[96,1792]{1,0:T(8,128)(2,1)}) %reduce-scatter.2.cloned.1.call-update) | async-done | bytes 344080 | tf_op jit(solution)/shard_map/reduce_scatter | solution.py:267
  362.9 1.9 add_convert_fusion.1
  (62 shorter events, 1.0 us)
Async XLA Ops:
  7.4 1.7 copy-start
  7.4 283.7 %all-reduce.2.cloned.1.call-start = ((), (), s32[]{:S(2)}) async-start(), calls=%async_computation.1 | async-start | bytes 5505024 | tf_op jit(solution)/shard_map/psum | solution.py:252
  12.9 1.4 copy-start.11
  12.9 2.1 copy-start.12
  12.9 2.3 copy-start.13
  141.0 2.4 copy-start.15
  141.0 4.1 %copy-start.16 = (f32[4]{0:T(128)S(1)}, f32[4]{0:T(128)}, u32[]{:S(2)}) copy-start(f32[4]{0:T(128)} %param.20) | copy-start | bytes 52
  141.0 4.1 %copy-start.17 = (s32[24]{0:T(128)S(1)}, s32[24]{0:T(128)}, u32[]{:S(2)}) copy-start(s32[24]{0:T(128)} %param.26) | copy-start | bytes 292
  141.0 4.3 %copy-start.10 = (s32[768]{0:T(1024)S(1)}, s32[768]{0:T(1024)}, u32[]{:S(2)}) copy-start(s32[768]{0:T(1024)} %param.24) | copy-start | bytes 9220
  141.2 4.2 %copy-start.9 = (bf16[8,1792,16]{1,2,0:T(8,128)(2,1)S(1)}, bf16[8,1792,16]{1,2,0:T(8,128)(2,1)}, u32[]{:S(2)}) copy-start(bf16[8,1792,16]{1,2,0:T(8,128)(2,1)} %param.18) | copy-start | bytes 1376260
  176.9 5.5 %copy-start.2 = (f32[1,768,224]{1,2,0:T(8,128)S(1)}, f32[1,768,224]{1,2,0:T(8,128)}, u32[]{:S(2)}) copy-start(f32[1,768,224]{1,2,0:T(8,128)} %get-tuple-element.11) | copy-start | bytes 2064388
  176.9 5.5 %copy-start.3 = (f32[1,768,224]{1,2,0:T(8,128)S(1)}, f32[1,768,224]{1,2,0:T(8,128)}, u32[]{:S(2)}) copy-start(f32[1,768,224]{1,2,0:T(8,128)} %get-tuple-element.12) | copy-start | bytes 2064388
  178.7 3.7 copy-start.4
  178.7 3.7 copy-start.5
  182.3 1.1 copy-start.7
  183.4 12.1 %copy-start.8 = (bf16[1536,2,112]{0,2,1:T(8,128)(2,1)S(1)}, bf16[1536,2,112]{0,2,1:T(8,128)(2,1)}, u32[]{:S(2)}) copy-start(bf16[1536,2,112]{0,2,1:T(8,128)(2,1)} %copy.31) | copy-start | bytes 2064388
  195.6 7.6 %copy-start.6 = (bf16[224,1792]{1,0:T(8,128)(2,1)S(1)}, bf16[224,1792]{1,0:T(8,128)(2,1)}, u32[]{:S(2)}) copy-start(bf16[224,1792]{1,0:T(8,128)(2,1)} %param.17) | copy-start | bytes 2408452
  203.2 3.4 copy-start.14
  205.7 104.8 %all-gather.2.cloned.1.call-start = ((), (), s32[]{:S(2)}) async-start(), calls=%async_computation.2 | async-start | bytes 7096320 | tf_op jit(solution)/shard_map/all_gather | solution.py:258
  206.3 156.6 %reduce-scatter.2.cloned.1.call-start = ((), (), s32[]{:S(2)}) async-start(), calls=%async_computation.3 | async-start | bytes 3096576 | tf_op jit(solution)/shard_map/reduce_scatter | solution.py:267
  316.3 48.4 %copy-start.1 = (bf16[3,224,1792]{2,1,0:T(8,128)(2,1)S(1)}, bf16[3,224,1792]{2,1,0:T(8,128)(2,1)}, u32[]{:S(2)}) copy-start(bf16[3,224,1792]{2,1,0:T(8,128)(2,1)} %param.16) | copy-start | bytes 7225348
Sparse Core Ops, SparseCore 0:
  205.8 85.1 all-reduce.1
  327.0 35.7 reduce-scatter.1
Sparse Core Ops, SparseCore 1:
  209.2 101.2 all-gather.1

commit v7 on v5

--- a/solution.py
+++ b/solution.py
@@ -201,18 +201,24 @@
     normed = (resid_wide * lax.rsqrt(mean_sq + 1e-06) * gain_wide).astype(jnp.bfloat16)
     resid_mine = lax.dynamic_slice_in_dim(resid_full, mdl_index * row_share, row_share, 0)
     full_mlp = lax.all_gather(feedforward_weight, "req", axis=1, tiled=True)
-    gate_part = jnp.dot(normed, full_mlp[0], preferred_element_type=jnp.float32)
-    up_part = jnp.dot(normed, full_mlp[1], preferred_element_type=jnp.float32)
-    hidden = (jax.nn.silu(gate_part) * up_part).astype(jnp.bfloat16)
-    mlp_part = (
-        jnp.einsum("tf,df->td", hidden, full_mlp[2], preferred_element_type=jnp.float32)
-        .astype(jnp.bfloat16)
-        .astype(jnp.float32)
-    )
-    mlp_mine = lax.psum_scatter(
-        mlp_part.astype(jnp.bfloat16), "mdl", scatter_dimension=0, tiled=True
-    ).astype(jnp.float32)
-    return (resid_mine.astype(jnp.float32) + mlp_mine).astype(jnp.bfloat16)
+    mdl_devices = lax.axis_size("mdl")
+    halves = 2
+    normed_split = normed.reshape(mdl_devices, halves, row_share // halves, model_width)
+    resid_split = resid_mine.reshape(halves, row_share // halves, model_width)
+    outputs = []
+    for half in range(halves):
+        normed_half = normed_split[:, half].reshape(-1, model_width)
+        gate_part = jnp.dot(normed_half, full_mlp[0], preferred_element_type=jnp.float32)
+        up_part = jnp.dot(normed_half, full_mlp[1], preferred_element_type=jnp.float32)
+        hidden = (jax.nn.silu(gate_part) * up_part).astype(jnp.bfloat16)
+        mlp_part = jnp.einsum(
+            "tf,df->td", hidden, full_mlp[2], preferred_element_type=jnp.float32
+        ).astype(jnp.bfloat16)
+        mlp_mine = lax.psum_scatter(mlp_part, "mdl", scatter_dimension=0, tiled=True).astype(
+            jnp.float32
+        )
+        outputs.append((resid_split[half].astype(jnp.float32) + mlp_mine).astype(jnp.bfloat16))
+    return jnp.concatenate(outputs, axis=0)
 
 
 def solution(mesh):

time: 313 us -> 340 us (1.086)
  waiting for transfers between devices: 172 us -> 194 us
    reduce_scatter x1 -> x2, waiting for transfers between devices: 36 us -> 59.8 us  [per_device(): lax.psum_scatter(mlp_part, 'mdl', scatter_dimension=0, tiled=True)]
    dot_general x1 -> x2, matrix products: 10.5 us -> 13.4 us  [per_device(): jnp.einsum('tf,df->td', hidden, full_mlp[2], preferred_element_type=jnp.f...]
  transfers between devices with their start and end apart: 4 -> 5, of which waited for: 4 -> 5; matrix products, arithmetic and copies ran while one was open for 7% -> 9% of each run, Pallas kernels for 0% -> 0%
where the time goes in v7:
time: 340 us; the launch traced here: 339 us
  waiting for transfers between devices  194 us (57%)
  matrix products  47 us (14%)
  blocking collectives  26.8 us (8%)
  Pallas kernels  16.5 us (5%)
  between operations  15 us (4%)
  local copies, waits for them, and re-layouts  14.5 us (4%)
  other arithmetic  13.2 us (4%)
  starting transfers between devices  12.2 us (4%)
    psum x1, waiting for transfers between devices, per_device(): lax.psum(attn_part.astype(jnp.bfloat16), 'mdl').astype(jnp.float32)  71.7 us
    reduce_scatter x2, waiting for transfers between devices, per_device(): lax.psum_scatter(mlp_part, 'mdl', scatter_dimension=0, tiled=True)  59.8 us
    all_to_all x1, waiting for transfers between devices, per_device(): lax.all_to_all(source_pages, 'req', split_axis=0, concat_axis=0, tiled=True)  49.6 us
    psum x1, blocking collectives, per_device(): rank_feat = lax.psum(rank_part.astype(jnp.bfloat16), 'mdl')  26.8 us
    pallas_call x1, Pallas kernels, cut_windows(): pl.pallas_call(window_kernel, grid_spec=pltpu.PrefetchScalarGridSpec(num_...  16.5 us
    dot_general x2, matrix products, per_device(): jnp.einsum('tf,df->td', hidden, full_mlp[2], preferred_element_type=jnp.f...  13.4 us
    all_gather x1, waiting for transfers between devices, per_device(): full_mlp = lax.all_gather(feedforward_weight, 'req', axis=1, tiled=True)  12.7 us
    all_to_all x1, starting transfers between devices, per_device(): lax.all_to_all(source_pages, 'req', split_axis=0, concat_axis=0, tiled=True)  11.8 us
  transfers between devices with their start and end apart: 5, of which 5 were waited for; matrix products, arithmetic and copies ran while one was open for 9% of the time, Pallas kernels for 0%

profile of v7, /device:TPU:8, one launch (start us, length us, event | category | flops | bytes accessed | tf_op | source)
XLA Modules:
  0.0 339.5 jit_solution(1881873393995390036)
XLA Ops:
  7.4 0.8 fusion.50
  8.4 0.2 reduce_window_sum.18
  8.6 0.8 mul.165
  9.5 0.8 mul.168
  10.5 0.6 min.12.slot_ref
  11.2 0.6 reshape.170.fill_ref
  11.8 16.5 %shard_map.145 = bf16[64,2,64,224]{3,2,1,0:T(8,128)(2,1)} custom-call(s32[64]{0:T(128)} %min.12.slot_ref, s32[64]{0:T(128)} %reshape.170.fill_ref, bf16[32,2,224,128]{3,2,1,0:T(8,128)(2,1)} %store_ref.1), custom_call_target="tpu_custom_call" | custom-call | tf_op jit(solution)/shard_map/pallas_call | solution.py:44
  28.3 11.8 %all-to-all-start = ((bf16[32,2,2,64,224]{4,3,2,1,0:T(8,128)(2,1)}), bf16[32,2,2,64,224]{4,3,2,1,0:T(8,128)(2,1)}, u32[]{:S(2)}, u32[]{:S(2)}) async-start(bf16[32,2,2,64,224]{4,3,2,1,0:T(8,128)(2,1)} %bitcast.83), calls=%async_computation | async-start | bytes 8388608 | tf_op jit(solution)/shard_map/all_to_all | solution.py:155
  40.5 3.9 %fusion.19 = f32[3,768,224]{1,2,0:T(8,128)S(1)} fusion(bf16[3,224,1792]{2,1,0:T(8,128)(2,1)S(1)} %copy-done, bf16[768,1792]{1,0:T(8,128)(2,1)} %param.15), kind=kOutput, calls=%fused_computation.35 | convolution fusion | flops 1849688064 | bytes 7225344 | tf_op jit(solution)/shard_map/td,kcd->ktc/dot_general | solution.py:88
  44.4 1.4 copy-done.3
  46.0 2.8 fusion.68
  48.8 26.8 %psum.14 = bf16[768,16]{0,1:T(8,128)(2,1)S(1)} all-reduce(bf16[768,16]{0,1:T(8,128)(2,1)S(1)} %multiply_reduce_fusion), channel_id=1, replica_groups=mesh['req'=32,'mdl'=8] {'mdl'}, use_global_device_ids=true, to_apply=%region_4.5 | all-reduce | flops 12288 | bytes 49152 | tf_op jit(solution)/shard_map/psum | solution.py:103
  75.6 0.8 fusion.53
  76.4 0.2 convert_reduce_fusion
  76.6 0.8 fusion.52
  77.7 0.1 broadcast_multiply_fusion
  77.8 1.4 fusion.64
  79.2 0.9 fusion.69
  80.2 0.3 fusion.14
  80.6 1.1 add_convert_fusion.2
  81.6 1.2 compare_and_fusion
  82.9 1.3 pad_add_fusion
  84.2 49.6 %all-to-all-done = bf16[32,2,2,64,224]{4,3,2,1,0:T(8,128)(2,1)} async-done(((bf16[32,2,2,64,224]{4,3,2,1,0:T(8,128)(2,1)}), bf16[32,2,2,64,224]{4,3,2,1,0:T(8,128)(2,1)}, u32[]{:S(2)}, u32[]{:S(2)}) %all-to-all-start) | async-done | bytes 3670048 | tf_op jit(solution)/shard_map/all_to_all | solution.py:155
  133.8 2.8 gather_fusion
  136.7 0.2 fusion.65
  136.8 0.4 concatenate.21
  137.3 0.6 copy.30
  137.9 0.4 concatenate.18
  138.3 0.6 copy.29
  138.9 9.6 %fusion.67 = (f32[2,768]{1,0:T(2,128)S(1)}, f32[2,768,2304]{2,1,0:T(8,128)}) fusion(pred[768,2304]{1,0:T(8,128)(4,1)} %pad_add_fusion, bf16[768,2,112]{0,2,1:T(8,128)(2,1)S(1)} %copy-done.8, bf16[1536,2,112]{0,2,1:T(8,128)(2,1)S(1)} %copy.30, bf16[768,2,112]{0,2,1:T(8,128)(2,1)S(1)} %bitcast.96), kind=kOutput, calls=%fused_computation.111 | convolution fusion | flops 808945920 | bytes 17307648 | tf_op jit(solution)/shard_map/sub | solution.py:184
  148.5 7.6 %fusion.28 = bf16[2,112,768]{2,1,0:T(8,128)(2,1)S(1)} fusion(f32[2,768,2304]{2,1,0:T(8,128)} %get-tuple-element.24, f32[2,768]{1,0:T(2,128)S(1)} %get-tuple-element.23, bf16[1536,2,112]{0,2,1:T(8,128)(2,1)S(1)} %copy.29, bf16[768,2,112]{0,2,1:T(8,128)(2,1)S(1)} %copy-done.7), kind=kOutput, calls=%fused_computation.41 | convolution fusion | flops 802037760 | bytes 15538176 | tf_op jit(solution)/shard_map/hts,shd->thd/dot_general | solution.py:187
  156.0 2.4 convolution_convert_fusion
  158.6 0.5 all-gather.2.cloned.1.call-update
  159.1 0.3 reduce-scatter.5.cloned.1.call-start
  159.4 71.7 %all-reduce.2.cloned.1.call-done = bf16[768,1792]{1,0:T(8,128)(2,1)} async-done(((bf16[768,1792]{1,0:T(8,128)(2,1)}), bf16[768,1792]{1,0:T(8,128)(2,1)}) %all-reduce.2.cloned.1.call-update) | async-done | bytes 2752528 | tf_op jit(solution)/shard_map/psum | solution.py:197
  231.1 3.8 %fusion.6 = (f32[768]{0:T(1024)S(1)}, bf16[768,1792]{1,0:T(8,128)(2,1)S(1)}) fusion(bf16[768,1792]{1,0:T(8,128)(2,1)} %all-reduce.2.cloned.1.call-done, bf16[768,1792]{1,0:T(8,128)(2,1)} %param.15), kind=kLoop, calls=%fused_computation.13 | loop fusion | flops 9633024 | bytes 8260608 | tf_op jit(solution)/shard_map/reduce_sum | solution.py:200
  234.9 0.7 fusion.8
  235.6 0.9 copy-done.2
  236.5 1.3 fusion.63
  237.9 12.7 %all-gather.2.cloned.1.call-done = bf16[3,1792,608]{2,1,0:T(8,128)(2,1)} async-done(((bf16[3,56,608]{2,1,0:T(8,128)(2,1)}), bf16[3,1792,608]{2,1,0:T(8,128)(2,1)}) %all-gather.2.cloned.1.call-update) | async-done | bytes 6537232 | tf_op jit(solution)/shard_map/all_gather | solution.py:203
  250.5 3.4 %fusion.15 = f32[384,608]{0,1:T(8,128)S(1)} fusion(bf16[384,1792]{1,0:T(8,128)(2,1)} %bitcast.93, bf16[3,1792,608]{2,1,0:T(8,128)(2,1)} %all-gather.2.cloned.1.call-done), kind=kOutput, calls=%fused_computation.31 | convolution fusion | flops 836763648 | bytes 4603904 | tf_op jit(solution)/shard_map/dot_general | solution.py:211
  253.9 6.6 %convolution_convert_fusion.1 = bf16[384,1792]{1,0:T(8,128)(2,1)} fusion(bf16[3,1792,608]{2,1,0:T(8,128)(2,1)} %all-gather.2.cloned.1.call-done, bf16[384,1792]{1,0:T(8,128)(2,1)} %bitcast.94, f32[384,608]{0,1:T(8,128)S(1)} %fusion.15), kind=kOutput, calls=%fused_computation.19 | convolution fusion | flops 1675616256 | bytes 8273920 | tf_op jit(solution)/shard_map/tf,df->td/dot_general | solution.py:214
  260.7 3.0 fusion.16
  263.7 6.8 %convolution_convert_fusion.2 = bf16[384,1792]{1,0:T(8,128)(2,1)} fusion(bf16[3,1792,608]{2,1,0:T(8,128)(2,1)} %all-gather.2.cloned.1.call-done, bf16[384,1792]{1,0:T(8,128)(2,1)} %bitcast.92, f32[384,608]{0,1:T(8,128)S(1)} %fusion.16), kind=kOutput, calls=%fused_computation.20 | convolution fusion | flops 1675616256 | bytes 8273920 | tf_op jit(solution)/shard_map/tf,df->td/dot_general | solution.py:214
  270.5 23.5 %reduce-scatter.5.cloned.1.call-done = bf16[48,1792]{1,0:T(8,128)(2,1)} async-done(((bf16[384,1792]{1,0:T(8,128)(2,1)}), bf16[48,1792]{1,0:T(8,128)(2,1)}) %reduce-scatter.5.cloned.1.call-update) | async-done | bytes 172048 | tf_op jit(solution)/shard_map/reduce_scatter | solution.py:217
  294.0 36.4 %reduce-scatter.3.cloned.1.call-done = bf16[48,1792]{1,0:T(8,128)(2,1)} async-done(((bf16[384,1792]{1,0:T(8,128)(2,1)}), bf16[48,1792]{1,0:T(8,128)(2,1)}) %reduce-scatter.3.cloned.1.call-update) | async-done | bytes 172048 | tf_op jit(solution)/shard_map/reduce_scatter | solution.py:217
  330.3 1.2 add_convert_fusion.4
  331.6 0.8 pad_maximum_fusion.7
  (65 shorter events, 1.8 us)
Async XLA Ops:
  7.4 33.2 %copy-start = (bf16[3,224,1792]{2,1,0:T(8,128)(2,1)S(1)}, bf16[3,224,1792]{2,1,0:T(8,128)(2,1)}, u32[]{:S(2)}) copy-start(bf16[3,224,1792]{2,1,0:T(8,128)(2,1)} %param.16) | copy-start | bytes 7225348
  28.3 11.8 %copy-start.11 = (s32[1,24]{1,0:T(1,128)S(1)}, s32[1,24]{1,0:T(1,128)}, u32[]{:S(2)}) copy-start(s32[1,24]{1,0:T(1,128)} %param.25) | copy-start | bytes 292
  28.3 105.5 %all-to-all-start = ((bf16[32,2,2,64,224]{4,3,2,1,0:T(8,128)(2,1)}), bf16[32,2,2,64,224]{4,3,2,1,0:T(8,128)(2,1)}, u32[]{:S(2)}, u32[]{:S(2)}) async-start(bf16[32,2,2,64,224]{4,3,2,1,0:T(8,128)(2,1)} %bitcast.83), calls=%async_computation | async-start | bytes 8388608 | tf_op jit(solution)/shard_map/all_to_all | solution.py:155
  40.1 191.0 %all-reduce.2.cloned.1.call-start = ((), (), s32[]{:S(2)}) async-start(), calls=%async_computation.3 | async-start | bytes 5505024 | tf_op jit(solution)/shard_map/psum | solution.py:197
  40.5 5.3 %copy-start.9 = (s32[768]{0:T(1024)S(1)}, s32[768]{0:T(1024)}, u32[]{:S(2)}) copy-start(s32[768]{0:T(1024)} %param.24) | copy-start | bytes 9220
  40.5 5.4 %copy-start.6 = (bf16[8,1792,16]{1,2,0:T(8,128)(2,1)S(1)}, bf16[8,1792,16]{1,2,0:T(8,128)(2,1)}, u32[]{:S(2)}) copy-start(bf16[8,1792,16]{1,2,0:T(8,128)(2,1)} %param.18) | copy-start | bytes 1376260
  44.4 1.4 copy-start.3
  46.0 31.4 %copy-start.13 = (f32[4]{0:T(128)S(1)}, f32[4]{0:T(128)}, u32[]{:S(2)}) copy-start(f32[4]{0:T(128)} %param.20) | copy-start | bytes 52
  46.0 31.4 %copy-start.14 = (s32[24]{0:T(128)S(1)}, s32[24]{0:T(128)}, u32[]{:S(2)}) copy-start(s32[24]{0:T(128)} %param.26) | copy-start | bytes 292
  48.8 30.4 %copy-start.12 = (bf16[2,224,1024]{2,1,0:T(8,128)(2,1)S(1)}, bf16[2,224,1024]{2,1,0:T(8,128)(2,1)}, u32[]{:S(2)}) copy-start(bf16[2,224,1024]{2,1,0:T(8,128)(2,1)} %param.19) | copy-start | bytes 2752516
  137.3 1.6 copy-start.8
  138.9 9.6 %copy-start.7 = (bf16[768,2,112]{0,2,1:T(8,128)(2,1)S(1)}, bf16[768,2,112]{0,2,1:T(8,128)(2,1)}, u32[]{:S(2)}) copy-start(bf16[768,2,112]{0,2,1:T(8,128)(2,1)} %get-tuple-element.21) | copy-start | bytes 1032196
  148.5 7.6 %copy-start.5 = (bf16[224,1792]{1,0:T(8,128)(2,1)S(1)}, bf16[224,1792]{1,0:T(8,128)(2,1)}, u32[]{:S(2)}) copy-start(bf16[224,1792]{1,0:T(8,128)(2,1)} %param.17) | copy-start | bytes 2408452
  158.5 0.9 copy-start.10
  158.5 92.0 %all-gather.2.cloned.1.call-start = ((), (), s32[]{:S(2)}) async-start(), calls=%async_computation.4 | async-start | bytes 7096320 | tf_op jit(solution)/shard_map/all_gather | solution.py:203
  159.1 134.9 %reduce-scatter.5.cloned.1.call-start = ((), (), s32[]{:S(2)}) async-start(), calls=%async_computation.6 | async-start | bytes 1548288 | tf_op jit(solution)/shard_map/reduce_scatter | solution.py:217
  234.9 1.6 copy-start.2
  237.9 22.8 %copy-start.4 = (bf16[8,1,48,1792]{3,2,1,0:T(8,128)(2,1)}, bf16[8,1,48,1792]{3,2,1,0:T(8,128)(2,1)S(1)}, u32[]{:S(2)}) copy-start(bf16[8,1,48,1792]{3,2,1,0:T(8,128)(2,1)S(1)} %get-tuple-element.13) | copy-start | bytes 4128772
  260.6 69.8 %reduce-scatter.3.cloned.1.call-start = ((), (), s32[]{:S(2)}) async-start(), calls=%async_computation.5 | async-start | bytes 1548288 | tf_op jit(solution)/shard_map/reduce_scatter | solution.py:217
  263.6 68.7 %copy-start.1 = (bf16[3,224,1792]{2,1,0:T(8,128)(2,1)S(1)}, bf16[3,224,1792]{2,1,0:T(8,128)(2,1)}, u32[]{:S(2)}) copy-start(bf16[3,224,1792]{2,1,0:T(8,128)(2,1)} %param.16) | copy-start | bytes 7225348
Sparse Core Ops, SparseCore 0:
  158.6 72.4 all-reduce.1
  260.7 33.2 reduce-scatter.4
  296.5 33.7 reduce-scatter.2
Sparse Core Ops, SparseCore 1:
  162.0 88.5 all-gather.1

commit v8 on v6

--- a/solution.py
+++ b/solution.py
@@ -57,16 +57,17 @@
     )(slots, fills, store)
 
 
-def exchange_kernel(sent, out_ref, got, send_sems, recv_sems):
-    peers = lax.axis_size("req")
-    cap = sent.shape[0] // peers
-    me = lax.axis_index("req")
-    mine = lax.axis_index("mdl")
+def scatter_sum_kernel(part_ref, out_ref, got, send_sems, recv_sems):
+    peers = lax.axis_size("mdl")
+    rows = out_ref.shape[0]
+    me = lax.axis_index("mdl")
+    group = lax.axis_index("req")
+    got[me] = part_ref[pl.ds(me * rows, rows)]
     barrier = pltpu.get_barrier_semaphore()
 
     def greet(k, carry):
         peer = lax.rem(me + k, peers)
-        pl.semaphore_signal(barrier, inc=1, device_id=(peer, mine), device_id_type=pl.DeviceIdType.MESH)
+        pl.semaphore_signal(barrier, inc=1, device_id=(group, peer), device_id_type=pl.DeviceIdType.MESH)
         return carry
 
     lax.fori_loop(1, peers, greet, 0)
@@ -75,11 +76,11 @@
     def send(k):
         peer = lax.rem(me + k, peers)
         return pltpu.make_async_remote_copy(
-            src_ref=sent.at[pl.ds(peer * cap, cap)],
-            dst_ref=got.at[pl.ds(me * cap, cap)],
+            src_ref=part_ref.at[pl.ds(peer * rows, rows)],
+            dst_ref=got.at[me],
             send_sem=send_sems.at[k],
             recv_sem=recv_sems.at[k],
-            device_id=(peer, mine),
+            device_id=(group, peer),
             device_id_type=pl.DeviceIdType.MESH,
         )
 
@@ -88,29 +89,32 @@
         return carry
 
     lax.fori_loop(1, peers, start_send, 0)
-    got[pl.ds(me * cap, cap)] = sent[pl.ds(me * cap, cap)]
 
     def finish(k, carry):
         send(k).wait()
         return carry
 
     lax.fori_loop(1, peers, finish, 0)
-    out_ref[...] = got[...]
-
-
-def exchange_windows(windows, peers):
+    total = got[0].astype(jnp.float32)
+    for source in range(1, peers):
+        total = total + got[source].astype(jnp.float32)
+    out_ref[...] = total
+
+
+def scatter_sum(part, peers, collective):
+    rows = part.shape[0] // peers
     return pl.pallas_call(
-        exchange_kernel,
+        scatter_sum_kernel,
         in_specs=[pl.BlockSpec(memory_space=pltpu.VMEM)],
         out_specs=pl.BlockSpec(memory_space=pltpu.VMEM),
         scratch_shapes=[
-            pltpu.VMEM(windows.shape, windows.dtype),
+            pltpu.VMEM((peers, rows) + part.shape[1:], part.dtype),
             pltpu.SemaphoreType.DMA((peers,)),
             pltpu.SemaphoreType.DMA((peers,)),
         ],
-        out_shape=jax.ShapeDtypeStruct(windows.shape, windows.dtype),
-        compiler_params=pltpu.CompilerParams(collective_id=0, has_side_effects=True),
-    )(windows)
+        out_shape=jax.ShapeDtypeStruct((rows,) + part.shape[1:], jnp.float32),
+        compiler_params=pltpu.CompilerParams(collective_id=collective, has_side_effects=True),
+    )(part)
 
 
 def per_device(
@@ -202,12 +206,13 @@
     flat_pick = my_owner * cap_slots + jnp.sum(earlier.astype(jnp.int32), axis=1)
     page_inner = prefix_cache_store.shape[1:3]
     page_rows = prefix_cache_store.shape[3]
-    windows = cut_windows(
+    source_pages = cut_windows(
         prefix_cache_store,
         jnp.clip(send_slot.reshape(-1), 0, prefix_cache_store.shape[0] - 1),
         send_fill.reshape(-1),
     )
-    arrived = exchange_windows(windows, req_devices)
+    source_pages = source_pages.reshape((req_devices, cap_slots, 2, WINDOW, head_column_set))
+    arrived = lax.all_to_all(source_pages, "req", split_axis=0, concat_axis=0, tiled=True)
     prefix = jnp.take(
         arrived.reshape((req_devices * cap_slots, 2, WINDOW, head_column_set)),
         flat_pick,
@@ -264,9 +269,7 @@
         .astype(jnp.bfloat16)
         .astype(jnp.float32)
     )
-    mlp_mine = lax.psum_scatter(
-        mlp_part.astype(jnp.bfloat16), "mdl", scatter_dimension=0, tiled=True
-    ).astype(jnp.float32)
+    mlp_mine = scatter_sum(mlp_part.astype(jnp.bfloat16), lax.axis_size("mdl"), 1)
     return (resid_mine.astype(jnp.float32) + mlp_mine).astype(jnp.bfloat16)
 
 

time: 373 us -> 317 us (0.85); the launches traced: 372 us -> 312 us
  Pallas kernels: 121 us -> 52.6 us
  starting transfers between devices: 0.31 us -> 12.1 us
    pallas_call x1, Pallas kernels: 105 us -> 36.2 us  [scatter_sum(): pl.pallas_call(scatter_sum_kernel, in_specs=[pl.BlockSpec(memory_space=pl...]
    all_to_all x0 -> x1, waiting for transfers between devices: none -> 49.6 us  [per_device(): lax.all_to_all(source_pages, 'req', split_axis=0, concat_axis=0, tiled=True)]
    reduce_scatter x1 -> x0, waiting for transfers between devices: 36 us -> none  [per_device(): lax.psum_scatter(mlp_part.astype(jnp.bfloat16), 'mdl', scatter_dimension=...]
    psum x1, waiting for transfers between devices: 84.5 us -> 72.1 us  [per_device(): lax.psum(attn_part.astype(jnp.bfloat16), 'mdl').astype(jnp.float32)]
    all_to_all x0 -> x1, starting transfers between devices: none -> 11.8 us  [per_device(): lax.all_to_all(source_pages, 'req', split_axis=0, concat_axis=0, tiled=True)]
  transfers between devices with their start and end apart: 3 -> 3, of which waited for: 3 -> 3; matrix products, arithmetic and copies ran while one was open for 1% -> 7% of each run, Pallas kernels for 0% -> 0%
where the time goes in v8:
time: 317 us; the launch traced here: 312 us
  waiting for transfers between devices  136 us (43%)
  Pallas kernels  52.6 us (17%)
  matrix products  43.6 us (14%)
  blocking collectives  26.8 us (8%)
  between operations  15.2 us (5%)
  other arithmetic  14 us (4%)
  local copies, waits for them, and re-layouts  12.3 us (4%)
  starting transfers between devices  12.1 us (4%)
    psum x1, waiting for transfers between devices, per_device(): lax.psum(attn_part.astype(jnp.bfloat16), 'mdl').astype(jnp.float32)  72.1 us
    all_to_all x1, waiting for transfers between devices, per_device(): lax.all_to_all(source_pages, 'req', split_axis=0, concat_axis=0, tiled=True)  49.6 us
    pallas_call x1, Pallas kernels, scatter_sum(): pl.pallas_call(scatter_sum_kernel, in_specs=[pl.BlockSpec(memory_space=pl...  36.2 us
    psum x1, blocking collectives, per_device(): rank_feat = lax.psum(rank_part.astype(jnp.bfloat16), 'mdl')  26.8 us
    pallas_call x1, Pallas kernels, cut_windows(): pl.pallas_call(window_kernel, grid_spec=pltpu.PrefetchScalarGridSpec(num_...  16.5 us
    all_gather x1, waiting for transfers between devices, per_device(): full_mlp = lax.all_gather(feedforward_weight, 'req', axis=1, tiled=True)  13.6 us
    all_to_all x1, starting transfers between devices, per_device(): lax.all_to_all(source_pages, 'req', split_axis=0, concat_axis=0, tiled=True)  11.8 us
    dot_general x1, matrix products, per_device(): jnp.einsum('tf,df->td', hidden, full_mlp[2], preferred_element_type=jnp.f...  10.5 us
  transfers between devices with their start and end apart: 3, of which 3 were waited for; matrix products, arithmetic and copies ran while one was open for 7% of the time, Pallas kernels for 0%

profile of v8, /device:TPU:8, one launch (start us, length us, event | category | flops | bytes accessed | tf_op | source)
XLA Modules:
  0.0 312.3 jit_solution(594859470633811642)
XLA Ops:
  7.4 0.8 fusion.36
  8.4 0.2 reduce_window_sum.18
  8.6 0.8 mul.159
  9.5 0.8 mul.162
  10.4 0.1 copy.26
  10.5 0.6 min.12.slot_ref
  11.1 0.1 copy.28
  11.2 0.6 reshape.162.fill_ref
  11.8 16.5 %shard_map.145 = bf16[64,2,64,224]{3,2,1,0:T(8,128)(2,1)} custom-call(s32[64]{0:T(128)} %min.12.slot_ref, s32[64]{0:T(128)} %reshape.162.fill_ref, bf16[32,2,224,128]{3,2,1,0:T(8,128)(2,1)} %store_ref.1), custom_call_target="tpu_custom_call" | custom-call | tf_op jit(solution)/shard_map/pallas_call | solution.py:44
  28.3 11.8 %all-to-all-start = ((bf16[32,2,2,64,224]{4,3,2,1,0:T(8,128)(2,1)}), bf16[32,2,2,64,224]{4,3,2,1,0:T(8,128)(2,1)}, u32[]{:S(2)}, u32[]{:S(2)}) async-start(bf16[32,2,2,64,224]{4,3,2,1,0:T(8,128)(2,1)} %bitcast.65), calls=%async_computation | async-start | bytes 8388608 | tf_op jit(solution)/shard_map/all_to_all | solution.py:215
  40.1 0.1 copy.21
  40.3 0.1 reduce
  40.5 3.9 %fusion.17 = f32[3,768,224]{1,2,0:T(8,128)S(1)} fusion(bf16[3,224,1792]{2,1,0:T(8,128)(2,1)S(1)} %copy-done, bf16[768,1792]{1,0:T(8,128)(2,1)} %param.15), kind=kOutput, calls=%fused_computation.33 | convolution fusion | flops 1849688064 | bytes 7225344 | tf_op jit(solution)/shard_map/td,kcd->ktc/dot_general | solution.py:148
  44.4 1.4 copy-done.2
  46.0 2.8 fusion.52
  48.8 26.8 %psum.14 = bf16[768,16]{0,1:T(8,128)(2,1)S(1)} all-reduce(bf16[768,16]{0,1:T(8,128)(2,1)S(1)} %multiply_reduce_fusion), channel_id=1, replica_groups=mesh['req'=32,'mdl'=8] {'mdl'}, use_global_device_ids=true, to_apply=%region_4.5 | all-reduce | flops 12288 | bytes 49152 | tf_op jit(solution)/shard_map/psum | solution.py:163
  75.6 0.8 fusion.39
  76.4 0.2 convert_reduce_fusion
  76.6 0.8 fusion.38
  77.4 0.1 select_reduce_fusion.2
  77.5 0.1 select_reduce_fusion.1
  77.7 0.1 broadcast_multiply_fusion
  77.8 1.4 fusion.48
  79.2 0.9 fusion.53
  80.1 0.1 fusion.50
  80.2 0.3 fusion.14
  80.5 1.1 add_convert_fusion.3
  81.6 1.2 compare_and_fusion
  82.9 1.3 pad_add_fusion
  84.2 49.6 %all-to-all-done = bf16[32,2,2,64,224]{4,3,2,1,0:T(8,128)(2,1)} async-done(((bf16[32,2,2,64,224]{4,3,2,1,0:T(8,128)(2,1)}), bf16[32,2,2,64,224]{4,3,2,1,0:T(8,128)(2,1)}, u32[]{:S(2)}, u32[]{:S(2)}) %all-to-all-start) | async-done | bytes 3670048 | tf_op jit(solution)/shard_map/all_to_all | solution.py:215
  133.8 2.8 gather_fusion
  136.7 0.2 fusion.49
  136.8 0.4 concatenate.18
  137.3 0.6 copy.30
  137.9 0.4 concatenate.15
  138.3 0.6 copy.29
  138.9 9.6 %fusion.51 = (f32[2,768]{1,0:T(2,128)S(1)}, f32[2,768,2304]{2,1,0:T(8,128)}) fusion(pred[768,2304]{1,0:T(8,128)(4,1)} %pad_add_fusion, bf16[768,2,112]{0,2,1:T(8,128)(2,1)S(1)} %copy-done.6, bf16[1536,2,112]{0,2,1:T(8,128)(2,1)S(1)} %copy.30, bf16[768,2,112]{0,2,1:T(8,128)(2,1)S(1)} %bitcast.73), kind=kOutput, calls=%fused_computation.90 | convolution fusion | flops 808945920 | bytes 17307648 | tf_op jit(solution)/shard_map/sub | solution.py:244
  148.5 7.6 %fusion.22 = bf16[2,112,768]{2,1,0:T(8,128)(2,1)S(1)} fusion(f32[2,768,2304]{2,1,0:T(8,128)} %get-tuple-element.20, f32[2,768]{1,0:T(2,128)S(1)} %get-tuple-element.19, bf16[1536,2,112]{0,2,1:T(8,128)(2,1)S(1)} %copy.29, bf16[768,2,112]{0,2,1:T(8,128)(2,1)S(1)} %copy-done.5), kind=kOutput, calls=%fused_computation.35 | convolution fusion | flops 802037760 | bytes 15538176 | tf_op jit(solution)/shard_map/hts,shd->thd/dot_general | solution.py:247
  156.1 2.5 convolution_convert_fusion
  158.6 0.3 all-gather.2.cloned.1.call-start
  158.9 0.3 all-gather.2.cloned.1.call-update
  159.2 72.1 %all-reduce.2.cloned.1.call-done = bf16[768,1792]{1,0:T(8,128)(2,1)} async-done(((bf16[768,1792]{1,0:T(8,128)(2,1)}), bf16[768,1792]{1,0:T(8,128)(2,1)}) %all-reduce.2.cloned.1.call-update) | async-done | bytes 2752528 | tf_op jit(solution)/shard_map/psum | solution.py:257
  231.3 5.4 %fusion.6 = (f32[768]{0:T(1024)S(1)}, bf16[768,1792]{1,0:T(8,128)(2,1)}) fusion(bf16[768,1792]{1,0:T(8,128)(2,1)} %all-reduce.2.cloned.1.call-done, bf16[768,1792]{1,0:T(8,128)(2,1)} %param.15), kind=kLoop, calls=%fused_computation.13 | loop fusion | flops 9633024 | bytes 8260608 | tf_op jit(solution)/shard_map/reduce_sum | solution.py:260
  236.7 13.6 %all-gather.2.cloned.1.call-done = bf16[3,1792,608]{2,1,0:T(8,128)(2,1)} async-done(((bf16[3,56,608]{2,1,0:T(8,128)(2,1)}), bf16[3,1792,608]{2,1,0:T(8,128)(2,1)}) %all-gather.2.cloned.1.call-update) | async-done | bytes 6537232 | tf_op jit(solution)/shard_map/all_gather | solution.py:263
  250.3 5.8 %fusion.16 = f32[768,608]{0,1:T(8,128)} fusion(bf16[3,1792,608]{2,1,0:T(8,128)(2,1)} %all-gather.2.cloned.1.call-done, bf16[768,1792]{1,0:T(8,128)(2,1)} %get-tuple-element.10, f32[1792]{0:T(1024)S(1)} %convert_element_type.115, f32[768]{0:T(1024)S(1)} %add_rsqrt_fusion), kind=kOutput, calls=%fused_computation.31 | convolution fusion | flops 1679032320 | bytes 6924288 | tf_op jit(solution)/shard_map/dot_general | solution.py:264
  256.1 10.5 %convolution_convert_fusion.1.part_ref = bf16[768,1792]{1,0:T(8,128)(2,1)} fusion(bf16[3,1792,608]{2,1,0:T(8,128)(2,1)} %all-gather.2.cloned.1.call-done, f32[768,608]{0,1:T(8,128)} %fusion.16, bf16[768,1792]{1,0:T(8,128)(2,1)} %get-tuple-element.10, f32[1792]{0:T(1024)S(1)} %convert_element_type.115, f32[768]{0:T(1024)S(1)} %add_rsqrt_fusion), kind=kOutput, calls=%fused_computation.19 | convolution fusion | flops 3356737536 | bytes 11970560 | tf_op jit(solution)/shard_map/tf,df->td/dot_general | solution.py:268
  266.7 36.2 %shard_map.146 = f32[96,1792]{1,0:T(8,128)} custom-call(bf16[768,1792]{1,0:T(8,128)(2,1)} %convolution_convert_fusion.1.part_ref), custom_call_target="tpu_custom_call" | custom-call | tf_op jit(solution)/shard_map/pallas_call | solution.py:106
  302.9 2.0 add_convert_fusion.1
  (51 shorter events, 1.0 us)
Async XLA Ops:
  7.4 33.2 %copy-start = (bf16[3,224,1792]{2,1,0:T(8,128)(2,1)S(1)}, bf16[3,224,1792]{2,1,0:T(8,128)(2,1)}, u32[]{:S(2)}) copy-start(bf16[3,224,1792]{2,1,0:T(8,128)(2,1)} %param.16) | copy-start | bytes 7225348
  28.3 11.8 %copy-start.9 = (s32[1,24]{1,0:T(1,128)S(1)}, s32[1,24]{1,0:T(1,128)}, u32[]{:S(2)}) copy-start(s32[1,24]{1,0:T(1,128)} %param.25) | copy-start | bytes 292
  28.3 105.5 %all-to-all-start = ((bf16[32,2,2,64,224]{4,3,2,1,0:T(8,128)(2,1)}), bf16[32,2,2,64,224]{4,3,2,1,0:T(8,128)(2,1)}, u32[]{:S(2)}, u32[]{:S(2)}) async-start(bf16[32,2,2,64,224]{4,3,2,1,0:T(8,128)(2,1)} %bitcast.65), calls=%async_computation | async-start | bytes 8388608 | tf_op jit(solution)/shard_map/all_to_all | solution.py:215
  40.1 191.2 %all-reduce.2.cloned.1.call-start = ((), (), s32[]{:S(2)}) async-start(), calls=%async_computation.1 | async-start | bytes 5505024 | tf_op jit(solution)/shard_map/psum | solution.py:257
  40.5 5.4 %copy-start.7 = (s32[768]{0:T(1024)S(1)}, s32[768]{0:T(1024)}, u32[]{:S(2)}) copy-start(s32[768]{0:T(1024)} %param.24) | copy-start | bytes 9220
  40.5 5.4 %copy-start.4 = (bf16[8,1792,16]{1,2,0:T(8,128)(2,1)S(1)}, bf16[8,1792,16]{1,2,0:T(8,128)(2,1)}, u32[]{:S(2)}) copy-start(bf16[8,1792,16]{1,2,0:T(8,128)(2,1)} %param.18) | copy-start | bytes 1376260
  44.4 1.4 copy-start.2
  45.9 31.5 %copy-start.11 = (f32[4]{0:T(128)S(1)}, f32[4]{0:T(128)}, u32[]{:S(2)}) copy-start(f32[4]{0:T(128)} %param.20) | copy-start | bytes 52
  45.9 31.5 %copy-start.12 = (s32[24]{0:T(128)S(1)}, s32[24]{0:T(128)}, u32[]{:S(2)}) copy-start(s32[24]{0:T(128)} %param.26) | copy-start | bytes 292
  48.8 30.4 %copy-start.10 = (bf16[2,224,1024]{2,1,0:T(8,128)(2,1)S(1)}, bf16[2,224,1024]{2,1,0:T(8,128)(2,1)}, u32[]{:S(2)}) copy-start(bf16[2,224,1024]{2,1,0:T(8,128)(2,1)} %param.19) | copy-start | bytes 2752516
  137.3 1.6 copy-start.6
  138.9 9.6 %copy-start.5 = (bf16[768,2,112]{0,2,1:T(8,128)(2,1)S(1)}, bf16[768,2,112]{0,2,1:T(8,128)(2,1)}, u32[]{:S(2)}) copy-start(bf16[768,2,112]{0,2,1:T(8,128)(2,1)} %get-tuple-element.17) | copy-start | bytes 1032196
  148.5 7.6 %copy-start.3 = (bf16[224,1792]{1,0:T(8,128)(2,1)S(1)}, bf16[224,1792]{1,0:T(8,128)(2,1)}, u32[]{:S(2)}) copy-start(bf16[224,1792]{1,0:T(8,128)(2,1)} %param.17) | copy-start | bytes 2408452
  156.0 3.2 %copy-start.8 = (bf16[1792]{0:T(1024)(128)(2,1)S(1)}, bf16[1792]{0:T(1024)(128)(2,1)}, u32[]{:S(2)}) copy-start(bf16[1792]{0:T(1024)(128)(2,1)} %param.21) | copy-start | bytes 10756
  158.6 91.7 %all-gather.2.cloned.1.call-start = ((), (), s32[]{:S(2)}) async-start(), calls=%async_computation.2 | async-start | bytes 7096320 | tf_op jit(solution)/shard_map/all_gather | solution.py:263
  256.1 48.7 %copy-start.1 = (bf16[3,224,1792]{2,1,0:T(8,128)(2,1)S(1)}, bf16[3,224,1792]{2,1,0:T(8,128)(2,1)}, u32[]{:S(2)}) copy-start(bf16[3,224,1792]{2,1,0:T(8,128)(2,1)} %param.16) | copy-start | bytes 7225348
Sparse Core Ops, SparseCore 0:
  158.7 72.5 all-reduce.1
Sparse Core Ops, SparseCore 1:
  161.8 88.5 all-gather.1

commit v9 on v5

--- a/solution.py
+++ b/solution.py
@@ -159,35 +159,56 @@
         axis=0,
         mode="clip",
     )
+    ext_len = tok_count + req_per_dev * WINDOW
+    block_count = ext_len // WINDOW
+    ext_pos = jnp.arange(ext_len, dtype=jnp.int32)
+    ext_start = starts + WINDOW * jnp.arange(req_per_dev, dtype=jnp.int32)
+    in_req = (
+        (ext_pos[:, None] >= ext_start[None, :])
+        & (ext_pos[:, None] < (ext_start + WINDOW + lengths_row)[None, :])
+    ).astype(jnp.int32)
+    ext_req = jnp.sum(in_req * jnp.arange(req_per_dev, dtype=jnp.int32)[None, :], axis=1)
+    ext_off = ext_pos - jnp.sum(in_req * ext_start[None, :], axis=1)
+    token_src = jnp.sum(in_req * starts[None, :], axis=1) + ext_off - WINDOW
+    prefix_src = tok_count + ext_req * WINDOW + ext_off
+    src = jnp.where(ext_off < WINDOW, prefix_src, token_src)
     key_all = jnp.concatenate(
         [key_rows, prefix[:, 0].reshape(req_per_dev * WINDOW, head_column_set)], axis=0
     )
     value_all = jnp.concatenate(
         [value_row_block, prefix[:, 1].reshape(req_per_dev * WINDOW, head_column_set)], axis=0
     )
-    distance = positions[:, None] - positions[None, :]
-    local_ok = (request_of[:, None] == request_of[None, :]) & (distance >= 0) & (distance <= WINDOW)
-    key_request = jnp.repeat(jnp.arange(req_per_dev, dtype=jnp.int32), WINDOW)
-    key_offset = jnp.tile(jnp.arange(WINDOW, dtype=jnp.int32), req_per_dev)
-    prefix_ok = (request_of[:, None] == key_request[None, :]) & (
-        key_offset[None, :] >= relative[:, None]
-    )
-    allowed = jnp.concatenate([local_ok, prefix_ok], axis=1)
-    query_heads = query_rows.reshape(tok_count, head_local, HEAD_SIZE)
-    key_heads = key_all.reshape(-1, head_local, HEAD_SIZE)
-    value_heads = value_all.reshape(-1, head_local, HEAD_SIZE)
+    key_ext = jnp.take(key_all, src, axis=0, mode="clip")
+    value_ext = jnp.take(value_all, src, axis=0, mode="clip")
+    query_ext = jnp.take(query_rows, jnp.clip(src, 0, tok_count - 1), axis=0, mode="clip")
+
+    def pair_blocks(rows, fill):
+        padded = jnp.concatenate(
+            [jnp.full((WINDOW,) + rows.shape[1:], fill, rows.dtype), rows], axis=0
+        ).reshape((block_count + 1, WINDOW) + rows.shape[1:])
+        return jnp.concatenate([padded[:-1], padded[1:]], axis=1)
+
+    query_heads = query_ext.reshape(block_count, WINDOW, head_local, HEAD_SIZE)
+    key_heads = pair_blocks(key_ext, 0).reshape(block_count, 2 * WINDOW, head_local, HEAD_SIZE)
+    value_heads = pair_blocks(value_ext, 0).reshape(block_count, 2 * WINDOW, head_local, HEAD_SIZE)
+    key_req = pair_blocks(ext_req, -1)
+    query_req = ext_req.reshape(block_count, WINDOW)
+    gap = WINDOW + jnp.arange(WINDOW, dtype=jnp.int32)[:, None] - jnp.arange(2 * WINDOW, dtype=jnp.int32)[None, :]
+    allowed = (query_req[:, :, None] == key_req[:, None, :]) & (gap >= 0)[None] & (gap <= WINDOW)[None]
     scores = jnp.einsum(
-        "thd,shd->hts", query_heads, key_heads, preferred_element_type=jnp.float32
+        "bqhd,bkhd->hbqk", query_heads, key_heads, preferred_element_type=jnp.float32
     ) * (1.0 / math.sqrt(HEAD_SIZE))
     masked = jnp.where(allowed[None], scores, -1e30)
     row_max = jnp.max(masked, axis=-1, keepdims=True)
     exp_scores = jnp.exp(masked - row_max)
     weights = (exp_scores / jnp.sum(exp_scores, axis=-1, keepdims=True)).astype(jnp.bfloat16)
-    mixed = (
-        jnp.einsum("hts,shd->thd", weights, value_heads, preferred_element_type=jnp.float32)
+    mixed_ext = (
+        jnp.einsum("hbqk,bkhd->bqhd", weights, value_heads, preferred_element_type=jnp.float32)
         .astype(jnp.bfloat16)
-        .reshape(tok_count, head_column_set)
-    )
+        .reshape(ext_len, head_column_set)
+    )
+    token_ext = positions + WINDOW * (request_of + 1)
+    mixed = jnp.take(mixed_ext, token_ext, axis=0, mode="clip")
     attn_part = (
         jnp.dot(mixed, head_output_weight, preferred_element_type=jnp.float32)
         .astype(jnp.bfloat16)

time: 313 us -> 345 us (1.10)
  local copies, waits for them, and re-layouts: 12.3 us -> 59.6 us
  waiting for transfers between devices: 172 us -> 164 us
  matrix products: 43.6 us -> 37.6 us
    gather x0 -> x4, local copies, waits for them, and re-layouts: none -> 23.2 us  [the longest x1 6.86 us: per_device(): jnp.take(query_rows, jnp.clip(src, 0, tok_count - 1), axis=0, mode='clip')]
    concatenate x4 -> x8, local copies, waits for them, and re-layouts: 1.99 us -> 18.8 us  [pair_blocks(): return jnp.concatenate([padded[:-1], padded[1:]], axis=1)]
    all_to_all x1, waiting for transfers between devices: 49.6 us -> 42.2 us  [per_device(): lax.all_to_all(source_pages, 'req', split_axis=0, concat_axis=0, tiled=True)]
    dot_general x1, matrix products: 7.56 us -> 3.75 us  [per_device(): jnp.einsum('hbqk,bkhd->bqhd', weights, value_heads, preferred_element_typ...]
    sub x1, matrix products: 9.57 us -> 6.03 us  [per_device(): exp_scores = jnp.exp(masked - row_max)]
  transfers between devices with their start and end apart: 4 -> 4, of which waited for: 4 -> 4; matrix products, arithmetic and copies ran while one was open for 7% -> 8% of each run, Pallas kernels for 0% -> 0%
where the time goes in v9:
time: 345 us
  waiting for transfers between devices  164 us (48%)
  local copies, waits for them, and re-layouts  59.6 us (17%)
  matrix products  37.6 us (11%)
  blocking collectives  26.7 us (8%)
  Pallas kernels  16.5 us (5%)
  between operations  15.3 us (4%)
  other arithmetic  12.6 us (4%)
  starting transfers between devices  12.2 us (4%)
    psum x1, waiting for transfers between devices, per_device(): lax.psum(attn_part.astype(jnp.bfloat16), 'mdl').astype(jnp.float32)  71.7 us
    all_to_all x1, waiting for transfers between devices, per_device(): lax.all_to_all(source_pages, 'req', split_axis=0, concat_axis=0, tiled=True)  42.2 us
    reduce_scatter x1, waiting for transfers between devices, per_device(): lax.psum_scatter(mlp_part.astype(jnp.bfloat16), 'mdl', scatter_dimension=...  36 us
    psum x1, blocking collectives, per_device(): rank_feat = lax.psum(rank_part.astype(jnp.bfloat16), 'mdl')  26.7 us
    concatenate x8, local copies, waits for them, and re-layouts, pair_blocks(): return jnp.concatenate([padded[:-1], padded[1:]], axis=1)  18.8 us
    pallas_call x1, Pallas kernels, cut_windows(): pl.pallas_call(window_kernel, grid_spec=pltpu.PrefetchScalarGridSpec(num_...  16.5 us
    all_gather x1, waiting for transfers between devices, per_device(): full_mlp = lax.all_gather(feedforward_weight, 'req', axis=1, tiled=True)  14.1 us
    all_to_all x1, starting transfers between devices, per_device(): lax.all_to_all(source_pages, 'req', split_axis=0, concat_axis=0, tiled=True)  11.8 us
  transfers between devices with their start and end apart: 4, of which 4 were waited for; matrix products, arithmetic and copies ran while one was open for 8% of the time, Pallas kernels for 0%

profile of v9, /device:TPU:8, one launch (start us, length us, event | category | flops | bytes accessed | tf_op | source)
XLA Modules:
  0.0 344.8 jit_solution(15474620556009801512)
XLA Ops:
  7.4 0.8 fusion.50
  8.6 0.8 mul.215
  9.5 0.8 mul.218
  10.5 0.6 min.20.slot_ref
  11.2 0.6 reshape.299.fill_ref
  11.8 16.5 %shard_map.145 = bf16[64,2,64,224]{3,2,1,0:T(8,128)(2,1)} custom-call(s32[64]{0:T(128)} %min.20.slot_ref, s32[64]{0:T(128)} %reshape.299.fill_ref, bf16[32,2,224,128]{3,2,1,0:T(8,128)(2,1)} %store_ref.1), custom_call_target="tpu_custom_call" | custom-call | tf_op jit(solution)/shard_map/pallas_call | solution.py:44
  28.3 11.8 %all-to-all-start = ((bf16[32,2,2,64,224]{4,3,2,1,0:T(8,128)(2,1)}), bf16[32,2,2,64,224]{4,3,2,1,0:T(8,128)(2,1)}, u32[]{:S(2)}, u32[]{:S(2)}) async-start(bf16[32,2,2,64,224]{4,3,2,1,0:T(8,128)(2,1)} %bitcast.89), calls=%async_computation | async-start | bytes 8388608 | tf_op jit(solution)/shard_map/all_to_all | solution.py:155
  40.4 3.9 %fusion.17 = f32[3,768,224]{1,2,0:T(8,128)S(1)} fusion(bf16[3,224,1792]{2,1,0:T(8,128)(2,1)S(1)} %copy-done, bf16[768,1792]{1,0:T(8,128)(2,1)} %param.15), kind=kOutput, calls=%fused_computation.34 | convolution fusion | flops 1849688064 | bytes 7225344 | tf_op jit(solution)/shard_map/td,kcd->ktc/dot_general | solution.py:88
  44.3 1.4 copy-done.7
  45.7 0.9 copy.46
  46.7 2.8 fusion.70
  49.6 26.7 %psum.14 = bf16[768,16]{0,1:T(8,128)(2,1)S(1)} all-reduce(bf16[768,16]{0,1:T(8,128)(2,1)S(1)} %multiply_reduce_fusion), channel_id=1, replica_groups=mesh['req'=32,'mdl'=8] {'mdl'}, use_global_device_ids=true, to_apply=%region_4.5 | all-reduce | flops 12288 | bytes 49152 | tf_op jit(solution)/shard_map/psum | solution.py:103
  76.6 2.2 fusion.71
  79.7 6.9 %gather_fusion.2 = bf16[2304,224]{1,0:T(8,128)(2,1)S(1)} fusion(bf16[768,224]{1,0:T(8,128)(2,1)S(1)} %copy.45, s32[3072]{0:T(1024)S(1)} %get-tuple-element.27), kind=kCustom, calls=%fused_computation.2 | custom fusion | bytes 2073600 | tf_op jit(solution)/shard_map/jit(_take)/gather | solution.py:183
  86.5 1.5 reshape.302
  88.1 1.0 copy.42
  89.2 0.8 fusion.53
  90.2 0.8 fusion.51
  91.1 0.6 and_and_fusion
  91.7 42.2 %all-to-all-done = bf16[32,2,2,64,224]{4,3,2,1,0:T(8,128)(2,1)} async-done(((bf16[32,2,2,64,224]{4,3,2,1,0:T(8,128)(2,1)}), bf16[32,2,2,64,224]{4,3,2,1,0:T(8,128)(2,1)}, u32[]{:S(2)}, u32[]{:S(2)}) %all-to-all-start) | async-done | bytes 3670048 | tf_op jit(solution)/shard_map/all_to_all | solution.py:155
  133.8 2.8 gather_fusion
  136.9 0.8 copy-done.6
  137.9 6.9 %gather_fusion.3 = bf16[2304,224]{1,0:T(8,128)(2,1)S(1)} fusion(bf16[2304,224]{1,0:T(8,128)(2,1)S(1)} %pad_maximum_fusion.1, s32[3072]{0:T(1024)S(1)} %get-tuple-element.28), kind=kCustom, calls=%fused_computation.3 | custom fusion | bytes 2073600 | tf_op jit(solution)/shard_map/jit(_take)/gather | solution.py:181
  144.7 1.2 pad_slice_fusion
  145.9 1.5 concatenate.44
  147.4 1.2 pad_maximum_fusion
  148.6 6.9 %gather_fusion.1 = bf16[2304,224]{1,0:T(8,128)(2,1)S(1)} fusion(bf16[2304,224]{1,0:T(8,128)(2,1)S(1)} %pad_maximum_fusion, s32[3072]{0:T(1024)S(1)} %get-tuple-element.28), kind=kCustom, calls=%fused_computation.1 | custom fusion | bytes 2073600 | tf_op jit(solution)/shard_map/jit(_take)/gather | solution.py:182
  155.5 1.2 pad_slice_fusion.1
  156.7 1.5 concatenate.37
  158.2 0.7 concatenate.43
  158.9 3.0 copy.47
  161.9 3.0 copy.48
  165.0 3.1 concatenate.36
  168.1 3.0 copy.43
  171.1 3.0 copy.44
  174.1 6.0 %fusion.61 = (f32[2,36,64]{2,1,0:T(8,128)S(1)}, f32[2,36,64,128]{3,2,1,0:T(8,128)}) fusion(pred[36,64,128]{2,1,0:T(8,128)(4,1)S(1)} %and_and_fusion, bf16[36,64,2,112]{1,3,0,2:T(8,128)(2,1)} %copy.48, bf16[36,64,2,112]{1,3,0,2:T(8,128)(2,1)} %copy.47, bf16[36,64,2,112]{3,2,1,0:T(2,128)(2,1)} %reshape.302), kind=kOutput, calls=%fused_computation.123 | convolution fusion | flops 138608768 | bytes 5769216 | tf_op jit(solution)/shard_map/sub | solution.py:203
  180.1 3.7 %fusion.23 = bf16[36,64,2,112]{3,1,2,0:T(8,128)(2,1)S(1)} fusion(bf16[36,64,2,112]{1,3,2,0:T(8,128)(2,1)} %copy.44, bf16[36,64,2,112]{1,3,2,0:T(8,128)(2,1)S(1)} %copy-done.5, f32[2,36,64,128]{3,2,1,0:T(8,128)} %get-tuple-element.26, f32[2,36,64]{2,1,0:T(8,128)S(1)} %get-tuple-element.25), kind=kOutput, calls=%fused_computation.36 | convolution fusion | flops 137945088 | bytes 5474304 | tf_op jit(solution)/shard_map/hbqk,bkhd->bqhd/dot_general | solution.py:206
  183.9 1.2 copy.51
  185.1 0.7 reshape.303
  185.9 2.7 gather_fusion.4
  188.6 2.5 convolution_convert_fusion.1
  192.0 71.7 %all-reduce.5.cloned.1.call-done = bf16[768,1792]{1,0:T(8,128)(2,1)} async-done(((bf16[768,1792]{1,0:T(8,128)(2,1)}), bf16[768,1792]{1,0:T(8,128)(2,1)}) %all-reduce.5.cloned.1.call-update) | async-done | bytes 2752528 | tf_op jit(solution)/shard_map/psum | solution.py:218
  263.7 5.3 %fusion.1 = (f32[768]{0:T(1024)S(1)}, bf16[768,1792]{1,0:T(8,128)(2,1)}) fusion(bf16[768,1792]{1,0:T(8,128)(2,1)} %all-reduce.5.cloned.1.call-done, bf16[768,1792]{1,0:T(8,128)(2,1)} %param.15), kind=kLoop, calls=%fused_computation.8 | loop fusion | flops 9633024 | bytes 8260608 | tf_op jit(solution)/shard_map/reduce_sum | solution.py:221
  269.0 14.1 %all-gather.2.cloned.1.call-done = bf16[3,1792,608]{2,1,0:T(8,128)(2,1)} async-done(((bf16[3,56,608]{2,1,0:T(8,128)(2,1)}), bf16[3,1792,608]{2,1,0:T(8,128)(2,1)}) %all-gather.2.cloned.1.call-update) | async-done | bytes 6537232 | tf_op jit(solution)/shard_map/all_gather | solution.py:224
  283.1 5.8 %fusion.7 = f32[768,608]{0,1:T(8,128)} fusion(bf16[3,1792,608]{2,1,0:T(8,128)(2,1)} %all-gather.2.cloned.1.call-done, bf16[768,1792]{1,0:T(8,128)(2,1)} %get-tuple-element.13, f32[1792]{0:T(1024)S(1)} %convert_element_type.116, f32[768]{0:T(1024)S(1)} %add_rsqrt_fusion), kind=kOutput, calls=%fused_computation.23 | convolution fusion | flops 1679032320 | bytes 6924288 | tf_op jit(solution)/shard_map/dot_general | solution.py:225
  288.9 10.5 %convolution_convert_fusion = bf16[768,1792]{1,0:T(8,128)(2,1)} fusion(bf16[3,1792,608]{2,1,0:T(8,128)(2,1)} %all-gather.2.cloned.1.call-done, f32[768,608]{0,1:T(8,128)} %fusion.7, bf16[768,1792]{1,0:T(8,128)(2,1)} %get-tuple-element.13, f32[1792]{0:T(1024)S(1)} %convert_element_type.116, f32[768]{0:T(1024)S(1)} %add_rsqrt_fusion), kind=kOutput, calls=%fused_computation.12 | convolution fusion | flops 3356737536 | bytes 11970560 | tf_op jit(solution)/shard_map/tf,df->td/dot_general | solution.py:229
  299.5 36.0 %reduce-scatter.2.cloned.1.call-done = bf16[96,1792]{1,0:T(8,128)(2,1)} async-done(((bf16[768,1792]{1,0:T(8,128)(2,1)}), bf16[96,1792]{1,0:T(8,128)(2,1)}) %reduce-scatter.2.cloned.1.call-update) | async-done | bytes 344080 | tf_op jit(solution)/shard_map/reduce_scatter | solution.py:233
  335.5 1.9 add_convert_fusion.1
  (80 shorter events, 4.2 us)
Async XLA Ops:
  7.4 33.0 %copy-start = (bf16[3,224,1792]{2,1,0:T(8,128)(2,1)S(1)}, bf16[3,224,1792]{2,1,0:T(8,128)(2,1)}, u32[]{:S(2)}) copy-start(bf16[3,224,1792]{2,1,0:T(8,128)(2,1)} %param.16) | copy-start | bytes 7225348
  28.3 11.8 %copy-start.13 = (s32[1,24]{1,0:T(1,128)S(1)}, s32[1,24]{1,0:T(1,128)}, u32[]{:S(2)}) copy-start(s32[1,24]{1,0:T(1,128)} %param.25) | copy-start | bytes 292
  28.3 105.5 %all-to-all-start = ((bf16[32,2,2,64,224]{4,3,2,1,0:T(8,128)(2,1)}), bf16[32,2,2,64,224]{4,3,2,1,0:T(8,128)(2,1)}, u32[]{:S(2)}, u32[]{:S(2)}) async-start(bf16[32,2,2,64,224]{4,3,2,1,0:T(8,128)(2,1)} %bitcast.89), calls=%async_computation | async-start | bytes 8388608 | tf_op jit(solution)/shard_map/all_to_all | solution.py:155
  40.1 223.6 %all-reduce.5.cloned.1.call-start = ((), (), s32[]{:S(2)}) async-start(), calls=%async_computation.2 | async-start | bytes 5505024 | tf_op jit(solution)/shard_map/psum | solution.py:218
  40.4 6.3 %copy-start.11 = (s32[768]{0:T(1024)S(1)}, s32[768]{0:T(1024)}, u32[]{:S(2)}) copy-start(s32[768]{0:T(1024)} %param.24) | copy-start | bytes 9220
  40.4 6.3 %copy-start.10 = (bf16[8,1792,16]{1,2,0:T(8,128)(2,1)S(1)}, bf16[8,1792,16]{1,2,0:T(8,128)(2,1)}, u32[]{:S(2)}) copy-start(bf16[8,1792,16]{1,2,0:T(8,128)(2,1)} %param.18) | copy-start | bytes 1376260
  44.3 1.4 copy-start.7
  46.7 29.5 %copy-start.14 = (f32[4]{0:T(128)S(1)}, f32[4]{0:T(128)}, u32[]{:S(2)}) copy-start(f32[4]{0:T(128)} %param.20) | copy-start | bytes 52
  46.7 29.5 %copy-start.15 = (s32[24]{0:T(128)S(1)}, s32[24]{0:T(128)}, u32[]{:S(2)}) copy-start(s32[24]{0:T(128)} %param.26) | copy-start | bytes 292
  76.6 2.2 copy-start.8
  136.7 1.0 copy-start.6
  155.5 2.7 copy-start.4
  158.9 3.0 copy-start.2
  168.1 3.0 copy-start.3
  174.1 6.0 %copy-start.5 = (bf16[36,64,2,112]{1,3,2,0:T(8,128)(2,1)S(1)}, bf16[36,64,2,112]{1,3,2,0:T(8,128)(2,1)}, u32[]{:S(2)}) copy-start(bf16[36,64,2,112]{1,3,2,0:T(8,128)(2,1)} %copy.43) | copy-start | bytes 3096580
  185.9 2.7 copy-start.9
  191.0 0.9 copy-start.12
  191.1 92.0 %all-gather.2.cloned.1.call-start = ((), (), s32[]{:S(2)}) async-start(), calls=%async_computation.3 | async-start | bytes 7096320 | tf_op jit(solution)/shard_map/all_gather | solution.py:224
  191.6 143.8 %reduce-scatter.2.cloned.1.call-start = ((), (), s32[]{:S(2)}) async-start(), calls=%async_computation.4 | async-start | bytes 3096576 | tf_op jit(solution)/shard_map/reduce_scatter | solution.py:233
  288.9 48.4 %copy-start.1 = (bf16[3,224,1792]{2,1,0:T(8,128)(2,1)S(1)}, bf16[3,224,1792]{2,1,0:T(8,128)(2,1)}, u32[]{:S(2)}) copy-start(bf16[3,224,1792]{2,1,0:T(8,128)(2,1)} %param.16) | copy-start | bytes 7225348
Sparse Core Ops, SparseCore 0:
  191.2 72.4 all-reduce.4
  299.6 35.8 reduce-scatter.1
Sparse Core Ops, SparseCore 1:
  194.6 88.5 all-gather.1

commit v10 on v5

--- a/solution.py
+++ b/solution.py
@@ -21,7 +21,7 @@
         fetch(i).start()
         return carry
 
-    lax.fori_loop(0, count, start, 0)
+    lax.fori_loop(0, count, start, 0, unroll=8)
     page_rows = held.shape[-1]
     row_ids = lax.broadcasted_iota(jnp.int32, (WINDOW, page_rows), 1)
     out_ids = lax.broadcasted_iota(jnp.int32, (WINDOW, page_rows), 0)
@@ -35,7 +35,7 @@
             ).astype(out_ref.dtype)
         return carry
 
-    lax.fori_loop(0, count, pick_rows, 0)
+    lax.fori_loop(0, count, pick_rows, 0, unroll=8)
 
 
 def cut_windows(store, slots, fills):

time: 313 us -> 313 us (level)
  no operation moved by 1% of the time
where the time goes in v10:
time: 313 us; the launch traced here: 312 us
  waiting for transfers between devices  172 us (55%)
  matrix products  43.6 us (14%)
  blocking collectives  26.8 us (9%)
  Pallas kernels  16.5 us (5%)
  between operations  15.2 us (5%)
  other arithmetic  13.9 us (4%)
  local copies, waits for them, and re-layouts  12.3 us (4%)
  starting transfers between devices  12.1 us (4%)
    psum x1, waiting for transfers between devices, per_device(): lax.psum(attn_part.astype(jnp.bfloat16), 'mdl').astype(jnp.float32)  71.7 us
    all_to_all x1, waiting for transfers between devices, per_device(): lax.all_to_all(source_pages, 'req', split_axis=0, concat_axis=0, tiled=True)  49.6 us
    reduce_scatter x1, waiting for transfers between devices, per_device(): lax.psum_scatter(mlp_part.astype(jnp.bfloat16), 'mdl', scatter_dimension=...  36 us
    psum x1, blocking collectives, per_device(): rank_feat = lax.psum(rank_part.astype(jnp.bfloat16), 'mdl')  26.8 us
    pallas_call x1, Pallas kernels, cut_windows(): pl.pallas_call(window_kernel, grid_spec=pltpu.PrefetchScalarGridSpec(num_...  16.5 us
    all_gather x1, waiting for transfers between devices, per_device(): full_mlp = lax.all_gather(feedforward_weight, 'req', axis=1, tiled=True)  14.1 us
    all_to_all x1, starting transfers between devices, per_device(): lax.all_to_all(source_pages, 'req', split_axis=0, concat_axis=0, tiled=True)  11.8 us
    dot_general x1, matrix products, per_device(): jnp.einsum('tf,df->td', hidden, full_mlp[2], preferred_element_type=jnp.f...  10.5 us
  transfers between devices with their start and end apart: 4, of which 4 were waited for; matrix products, arithmetic and copies ran while one was open for 7% of the time, Pallas kernels for 0%

profile of v10, /device:TPU:8, one launch (start us, length us, event | category | flops | bytes accessed | tf_op | source)
XLA Modules:
  0.0 312.3 jit_solution(7779824217094965593)
XLA Ops:
  7.4 0.8 fusion.36
  8.4 0.2 reduce_window_sum.18
  8.6 0.8 mul.159
  9.5 0.8 mul.162
  10.4 0.1 copy.26
  10.5 0.6 min.12.slot_ref
  11.1 0.1 copy.28
  11.2 0.6 reshape.162.fill_ref
  11.8 16.5 %shard_map.145 = bf16[64,2,64,224]{3,2,1,0:T(8,128)(2,1)} custom-call(s32[64]{0:T(128)} %min.12.slot_ref, s32[64]{0:T(128)} %reshape.162.fill_ref, bf16[32,2,224,128]{3,2,1,0:T(8,128)(2,1)} %store_ref.1), custom_call_target="tpu_custom_call" | custom-call | tf_op jit(solution)/shard_map/pallas_call | solution.py:44
  28.3 11.8 %all-to-all-start = ((bf16[32,2,2,64,224]{4,3,2,1,0:T(8,128)(2,1)}), bf16[32,2,2,64,224]{4,3,2,1,0:T(8,128)(2,1)}, u32[]{:S(2)}, u32[]{:S(2)}) async-start(bf16[32,2,2,64,224]{4,3,2,1,0:T(8,128)(2,1)} %bitcast.65), calls=%async_computation | async-start | bytes 8388608 | tf_op jit(solution)/shard_map/all_to_all | solution.py:155
  40.1 0.1 copy.21
  40.3 0.1 reduce
  40.5 3.9 %fusion.17 = f32[3,768,224]{1,2,0:T(8,128)S(1)} fusion(bf16[3,224,1792]{2,1,0:T(8,128)(2,1)S(1)} %copy-done, bf16[768,1792]{1,0:T(8,128)(2,1)} %param.15), kind=kOutput, calls=%fused_computation.33 | convolution fusion | flops 1849688064 | bytes 7225344 | tf_op jit(solution)/shard_map/td,kcd->ktc/dot_general | solution.py:88
  44.4 1.4 copy-done.2
  46.0 2.8 fusion.52
  48.8 26.8 %psum.14 = bf16[768,16]{0,1:T(8,128)(2,1)S(1)} all-reduce(bf16[768,16]{0,1:T(8,128)(2,1)S(1)} %multiply_reduce_fusion), channel_id=1, replica_groups=mesh['req'=32,'mdl'=8] {'mdl'}, use_global_device_ids=true, to_apply=%region_4.5 | all-reduce | flops 12288 | bytes 49152 | tf_op jit(solution)/shard_map/psum | solution.py:103
  75.6 0.8 fusion.39
  76.4 0.2 convert_reduce_fusion
  76.6 0.8 fusion.38
  77.4 0.1 select_reduce_fusion.2
  77.5 0.1 select_reduce_fusion.1
  77.7 0.1 broadcast_multiply_fusion
  77.8 1.4 fusion.48
  79.2 0.9 fusion.53
  80.1 0.1 fusion.50
  80.2 0.3 fusion.14
  80.5 1.1 add_convert_fusion.3
  81.6 1.2 compare_and_fusion
  82.9 1.3 pad_add_fusion
  84.2 49.6 %all-to-all-done = bf16[32,2,2,64,224]{4,3,2,1,0:T(8,128)(2,1)} async-done(((bf16[32,2,2,64,224]{4,3,2,1,0:T(8,128)(2,1)}), bf16[32,2,2,64,224]{4,3,2,1,0:T(8,128)(2,1)}, u32[]{:S(2)}, u32[]{:S(2)}) %all-to-all-start) | async-done | bytes 3670048 | tf_op jit(solution)/shard_map/all_to_all | solution.py:155
  133.8 2.8 gather_fusion
  136.7 0.2 fusion.49
  136.8 0.4 concatenate.18
  137.3 0.6 copy.30
  137.9 0.4 concatenate.15
  138.3 0.6 copy.29
  138.9 9.6 %fusion.51 = (f32[2,768]{1,0:T(2,128)S(1)}, f32[2,768,2304]{2,1,0:T(8,128)}) fusion(pred[768,2304]{1,0:T(8,128)(4,1)} %pad_add_fusion, bf16[768,2,112]{0,2,1:T(8,128)(2,1)S(1)} %copy-done.6, bf16[1536,2,112]{0,2,1:T(8,128)(2,1)S(1)} %copy.30, bf16[768,2,112]{0,2,1:T(8,128)(2,1)S(1)} %bitcast.73), kind=kOutput, calls=%fused_computation.90 | convolution fusion | flops 808945920 | bytes 17307648 | tf_op jit(solution)/shard_map/sub | solution.py:184
  148.5 7.6 %fusion.22 = bf16[2,112,768]{2,1,0:T(8,128)(2,1)S(1)} fusion(f32[2,768,2304]{2,1,0:T(8,128)} %get-tuple-element.20, f32[2,768]{1,0:T(2,128)S(1)} %get-tuple-element.19, bf16[1536,2,112]{0,2,1:T(8,128)(2,1)S(1)} %copy.29, bf16[768,2,112]{0,2,1:T(8,128)(2,1)S(1)} %copy-done.5), kind=kOutput, calls=%fused_computation.35 | convolution fusion | flops 802037760 | bytes 15538176 | tf_op jit(solution)/shard_map/hts,shd->thd/dot_general | solution.py:187
  156.1 2.5 convolution_convert_fusion
  158.7 0.5 all-gather.2.cloned.1.call-update
  159.2 0.3 reduce-scatter.2.cloned.1.call-start
  159.5 71.7 %all-reduce.2.cloned.1.call-done = bf16[768,1792]{1,0:T(8,128)(2,1)} async-done(((bf16[768,1792]{1,0:T(8,128)(2,1)}), bf16[768,1792]{1,0:T(8,128)(2,1)}) %all-reduce.2.cloned.1.call-update) | async-done | bytes 2752528 | tf_op jit(solution)/shard_map/psum | solution.py:197
  231.2 5.3 %fusion.6 = (f32[768]{0:T(1024)S(1)}, bf16[768,1792]{1,0:T(8,128)(2,1)}) fusion(bf16[768,1792]{1,0:T(8,128)(2,1)} %all-reduce.2.cloned.1.call-done, bf16[768,1792]{1,0:T(8,128)(2,1)} %param.15), kind=kLoop, calls=%fused_computation.13 | loop fusion | flops 9633024 | bytes 8260608 | tf_op jit(solution)/shard_map/reduce_sum | solution.py:200
  236.6 14.1 %all-gather.2.cloned.1.call-done = bf16[3,1792,608]{2,1,0:T(8,128)(2,1)} async-done(((bf16[3,56,608]{2,1,0:T(8,128)(2,1)}), bf16[3,1792,608]{2,1,0:T(8,128)(2,1)}) %all-gather.2.cloned.1.call-update) | async-done | bytes 6537232 | tf_op jit(solution)/shard_map/all_gather | solution.py:203
  250.6 5.8 %fusion.16 = f32[768,608]{0,1:T(8,128)} fusion(bf16[3,1792,608]{2,1,0:T(8,128)(2,1)} %all-gather.2.cloned.1.call-done, bf16[768,1792]{1,0:T(8,128)(2,1)} %get-tuple-element.10, f32[1792]{0:T(1024)S(1)} %convert_element_type.118, f32[768]{0:T(1024)S(1)} %add_rsqrt_fusion), kind=kOutput, calls=%fused_computation.31 | convolution fusion | flops 1679032320 | bytes 6924288 | tf_op jit(solution)/shard_map/dot_general | solution.py:204
  256.5 10.5 %convolution_convert_fusion.1 = bf16[768,1792]{1,0:T(8,128)(2,1)} fusion(bf16[3,1792,608]{2,1,0:T(8,128)(2,1)} %all-gather.2.cloned.1.call-done, f32[768,608]{0,1:T(8,128)} %fusion.16, bf16[768,1792]{1,0:T(8,128)(2,1)} %get-tuple-element.10, f32[1792]{0:T(1024)S(1)} %convert_element_type.118, f32[768]{0:T(1024)S(1)} %add_rsqrt_fusion), kind=kOutput, calls=%fused_computation.19 | convolution fusion | flops 3356737536 | bytes 11970560 | tf_op jit(solution)/shard_map/tf,df->td/dot_general | solution.py:208
  267.1 36.0 %reduce-scatter.2.cloned.1.call-done = bf16[96,1792]{1,0:T(8,128)(2,1)} async-done(((bf16[768,1792]{1,0:T(8,128)(2,1)}), bf16[96,1792]{1,0:T(8,128)(2,1)}) %reduce-scatter.2.cloned.1.call-update) | async-done | bytes 344080 | tf_op jit(solution)/shard_map/reduce_scatter | solution.py:212
  303.0 1.9 add_convert_fusion.1
  (53 shorter events, 1.1 us)
Async XLA Ops:
  7.4 33.2 %copy-start = (bf16[3,224,1792]{2,1,0:T(8,128)(2,1)S(1)}, bf16[3,224,1792]{2,1,0:T(8,128)(2,1)}, u32[]{:S(2)}) copy-start(bf16[3,224,1792]{2,1,0:T(8,128)(2,1)} %param.16) | copy-start | bytes 7225348
  28.3 11.8 %copy-start.9 = (s32[1,24]{1,0:T(1,128)S(1)}, s32[1,24]{1,0:T(1,128)}, u32[]{:S(2)}) copy-start(s32[1,24]{1,0:T(1,128)} %param.25) | copy-start | bytes 292
  28.3 105.5 %all-to-all-start = ((bf16[32,2,2,64,224]{4,3,2,1,0:T(8,128)(2,1)}), bf16[32,2,2,64,224]{4,3,2,1,0:T(8,128)(2,1)}, u32[]{:S(2)}, u32[]{:S(2)}) async-start(bf16[32,2,2,64,224]{4,3,2,1,0:T(8,128)(2,1)} %bitcast.65), calls=%async_computation | async-start | bytes 8388608 | tf_op jit(solution)/shard_map/all_to_all | solution.py:155
  40.1 191.1 %all-reduce.2.cloned.1.call-start = ((), (), s32[]{:S(2)}) async-start(), calls=%async_computation.2 | async-start | bytes 5505024 | tf_op jit(solution)/shard_map/psum | solution.py:197
  40.5 5.4 %copy-start.7 = (s32[768]{0:T(1024)S(1)}, s32[768]{0:T(1024)}, u32[]{:S(2)}) copy-start(s32[768]{0:T(1024)} %param.24) | copy-start | bytes 9220
  40.5 5.4 %copy-start.4 = (bf16[8,1792,16]{1,2,0:T(8,128)(2,1)S(1)}, bf16[8,1792,16]{1,2,0:T(8,128)(2,1)}, u32[]{:S(2)}) copy-start(bf16[8,1792,16]{1,2,0:T(8,128)(2,1)} %param.18) | copy-start | bytes 1376260
  44.4 1.4 copy-start.2
  45.9 31.5 %copy-start.11 = (f32[4]{0:T(128)S(1)}, f32[4]{0:T(128)}, u32[]{:S(2)}) copy-start(f32[4]{0:T(128)} %param.20) | copy-start | bytes 52
  45.9 31.5 %copy-start.12 = (s32[24]{0:T(128)S(1)}, s32[24]{0:T(128)}, u32[]{:S(2)}) copy-start(s32[24]{0:T(128)} %param.26) | copy-start | bytes 292
  48.8 30.4 %copy-start.10 = (bf16[2,224,1024]{2,1,0:T(8,128)(2,1)S(1)}, bf16[2,224,1024]{2,1,0:T(8,128)(2,1)}, u32[]{:S(2)}) copy-start(bf16[2,224,1024]{2,1,0:T(8,128)(2,1)} %param.19) | copy-start | bytes 2752516
  137.3 1.6 copy-start.6
  138.9 9.6 %copy-start.5 = (bf16[768,2,112]{0,2,1:T(8,128)(2,1)S(1)}, bf16[768,2,112]{0,2,1:T(8,128)(2,1)}, u32[]{:S(2)}) copy-start(bf16[768,2,112]{0,2,1:T(8,128)(2,1)} %get-tuple-element.17) | copy-start | bytes 1032196
  148.5 7.6 %copy-start.3 = (bf16[224,1792]{1,0:T(8,128)(2,1)S(1)}, bf16[224,1792]{1,0:T(8,128)(2,1)}, u32[]{:S(2)}) copy-start(bf16[224,1792]{1,0:T(8,128)(2,1)} %param.17) | copy-start | bytes 2408452
  156.0 3.4 %copy-start.8 = (bf16[1792]{0:T(1024)(128)(2,1)S(1)}, bf16[1792]{0:T(1024)(128)(2,1)}, u32[]{:S(2)}) copy-start(bf16[1792]{0:T(1024)(128)(2,1)} %param.21) | copy-start | bytes 10756
  158.6 92.0 %all-gather.2.cloned.1.call-start = ((), (), s32[]{:S(2)}) async-start(), calls=%async_computation.3 | async-start | bytes 7096320 | tf_op jit(solution)/shard_map/all_gather | solution.py:203
  159.2 143.8 %reduce-scatter.2.cloned.1.call-start = ((), (), s32[]{:S(2)}) async-start(), calls=%async_computation.4 | async-start | bytes 3096576 | tf_op jit(solution)/shard_map/reduce_scatter | solution.py:212
  256.5 48.4 %copy-start.1 = (bf16[3,224,1792]{2,1,0:T(8,128)(2,1)S(1)}, bf16[3,224,1792]{2,1,0:T(8,128)(2,1)}, u32[]{:S(2)}) copy-start(bf16[3,224,1792]{2,1,0:T(8,128)(2,1)} %param.16) | copy-start | bytes 7225348
Sparse Core Ops, SparseCore 0:
  158.7 72.4 all-reduce.1
  267.2 35.7 reduce-scatter.1
Sparse Core Ops, SparseCore 1:
  162.1 88.5 all-gather.1

commit v11 on v10

--- a/solution.py
+++ b/solution.py
@@ -200,12 +200,13 @@
     mean_sq = jnp.mean(resid_wide * resid_wide, axis=1, keepdims=True)
     normed = (resid_wide * lax.rsqrt(mean_sq + 1e-06) * gain_wide).astype(jnp.bfloat16)
     resid_mine = lax.dynamic_slice_in_dim(resid_full, mdl_index * row_share, row_share, 0)
-    full_mlp = lax.all_gather(feedforward_weight, "req", axis=1, tiled=True)
+    full_mlp = lax.all_gather(feedforward_weight[:2], "req", axis=1, tiled=True)
+    down_rows = lax.all_gather(feedforward_weight[2].T, "req", axis=1, tiled=True)
     gate_part = jnp.dot(normed, full_mlp[0], preferred_element_type=jnp.float32)
     up_part = jnp.dot(normed, full_mlp[1], preferred_element_type=jnp.float32)
     hidden = (jax.nn.silu(gate_part) * up_part).astype(jnp.bfloat16)
     mlp_part = (
-        jnp.einsum("tf,df->td", hidden, full_mlp[2], preferred_element_type=jnp.float32)
+        jnp.dot(hidden, down_rows, preferred_element_type=jnp.float32)
         .astype(jnp.bfloat16)
         .astype(jnp.float32)
     )

time: 313 us -> 378 us (1.21)
  waiting for transfers between devices: 172 us -> 236 us
    all_gather x1 -> x2, waiting for transfers between devices: 14.1 us -> 79 us  [the longest x1 72.7 us: per_device(): lax.all_gather(feedforward_weight[2].T, 'req', axis=1, tiled=True)]
  transfers between devices with their start and end apart: 4 -> 5, of which waited for: 4 -> 5; matrix products, arithmetic and copies ran while one was open for 7% -> 7% of each run, Pallas kernels for 0% -> 0%
where the time goes in v11:
time: 378 us; the launch traced here: 377 us
  waiting for transfers between devices  236 us (62%)
  matrix products  43.7 us (12%)
  blocking collectives  26.8 us (7%)
  Pallas kernels  16.5 us (4%)
  between operations  15.2 us (4%)
  other arithmetic  13.7 us (4%)
  local copies, waits for them, and re-layouts  13.6 us (4%)
  starting transfers between devices  12.3 us (3%)
    all_gather x1, waiting for transfers between devices, per_device(): lax.all_gather(feedforward_weight[2].T, 'req', axis=1, tiled=True)  72.7 us
    psum x1, waiting for transfers between devices, per_device(): lax.psum(attn_part.astype(jnp.bfloat16), 'mdl').astype(jnp.float32)  70.8 us
    all_to_all x1, waiting for transfers between devices, per_device(): lax.all_to_all(source_pages, 'req', split_axis=0, concat_axis=0, tiled=True)  49.7 us
    reduce_scatter x1, waiting for transfers between devices, per_device(): lax.psum_scatter(mlp_part.astype(jnp.bfloat16), 'mdl', scatter_dimension=...  36.1 us
    psum x1, blocking collectives, per_device(): rank_feat = lax.psum(rank_part.astype(jnp.bfloat16), 'mdl')  26.8 us
    pallas_call x1, Pallas kernels, cut_windows(): pl.pallas_call(window_kernel, grid_spec=pltpu.PrefetchScalarGridSpec(num_...  16.5 us
    all_to_all x1, starting transfers between devices, per_device(): lax.all_to_all(source_pages, 'req', split_axis=0, concat_axis=0, tiled=True)  11.9 us
    dot_general x1, matrix products, per_device(): jnp.dot(hidden, down_rows, preferred_element_type=jnp.float32)  10.6 us
  transfers between devices with their start and end apart: 5, of which 5 were waited for; matrix products, arithmetic and copies ran while one was open for 7% of the time, Pallas kernels for 0%

profile of v11, /device:TPU:8, one launch (start us, length us, event | category | flops | bytes accessed | tf_op | source)
XLA Modules:
  0.0 377.5 jit_solution(12149505573380383977)
XLA Ops:
  7.4 0.8 fusion.36
  8.4 0.2 reduce_window_sum.18
  8.6 0.8 mul.159
  9.5 0.8 mul.162
  10.4 0.1 copy.26
  10.5 0.6 min.12.slot_ref
  11.2 0.6 reshape.162.fill_ref
  11.8 16.5 %shard_map.145 = bf16[64,2,64,224]{3,2,1,0:T(8,128)(2,1)} custom-call(s32[64]{0:T(128)} %min.12.slot_ref, s32[64]{0:T(128)} %reshape.162.fill_ref, bf16[32,2,224,128]{3,2,1,0:T(8,128)(2,1)} %store_ref.1), custom_call_target="tpu_custom_call" | custom-call | tf_op jit(solution)/shard_map/pallas_call | solution.py:44
  28.3 11.9 %all-to-all-start = ((bf16[32,2,2,64,224]{4,3,2,1,0:T(8,128)(2,1)}), bf16[32,2,2,64,224]{4,3,2,1,0:T(8,128)(2,1)}, u32[]{:S(2)}, u32[]{:S(2)}) async-start(bf16[32,2,2,64,224]{4,3,2,1,0:T(8,128)(2,1)} %bitcast.67), calls=%async_computation | async-start | bytes 8388608 | tf_op jit(solution)/shard_map/all_to_all | solution.py:155
  40.3 0.1 reduce
  40.6 3.9 %fusion.17 = f32[3,768,224]{1,2,0:T(8,128)S(1)} fusion(bf16[3,224,1792]{2,1,0:T(8,128)(2,1)S(1)} %copy-done, bf16[768,1792]{1,0:T(8,128)(2,1)} %param.15), kind=kOutput, calls=%fused_computation.32 | convolution fusion | flops 1849688064 | bytes 7225344 | tf_op jit(solution)/shard_map/td,kcd->ktc/dot_general | solution.py:88
  44.5 1.4 copy-done.2
  46.1 2.8 fusion.52
  48.9 26.8 %psum.14 = bf16[768,16]{0,1:T(8,128)(2,1)S(1)} all-reduce(bf16[768,16]{0,1:T(8,128)(2,1)S(1)} %multiply_reduce_fusion), channel_id=1, replica_groups=mesh['req'=32,'mdl'=8] {'mdl'}, use_global_device_ids=true, to_apply=%region_4.5 | all-reduce | flops 12288 | bytes 49152 | tf_op jit(solution)/shard_map/psum | solution.py:103
  75.7 0.8 fusion.39
  76.5 0.2 convert_reduce_fusion
  76.7 0.8 fusion.38
  77.5 0.1 select_reduce_fusion.2
  77.6 0.1 select_reduce_fusion.1
  77.8 0.1 broadcast_multiply_fusion
  77.9 1.4 fusion.48
  79.3 0.9 fusion.53
  80.2 0.1 fusion.50
  80.3 0.3 fusion.14
  80.6 1.1 add_convert_fusion.3
  81.7 1.2 compare_and_fusion
  83.0 1.3 pad_add_fusion
  84.3 49.7 %all-to-all-done = bf16[32,2,2,64,224]{4,3,2,1,0:T(8,128)(2,1)} async-done(((bf16[32,2,2,64,224]{4,3,2,1,0:T(8,128)(2,1)}), bf16[32,2,2,64,224]{4,3,2,1,0:T(8,128)(2,1)}, u32[]{:S(2)}, u32[]{:S(2)}) %all-to-all-start) | async-done | bytes 3670048 | tf_op jit(solution)/shard_map/all_to_all | solution.py:155
  134.0 2.8 gather_fusion
  136.8 0.2 fusion.49
  137.0 0.4 concatenate.18
  137.4 0.6 copy.30
  138.0 0.4 concatenate.15
  138.4 0.6 copy.29
  139.0 9.6 %fusion.51 = (f32[2,768]{1,0:T(2,128)S(1)}, f32[2,768,2304]{2,1,0:T(8,128)}) fusion(pred[768,2304]{1,0:T(8,128)(4,1)} %pad_add_fusion, bf16[768,2,112]{0,2,1:T(8,128)(2,1)S(1)} %copy-done.6, bf16[1536,2,112]{0,2,1:T(8,128)(2,1)S(1)} %copy.30, bf16[768,2,112]{0,2,1:T(8,128)(2,1)S(1)} %bitcast.75), kind=kOutput, calls=%fused_computation.90 | convolution fusion | flops 808945920 | bytes 17307648 | tf_op jit(solution)/shard_map/sub | solution.py:184
  148.6 7.6 %fusion.22 = bf16[2,112,768]{2,1,0:T(8,128)(2,1)S(1)} fusion(f32[2,768,2304]{2,1,0:T(8,128)} %get-tuple-element.20, f32[2,768]{1,0:T(2,128)S(1)} %get-tuple-element.19, bf16[1536,2,112]{0,2,1:T(8,128)(2,1)S(1)} %copy.29, bf16[768,2,112]{0,2,1:T(8,128)(2,1)S(1)} %copy-done.5), kind=kOutput, calls=%fused_computation.34 | convolution fusion | flops 802037760 | bytes 15538176 | tf_op jit(solution)/shard_map/hts,shd->thd/dot_general | solution.py:187
  156.2 2.5 convolution_convert_fusion
  158.8 0.7 slice.41
  159.5 0.6 slice_bitcast_fusion.8
  160.2 0.3 reduce-scatter.2.cloned.1.call-start
  160.5 70.8 %all-reduce.2.cloned.1.call-done = bf16[768,1792]{1,0:T(8,128)(2,1)} async-done(((bf16[768,1792]{1,0:T(8,128)(2,1)}), bf16[768,1792]{1,0:T(8,128)(2,1)}) %all-reduce.2.cloned.1.call-update) | async-done | bytes 2752528 | tf_op jit(solution)/shard_map/psum | solution.py:197
  231.3 5.2 %fusion.6 = (f32[768]{0:T(1024)S(1)}, bf16[768,1792]{1,0:T(8,128)(2,1)}) fusion(bf16[768,1792]{1,0:T(8,128)(2,1)} %all-reduce.2.cloned.1.call-done, bf16[768,1792]{1,0:T(8,128)(2,1)} %param.15), kind=kLoop, calls=%fused_computation.13 | loop fusion | flops 9633024 | bytes 8260608 | tf_op jit(solution)/shard_map/reduce_sum | solution.py:200
  236.5 6.3 %all-gather.3.cloned.1.call-done = bf16[2,1792,608]{2,1,0:T(8,128)(2,1)} async-done(((bf16[2,56,608]{2,1,0:T(8,128)(2,1)}), bf16[2,1792,608]{2,1,0:T(8,128)(2,1)}) %all-gather.3.cloned.1.call-update) | async-done | bytes 4358160 | tf_op jit(solution)/shard_map/all_gather | solution.py:203
  242.8 5.8 %fusion.16 = f32[768,608]{0,1:T(8,128)} fusion(bf16[2,1792,608]{2,1,0:T(8,128)(2,1)} %all-gather.3.cloned.1.call-done, bf16[768,1792]{1,0:T(8,128)(2,1)} %get-tuple-element.10, f32[1792]{0:T(1024)S(1)} %convert_element_type.118, f32[768]{0:T(1024)S(1)} %add_rsqrt_fusion), kind=kOutput, calls=%fused_computation.30 | convolution fusion | flops 1679032320 | bytes 6924288 | tf_op jit(solution)/shard_map/dot_general | solution.py:205
  248.6 72.7 %all-gather.5.cloned.1.call-done = bf16[608,1792]{0,1:T(8,128)(2,1)} async-done(((bf16[608,56]{0,1:T(8,128)(2,1)}), bf16[608,1792]{0,1:T(8,128)(2,1)}) %all-gather.5.cloned.1.call-update) | async-done | bytes 2179088 | tf_op jit(solution)/shard_map/all_gather | solution.py:204
  321.4 10.6 %convolution_convert_fusion.1 = bf16[768,1792]{1,0:T(8,128)(2,1)} fusion(bf16[608,1792]{0,1:T(8,128)(2,1)} %all-gather.5.cloned.1.call-done, f32[768,608]{0,1:T(8,128)} %fusion.16, bf16[2,1792,608]{2,1,0:T(8,128)(2,1)} %all-gather.3.cloned.1.call-done, bf16[768,1792]{1,0:T(8,128)(2,1)} %get-tuple-element.10, f32[1792]{0:T(1024)S(1)} %convert_element_type.118, ...), kind=kOutput, calls=%fused_computation.19 | convolution fusion | flops 3356737536 | bytes 11970560 | tf_op jit(solution)/shard_map/dot_general | solution.py:209
  332.0 36.1 %reduce-scatter.2.cloned.1.call-done = bf16[96,1792]{1,0:T(8,128)(2,1)} async-done(((bf16[768,1792]{1,0:T(8,128)(2,1)}), bf16[96,1792]{1,0:T(8,128)(2,1)}) %reduce-scatter.2.cloned.1.call-update) | async-done | bytes 344080 | tf_op jit(solution)/shard_map/reduce_scatter | solution.py:213
  368.2 1.9 add_convert_fusion.1
  (60 shorter events, 1.3 us)
Async XLA Ops:
  7.4 33.3 %copy-start = (bf16[3,224,1792]{2,1,0:T(8,128)(2,1)S(1)}, bf16[3,224,1792]{2,1,0:T(8,128)(2,1)}, u32[]{:S(2)}) copy-start(bf16[3,224,1792]{2,1,0:T(8,128)(2,1)} %param.16) | copy-start | bytes 7225348
  28.3 11.9 %copy-start.10 = (s32[1,24]{1,0:T(1,128)S(1)}, s32[1,24]{1,0:T(1,128)}, u32[]{:S(2)}) copy-start(s32[1,24]{1,0:T(1,128)} %param.25) | copy-start | bytes 292
  28.3 105.7 %all-to-all-start = ((bf16[32,2,2,64,224]{4,3,2,1,0:T(8,128)(2,1)}), bf16[32,2,2,64,224]{4,3,2,1,0:T(8,128)(2,1)}, u32[]{:S(2)}, u32[]{:S(2)}) async-start(bf16[32,2,2,64,224]{4,3,2,1,0:T(8,128)(2,1)} %bitcast.67), calls=%async_computation | async-start | bytes 8388608 | tf_op jit(solution)/shard_map/all_to_all | solution.py:155
  40.2 191.1 %all-reduce.2.cloned.1.call-start = ((), (), s32[]{:S(2)}) async-start(), calls=%async_computation.2 | async-start | bytes 5505024 | tf_op jit(solution)/shard_map/psum | solution.py:197
  40.6 5.4 %copy-start.8 = (s32[768]{0:T(1024)S(1)}, s32[768]{0:T(1024)}, u32[]{:S(2)}) copy-start(s32[768]{0:T(1024)} %param.24) | copy-start | bytes 9220
  40.6 5.4 %copy-start.4 = (bf16[8,1792,16]{1,2,0:T(8,128)(2,1)S(1)}, bf16[8,1792,16]{1,2,0:T(8,128)(2,1)}, u32[]{:S(2)}) copy-start(bf16[8,1792,16]{1,2,0:T(8,128)(2,1)} %param.18) | copy-start | bytes 1376260
  44.5 1.4 copy-start.2
  45.9 31.5 %copy-start.12 = (f32[4]{0:T(128)S(1)}, f32[4]{0:T(128)}, u32[]{:S(2)}) copy-start(f32[4]{0:T(128)} %param.20) | copy-start | bytes 52
  46.0 31.5 %copy-start.13 = (s32[24]{0:T(128)S(1)}, s32[24]{0:T(128)}, u32[]{:S(2)}) copy-start(s32[24]{0:T(128)} %param.26) | copy-start | bytes 292
  48.9 30.4 %copy-start.11 = (bf16[2,224,1024]{2,1,0:T(8,128)(2,1)S(1)}, bf16[2,224,1024]{2,1,0:T(8,128)(2,1)}, u32[]{:S(2)}) copy-start(bf16[2,224,1024]{2,1,0:T(8,128)(2,1)} %param.19) | copy-start | bytes 2752516
  137.4 1.6 copy-start.6
  139.0 9.6 %copy-start.5 = (bf16[768,2,112]{0,2,1:T(8,128)(2,1)S(1)}, bf16[768,2,112]{0,2,1:T(8,128)(2,1)}, u32[]{:S(2)}) copy-start(bf16[768,2,112]{0,2,1:T(8,128)(2,1)} %get-tuple-element.17) | copy-start | bytes 1032196
  148.6 7.6 %copy-start.3 = (bf16[224,1792]{1,0:T(8,128)(2,1)S(1)}, bf16[224,1792]{1,0:T(8,128)(2,1)}, u32[]{:S(2)}) copy-start(bf16[224,1792]{1,0:T(8,128)(2,1)} %param.17) | copy-start | bytes 2408452
  156.2 2.6 copy-start.7
  156.2 4.3 %copy-start.9 = (bf16[1792]{0:T(1024)(128)(2,1)S(1)}, bf16[1792]{0:T(1024)(128)(2,1)}, u32[]{:S(2)}) copy-start(bf16[1792]{0:T(1024)(128)(2,1)} %param.21) | copy-start | bytes 10756
  158.7 84.1 %all-gather.3.cloned.1.call-start = ((), (), s32[]{:S(2)}) async-start(), calls=%async_computation.3 | async-start | bytes 4730880 | tf_op jit(solution)/shard_map/all_gather | solution.py:203
  159.5 161.9 %all-gather.5.cloned.1.call-start = ((), (), s32[]{:S(2)}) async-start(), calls=%async_computation.4 | async-start | bytes 2365440 | tf_op jit(solution)/shard_map/all_gather | solution.py:204
  160.2 208.0 %reduce-scatter.2.cloned.1.call-start = ((), (), s32[]{:S(2)}) async-start(), calls=%async_computation.5 | async-start | bytes 3096576 | tf_op jit(solution)/shard_map/reduce_scatter | solution.py:213
  321.4 48.7 %copy-start.1 = (bf16[3,224,1792]{2,1,0:T(8,128)(2,1)S(1)}, bf16[3,224,1792]{2,1,0:T(8,128)(2,1)}, u32[]{:S(2)}) copy-start(bf16[3,224,1792]{2,1,0:T(8,128)(2,1)} %param.16) | copy-start | bytes 7225348
Sparse Core Ops, SparseCore 0:
  158.8 72.4 all-reduce.1
  332.1 35.9 reduce-scatter.1
Sparse Core Ops, SparseCore 1:
  162.2 80.5 all-gather.2
  245.6 75.7 all-gather.4

commit v12 on v10

--- a/solution.py
+++ b/solution.py
@@ -11,27 +11,20 @@
 WINDOW = 64
 
 
-def window_kernel(slot_ref, fill_ref, store_ref, out_ref, held, sems):
+def window_kernel(slot_ref, fill_ref, store_ref, out_ref):
     count = out_ref.shape[0]
-
-    def fetch(i):
-        return pltpu.make_async_copy(store_ref.at[slot_ref[i]], held.at[i], sems.at[i])
-
-    def start(i, carry):
-        fetch(i).start()
-        return carry
-
-    lax.fori_loop(0, count, start, 0, unroll=8)
-    page_rows = held.shape[-1]
+    page_rows = store_ref.shape[-1]
     row_ids = lax.broadcasted_iota(jnp.int32, (WINDOW, page_rows), 1)
     out_ids = lax.broadcasted_iota(jnp.int32, (WINDOW, page_rows), 0)
 
     def pick_rows(i, carry):
-        fetch(i).wait()
-        pick = (row_ids == out_ids + (fill_ref[i] - WINDOW)).astype(held.dtype)
-        for part in range(held.shape[1]):
+        pick = (row_ids == out_ids + (fill_ref[i] - WINDOW)).astype(store_ref.dtype)
+        for part in range(store_ref.shape[1]):
             out_ref[i, part] = lax.dot_general(
-                pick, held[i, part], (((1,), (1,)), ((), ())), preferred_element_type=jnp.float32
+                pick,
+                store_ref[slot_ref[i], part],
+                (((1,), (1,)), ((), ())),
+                preferred_element_type=jnp.float32,
             ).astype(out_ref.dtype)
         return carry
 
@@ -46,12 +39,8 @@
         grid_spec=pltpu.PrefetchScalarGridSpec(
             num_scalar_prefetch=2,
             grid=(1,),
-            in_specs=[pl.BlockSpec(memory_space=pl.ANY)],
+            in_specs=[pl.BlockSpec(memory_space=pltpu.VMEM)],
             out_specs=pl.BlockSpec(memory_space=pltpu.VMEM),
-            scratch_shapes=[
-                pltpu.VMEM((count, parts, width, page_rows), store.dtype),
-                pltpu.SemaphoreType.DMA((count,)),
-            ],
         ),
         out_shape=jax.ShapeDtypeStruct((count, parts, WINDOW, width), store.dtype),
     )(slots, fills, store)

time: 313 us -> 307 us (0.981)
  Pallas kernels: 16.5 us -> 10.1 us
    pallas_call x1, Pallas kernels: 16.5 us -> 10.1 us  [cut_windows(): pl.pallas_call(window_kernel, grid_spec=pltpu.PrefetchScalarGridSpec(num_...]
where the time goes in v12:
time: 307 us; the launch traced here: 306 us
  waiting for transfers between devices  172 us (56%)
  matrix products  43.6 us (14%)
  blocking collectives  26.8 us (9%)
  between operations  15.2 us (5%)
  other arithmetic  13.9 us (5%)
  local copies, waits for them, and re-layouts  12.3 us (4%)
  starting transfers between devices  12.2 us (4%)
  Pallas kernels  10.1 us (3%)
    psum x1, waiting for transfers between devices, per_device(): lax.psum(attn_part.astype(jnp.bfloat16), 'mdl').astype(jnp.float32)  71.7 us
    all_to_all x1, waiting for transfers between devices, per_device(): lax.all_to_all(source_pages, 'req', split_axis=0, concat_axis=0, tiled=True)  49.7 us
    reduce_scatter x1, waiting for transfers between devices, per_device(): lax.psum_scatter(mlp_part.astype(jnp.bfloat16), 'mdl', scatter_dimension=...  36 us
    psum x1, blocking collectives, per_device(): rank_feat = lax.psum(rank_part.astype(jnp.bfloat16), 'mdl')  26.8 us
    all_gather x1, waiting for transfers between devices, per_device(): full_mlp = lax.all_gather(feedforward_weight, 'req', axis=1, tiled=True)  14.1 us
    all_to_all x1, starting transfers between devices, per_device(): lax.all_to_all(source_pages, 'req', split_axis=0, concat_axis=0, tiled=True)  11.9 us
    dot_general x1, matrix products, per_device(): jnp.einsum('tf,df->td', hidden, full_mlp[2], preferred_element_type=jnp.f...  10.5 us
    pallas_call x1, Pallas kernels, cut_windows(): pl.pallas_call(window_kernel, grid_spec=pltpu.PrefetchScalarGridSpec(num_...  10.1 us
  transfers between devices with their start and end apart: 4, of which 4 were waited for; matrix products, arithmetic and copies ran while one was open for 7% of the time, Pallas kernels for 0%

profile of v12, /device:TPU:8, one launch (start us, length us, event | category | flops | bytes accessed | tf_op | source)
XLA Modules:
  0.0 306.1 jit_solution(16887415075482708849)
XLA Ops:
  7.4 0.8 fusion.36
  8.4 0.2 reduce_window_sum.18
  8.6 0.8 mul.159
  9.5 0.8 mul.162
  10.4 0.1 copy.26
  10.5 0.6 min.12.slot_ref
  11.1 0.1 copy.28
  11.2 0.6 reshape.162.fill_ref
  11.8 10.1 %shard_map.145 = bf16[64,2,64,224]{3,2,1,0:T(8,128)(2,1)} custom-call(s32[64]{0:T(128)} %min.12.slot_ref, s32[64]{0:T(128)} %reshape.162.fill_ref, bf16[32,2,224,128]{3,2,1,0:T(8,128)(2,1)} %store_ref.1), custom_call_target="tpu_custom_call" | custom-call | tf_op jit(solution)/shard_map/pallas_call | solution.py:37
  21.9 11.9 %all-to-all-start = ((bf16[32,2,2,64,224]{4,3,2,1,0:T(8,128)(2,1)}), bf16[32,2,2,64,224]{4,3,2,1,0:T(8,128)(2,1)}, u32[]{:S(2)}, u32[]{:S(2)}) async-start(bf16[32,2,2,64,224]{4,3,2,1,0:T(8,128)(2,1)} %bitcast.65), calls=%async_computation | async-start | bytes 8388608 | tf_op jit(solution)/shard_map/all_to_all | solution.py:144
  33.9 0.1 copy.21
  34.0 0.1 reduce
  34.3 3.9 %fusion.17 = f32[3,768,224]{1,2,0:T(8,128)S(1)} fusion(bf16[3,224,1792]{2,1,0:T(8,128)(2,1)S(1)} %copy-done, bf16[768,1792]{1,0:T(8,128)(2,1)} %param.15), kind=kOutput, calls=%fused_computation.33 | convolution fusion | flops 1849688064 | bytes 7225344 | tf_op jit(solution)/shard_map/td,kcd->ktc/dot_general | solution.py:77
  38.2 1.4 copy-done.2
  39.8 2.8 fusion.52
  42.6 26.8 %psum.14 = bf16[768,16]{0,1:T(8,128)(2,1)S(1)} all-reduce(bf16[768,16]{0,1:T(8,128)(2,1)S(1)} %multiply_reduce_fusion), channel_id=1, replica_groups=mesh['req'=32,'mdl'=8] {'mdl'}, use_global_device_ids=true, to_apply=%region_4.5 | all-reduce | flops 12288 | bytes 49152 | tf_op jit(solution)/shard_map/psum | solution.py:92
  69.4 0.8 fusion.39
  70.2 0.2 convert_reduce_fusion
  70.4 0.8 fusion.38
  71.2 0.1 select_reduce_fusion.2
  71.3 0.1 select_reduce_fusion.1
  71.5 0.1 broadcast_multiply_fusion
  71.6 1.4 fusion.48
  73.0 0.9 fusion.53
  73.9 0.1 fusion.50
  74.0 0.3 fusion.14
  74.3 1.1 add_convert_fusion.3
  75.4 1.2 compare_and_fusion
  76.6 1.3 pad_add_fusion
  78.0 49.7 %all-to-all-done = bf16[32,2,2,64,224]{4,3,2,1,0:T(8,128)(2,1)} async-done(((bf16[32,2,2,64,224]{4,3,2,1,0:T(8,128)(2,1)}), bf16[32,2,2,64,224]{4,3,2,1,0:T(8,128)(2,1)}, u32[]{:S(2)}, u32[]{:S(2)}) %all-to-all-start) | async-done | bytes 3670048 | tf_op jit(solution)/shard_map/all_to_all | solution.py:144
  127.6 2.8 gather_fusion
  130.5 0.2 fusion.49
  130.6 0.4 concatenate.18
  131.1 0.6 copy.30
  131.7 0.4 concatenate.15
  132.1 0.6 copy.29
  132.7 9.6 %fusion.51 = (f32[2,768]{1,0:T(2,128)S(1)}, f32[2,768,2304]{2,1,0:T(8,128)}) fusion(pred[768,2304]{1,0:T(8,128)(4,1)} %pad_add_fusion, bf16[768,2,112]{0,2,1:T(8,128)(2,1)S(1)} %copy-done.6, bf16[1536,2,112]{0,2,1:T(8,128)(2,1)S(1)} %copy.30, bf16[768,2,112]{0,2,1:T(8,128)(2,1)S(1)} %bitcast.73), kind=kOutput, calls=%fused_computation.90 | convolution fusion | flops 808945920 | bytes 17307648 | tf_op jit(solution)/shard_map/sub | solution.py:173
  142.3 7.6 %fusion.22 = bf16[2,112,768]{2,1,0:T(8,128)(2,1)S(1)} fusion(f32[2,768,2304]{2,1,0:T(8,128)} %get-tuple-element.20, f32[2,768]{1,0:T(2,128)S(1)} %get-tuple-element.19, bf16[1536,2,112]{0,2,1:T(8,128)(2,1)S(1)} %copy.29, bf16[768,2,112]{0,2,1:T(8,128)(2,1)S(1)} %copy-done.5), kind=kOutput, calls=%fused_computation.35 | convolution fusion | flops 802037760 | bytes 15538176 | tf_op jit(solution)/shard_map/hts,shd->thd/dot_general | solution.py:176
  149.8 2.5 convolution_convert_fusion
  152.4 0.5 all-gather.2.cloned.1.call-update
  153.0 0.3 reduce-scatter.2.cloned.1.call-start
  153.3 71.7 %all-reduce.2.cloned.1.call-done = bf16[768,1792]{1,0:T(8,128)(2,1)} async-done(((bf16[768,1792]{1,0:T(8,128)(2,1)}), bf16[768,1792]{1,0:T(8,128)(2,1)}) %all-reduce.2.cloned.1.call-update) | async-done | bytes 2752528 | tf_op jit(solution)/shard_map/psum | solution.py:186
  225.0 5.3 %fusion.6 = (f32[768]{0:T(1024)S(1)}, bf16[768,1792]{1,0:T(8,128)(2,1)}) fusion(bf16[768,1792]{1,0:T(8,128)(2,1)} %all-reduce.2.cloned.1.call-done, bf16[768,1792]{1,0:T(8,128)(2,1)} %param.15), kind=kLoop, calls=%fused_computation.13 | loop fusion | flops 9633024 | bytes 8260608 | tf_op jit(solution)/shard_map/reduce_sum | solution.py:189
  230.3 14.1 %all-gather.2.cloned.1.call-done = bf16[3,1792,608]{2,1,0:T(8,128)(2,1)} async-done(((bf16[3,56,608]{2,1,0:T(8,128)(2,1)}), bf16[3,1792,608]{2,1,0:T(8,128)(2,1)}) %all-gather.2.cloned.1.call-update) | async-done | bytes 6537232 | tf_op jit(solution)/shard_map/all_gather | solution.py:192
  244.4 5.8 %fusion.16 = f32[768,608]{0,1:T(8,128)} fusion(bf16[3,1792,608]{2,1,0:T(8,128)(2,1)} %all-gather.2.cloned.1.call-done, bf16[768,1792]{1,0:T(8,128)(2,1)} %get-tuple-element.10, f32[1792]{0:T(1024)S(1)} %convert_element_type.118, f32[768]{0:T(1024)S(1)} %add_rsqrt_fusion), kind=kOutput, calls=%fused_computation.31 | convolution fusion | flops 1679032320 | bytes 6924288 | tf_op jit(solution)/shard_map/dot_general | solution.py:193
  250.3 10.5 %convolution_convert_fusion.1 = bf16[768,1792]{1,0:T(8,128)(2,1)} fusion(bf16[3,1792,608]{2,1,0:T(8,128)(2,1)} %all-gather.2.cloned.1.call-done, f32[768,608]{0,1:T(8,128)} %fusion.16, bf16[768,1792]{1,0:T(8,128)(2,1)} %get-tuple-element.10, f32[1792]{0:T(1024)S(1)} %convert_element_type.118, f32[768]{0:T(1024)S(1)} %add_rsqrt_fusion), kind=kOutput, calls=%fused_computation.19 | convolution fusion | flops 3356737536 | bytes 11970560 | tf_op jit(solution)/shard_map/tf,df->td/dot_general | solution.py:197
  260.8 36.0 %reduce-scatter.2.cloned.1.call-done = bf16[96,1792]{1,0:T(8,128)(2,1)} async-done(((bf16[768,1792]{1,0:T(8,128)(2,1)}), bf16[96,1792]{1,0:T(8,128)(2,1)}) %reduce-scatter.2.cloned.1.call-update) | async-done | bytes 344080 | tf_op jit(solution)/shard_map/reduce_scatter | solution.py:201
  296.8 1.9 add_convert_fusion.1
  (53 shorter events, 1.1 us)
Async XLA Ops:
  7.4 26.9 %copy-start = (bf16[3,224,1792]{2,1,0:T(8,128)(2,1)S(1)}, bf16[3,224,1792]{2,1,0:T(8,128)(2,1)}, u32[]{:S(2)}) copy-start(bf16[3,224,1792]{2,1,0:T(8,128)(2,1)} %param.16) | copy-start | bytes 7225348
  21.9 11.9 %copy-start.9 = (s32[1,24]{1,0:T(1,128)S(1)}, s32[1,24]{1,0:T(1,128)}, u32[]{:S(2)}) copy-start(s32[1,24]{1,0:T(1,128)} %param.25) | copy-start | bytes 292
  21.9 105.7 %all-to-all-start = ((bf16[32,2,2,64,224]{4,3,2,1,0:T(8,128)(2,1)}), bf16[32,2,2,64,224]{4,3,2,1,0:T(8,128)(2,1)}, u32[]{:S(2)}, u32[]{:S(2)}) async-start(bf16[32,2,2,64,224]{4,3,2,1,0:T(8,128)(2,1)} %bitcast.65), calls=%async_computation | async-start | bytes 8388608 | tf_op jit(solution)/shard_map/all_to_all | solution.py:144
  33.8 191.1 %all-reduce.2.cloned.1.call-start = ((), (), s32[]{:S(2)}) async-start(), calls=%async_computation.2 | async-start | bytes 5505024 | tf_op jit(solution)/shard_map/psum | solution.py:186
  34.3 5.4 %copy-start.7 = (s32[768]{0:T(1024)S(1)}, s32[768]{0:T(1024)}, u32[]{:S(2)}) copy-start(s32[768]{0:T(1024)} %param.24) | copy-start | bytes 9220
  34.3 5.4 %copy-start.4 = (bf16[8,1792,16]{1,2,0:T(8,128)(2,1)S(1)}, bf16[8,1792,16]{1,2,0:T(8,128)(2,1)}, u32[]{:S(2)}) copy-start(bf16[8,1792,16]{1,2,0:T(8,128)(2,1)} %param.18) | copy-start | bytes 1376260
  38.2 1.4 copy-start.2
  39.6 31.5 %copy-start.11 = (f32[4]{0:T(128)S(1)}, f32[4]{0:T(128)}, u32[]{:S(2)}) copy-start(f32[4]{0:T(128)} %param.20) | copy-start | bytes 52
  39.6 31.5 %copy-start.12 = (s32[24]{0:T(128)S(1)}, s32[24]{0:T(128)}, u32[]{:S(2)}) copy-start(s32[24]{0:T(128)} %param.26) | copy-start | bytes 292
  42.6 30.4 %copy-start.10 = (bf16[2,224,1024]{2,1,0:T(8,128)(2,1)S(1)}, bf16[2,224,1024]{2,1,0:T(8,128)(2,1)}, u32[]{:S(2)}) copy-start(bf16[2,224,1024]{2,1,0:T(8,128)(2,1)} %param.19) | copy-start | bytes 2752516
  131.0 1.6 copy-start.6
  132.7 9.6 %copy-start.5 = (bf16[768,2,112]{0,2,1:T(8,128)(2,1)S(1)}, bf16[768,2,112]{0,2,1:T(8,128)(2,1)}, u32[]{:S(2)}) copy-start(bf16[768,2,112]{0,2,1:T(8,128)(2,1)} %get-tuple-element.17) | copy-start | bytes 1032196
  142.2 7.6 %copy-start.3 = (bf16[224,1792]{1,0:T(8,128)(2,1)S(1)}, bf16[224,1792]{1,0:T(8,128)(2,1)}, u32[]{:S(2)}) copy-start(bf16[224,1792]{1,0:T(8,128)(2,1)} %param.17) | copy-start | bytes 2408452
  149.8 3.4 %copy-start.8 = (bf16[1792]{0:T(1024)(128)(2,1)S(1)}, bf16[1792]{0:T(1024)(128)(2,1)}, u32[]{:S(2)}) copy-start(bf16[1792]{0:T(1024)(128)(2,1)} %param.21) | copy-start | bytes 10756
  152.4 92.0 %all-gather.2.cloned.1.call-start = ((), (), s32[]{:S(2)}) async-start(), calls=%async_computation.3 | async-start | bytes 7096320 | tf_op jit(solution)/shard_map/all_gather | solution.py:192
  153.0 143.8 %reduce-scatter.2.cloned.1.call-start = ((), (), s32[]{:S(2)}) async-start(), calls=%async_computation.4 | async-start | bytes 3096576 | tf_op jit(solution)/shard_map/reduce_scatter | solution.py:201
  250.3 48.4 %copy-start.1 = (bf16[3,224,1792]{2,1,0:T(8,128)(2,1)S(1)}, bf16[3,224,1792]{2,1,0:T(8,128)(2,1)}, u32[]{:S(2)}) copy-start(bf16[3,224,1792]{2,1,0:T(8,128)(2,1)} %param.16) | copy-start | bytes 7225348
Sparse Core Ops, SparseCore 0:
  152.5 72.4 all-reduce.1
  261.0 35.7 reduce-scatter.1
Sparse Core Ops, SparseCore 1:
  155.9 88.5 all-gather.1

commit v13 on v12

--- a/solution.py
+++ b/solution.py
@@ -19,13 +19,10 @@
 
     def pick_rows(i, carry):
         pick = (row_ids == out_ids + (fill_ref[i] - WINDOW)).astype(store_ref.dtype)
-        for part in range(store_ref.shape[1]):
-            out_ref[i, part] = lax.dot_general(
-                pick,
-                store_ref[slot_ref[i], part],
-                (((1,), (1,)), ((), ())),
-                preferred_element_type=jnp.float32,
-            ).astype(out_ref.dtype)
+        page = store_ref[slot_ref[i]].reshape(-1, page_rows)
+        out_ref[i] = lax.dot_general(
+            pick, page, (((1,), (1,)), ((), ())), preferred_element_type=jnp.float32
+        ).astype(out_ref.dtype)
         return carry
 
     lax.fori_loop(0, count, pick_rows, 0, unroll=8)
@@ -42,7 +39,7 @@
             in_specs=[pl.BlockSpec(memory_space=pltpu.VMEM)],
             out_specs=pl.BlockSpec(memory_space=pltpu.VMEM),
         ),
-        out_shape=jax.ShapeDtypeStruct((count, parts, WINDOW, width), store.dtype),
+        out_shape=jax.ShapeDtypeStruct((count, WINDOW, parts * width), store.dtype),
     )(slots, fills, store)
 
 
@@ -140,19 +137,19 @@
         jnp.clip(send_slot.reshape(-1), 0, prefix_cache_store.shape[0] - 1),
         send_fill.reshape(-1),
     )
-    source_pages = source_pages.reshape((req_devices, cap_slots, 2, WINDOW, head_column_set))
+    source_pages = source_pages.reshape((req_devices, cap_slots, WINDOW, 2 * head_column_set))
     arrived = lax.all_to_all(source_pages, "req", split_axis=0, concat_axis=0, tiled=True)
     prefix = jnp.take(
-        arrived.reshape((req_devices * cap_slots, 2, WINDOW, head_column_set)),
+        arrived.reshape((req_devices * cap_slots, WINDOW, 2 * head_column_set)),
         flat_pick,
         axis=0,
         mode="clip",
     )
     key_all = jnp.concatenate(
-        [key_rows, prefix[:, 0].reshape(req_per_dev * WINDOW, head_column_set)], axis=0
+        [key_rows, prefix[:, :, :head_column_set].reshape(req_per_dev * WINDOW, head_column_set)], axis=0
     )
     value_all = jnp.concatenate(
-        [value_row_block, prefix[:, 1].reshape(req_per_dev * WINDOW, head_column_set)], axis=0
+        [value_row_block, prefix[:, :, head_column_set:].reshape(req_per_dev * WINDOW, head_column_set)], axis=0
     )
     distance = positions[:, None] - positions[None, :]
     local_ok = (request_of[:, None] == request_of[None, :]) & (distance >= 0) & (distance <= WINDOW)

time: 307 us -> 305 us (level)
  no operation moved by 1% of the time
where the time goes in v13:
time: 305 us
  waiting for transfers between devices  172 us (56%)
  matrix products  43.6 us (14%)
  blocking collectives  26.8 us (9%)
  between operations  15.2 us (5%)
  other arithmetic  13.9 us (5%)
  local copies, waits for them, and re-layouts  12.5 us (4%)
  starting transfers between devices  12.2 us (4%)
  Pallas kernels  8.82 us (3%)
    psum x1, waiting for transfers between devices, per_device(): lax.psum(attn_part.astype(jnp.bfloat16), 'mdl').astype(jnp.float32)  71.7 us
    all_to_all x1, waiting for transfers between devices, per_device(): lax.all_to_all(source_pages, 'req', split_axis=0, concat_axis=0, tiled=True)  49.7 us
    reduce_scatter x1, waiting for transfers between devices, per_device(): lax.psum_scatter(mlp_part.astype(jnp.bfloat16), 'mdl', scatter_dimension=...  36 us
    psum x1, blocking collectives, per_device(): rank_feat = lax.psum(rank_part.astype(jnp.bfloat16), 'mdl')  26.8 us
    all_gather x1, waiting for transfers between devices, per_device(): full_mlp = lax.all_gather(feedforward_weight, 'req', axis=1, tiled=True)  14.1 us
    all_to_all x1, starting transfers between devices, per_device(): lax.all_to_all(source_pages, 'req', split_axis=0, concat_axis=0, tiled=True)  11.9 us
    dot_general x1, matrix products, per_device(): jnp.einsum('tf,df->td', hidden, full_mlp[2], preferred_element_type=jnp.f...  10.5 us
    sub x1, matrix products, per_device(): exp_scores = jnp.exp(masked - row_max)  9.55 us
  transfers between devices with their start and end apart: 4, of which 4 were waited for; matrix products, arithmetic and copies ran while one was open for 7% of the time, Pallas kernels for 0%

profile of v13, /device:TPU:8, one launch (start us, length us, event | category | flops | bytes accessed | tf_op | source)
XLA Modules:
  0.0 305.0 jit_solution(5790941410232082883)
XLA Ops:
  7.4 0.8 fusion.36
  8.4 0.2 reduce_window_sum.18
  8.6 0.8 mul.159
  9.5 0.8 mul.162
  10.4 0.1 copy.26
  10.5 0.6 min.12.slot_ref
  11.1 0.1 copy.28
  11.2 0.6 reshape.164.fill_ref
  11.8 8.8 %shard_map.145 = bf16[64,64,448]{2,1,0:T(8,128)(2,1)} custom-call(s32[64]{0:T(128)} %min.12.slot_ref, s32[64]{0:T(128)} %reshape.164.fill_ref, bf16[32,2,224,128]{3,2,1,0:T(8,128)(2,1)} %store_ref.1), custom_call_target="tpu_custom_call" | custom-call | tf_op jit(solution)/shard_map/pallas_call | solution.py:34
  20.6 11.9 %all-to-all-start = ((bf16[32,2,64,448]{3,2,1,0:T(8,128)(2,1)}), bf16[32,2,64,448]{3,2,1,0:T(8,128)(2,1)}, u32[]{:S(2)}, u32[]{:S(2)}) async-start(bf16[32,2,64,448]{3,2,1,0:T(8,128)(2,1)} %bitcast.61), calls=%async_computation | async-start | bytes 8388608 | tf_op jit(solution)/shard_map/all_to_all | solution.py:141
  32.6 0.1 copy.21
  32.7 0.1 reduce
  33.0 3.9 %fusion.17 = f32[3,768,224]{1,2,0:T(8,128)S(1)} fusion(bf16[3,224,1792]{2,1,0:T(8,128)(2,1)S(1)} %copy-done, bf16[768,1792]{1,0:T(8,128)(2,1)} %param.15), kind=kOutput, calls=%fused_computation.33 | convolution fusion | flops 1849688064 | bytes 7225344 | tf_op jit(solution)/shard_map/td,kcd->ktc/dot_general | solution.py:74
  36.9 1.4 copy-done.2
  38.4 2.8 fusion.52
  41.3 26.8 %psum.14 = bf16[768,16]{0,1:T(8,128)(2,1)S(1)} all-reduce(bf16[768,16]{0,1:T(8,128)(2,1)S(1)} %multiply_reduce_fusion), channel_id=1, replica_groups=mesh['req'=32,'mdl'=8] {'mdl'}, use_global_device_ids=true, to_apply=%region_4.5 | all-reduce | flops 12288 | bytes 49152 | tf_op jit(solution)/shard_map/psum | solution.py:89
  68.1 0.8 fusion.39
  68.9 0.2 convert_reduce_fusion
  69.0 0.8 fusion.38
  69.9 0.1 select_reduce_fusion.2
  70.0 0.1 select_reduce_fusion.1
  70.1 0.1 broadcast_multiply_fusion
  70.3 1.4 fusion.48
  71.7 0.9 fusion.53
  72.6 0.1 fusion.50
  72.7 0.3 fusion.14
  73.0 1.1 add_convert_fusion.3
  74.1 1.2 compare_and_fusion
  75.3 1.3 pad_add_fusion
  76.7 49.7 %all-to-all-done = bf16[32,2,64,448]{3,2,1,0:T(8,128)(2,1)} async-done(((bf16[32,2,64,448]{3,2,1,0:T(8,128)(2,1)}), bf16[32,2,64,448]{3,2,1,0:T(8,128)(2,1)}, u32[]{:S(2)}, u32[]{:S(2)}) %all-to-all-start) | async-done | bytes 3670048 | tf_op jit(solution)/shard_map/all_to_all | solution.py:141
  126.3 2.8 gather_fusion
  129.2 0.4 fusion.49
  129.6 0.4 concatenate.18
  130.0 0.6 copy.30
  130.6 0.4 concatenate.15
  131.0 0.6 copy.29
  131.6 9.5 %fusion.51 = (f32[2,768]{1,0:T(2,128)S(1)}, f32[2,768,2304]{2,1,0:T(8,128)}) fusion(pred[768,2304]{1,0:T(8,128)(4,1)} %pad_add_fusion, bf16[768,2,112]{0,2,1:T(8,128)(2,1)S(1)} %copy-done.6, bf16[1536,2,112]{0,2,1:T(8,128)(2,1)S(1)} %copy.30, bf16[768,2,112]{0,2,1:T(8,128)(2,1)S(1)} %bitcast.69), kind=kOutput, calls=%fused_computation.90 | convolution fusion | flops 808945920 | bytes 17307648 | tf_op jit(solution)/shard_map/sub | solution.py:170
  141.2 7.6 %fusion.22 = bf16[2,112,768]{2,1,0:T(8,128)(2,1)S(1)} fusion(f32[2,768,2304]{2,1,0:T(8,128)} %get-tuple-element.20, f32[2,768]{1,0:T(2,128)S(1)} %get-tuple-element.19, bf16[1536,2,112]{0,2,1:T(8,128)(2,1)S(1)} %copy.29, bf16[768,2,112]{0,2,1:T(8,128)(2,1)S(1)} %copy-done.5), kind=kOutput, calls=%fused_computation.35 | convolution fusion | flops 802037760 | bytes 15538176 | tf_op jit(solution)/shard_map/hts,shd->thd/dot_general | solution.py:173
  148.8 2.5 convolution_convert_fusion
  151.4 0.5 all-gather.2.cloned.1.call-update
  151.9 0.3 reduce-scatter.2.cloned.1.call-start
  152.2 71.7 %all-reduce.2.cloned.1.call-done = bf16[768,1792]{1,0:T(8,128)(2,1)} async-done(((bf16[768,1792]{1,0:T(8,128)(2,1)}), bf16[768,1792]{1,0:T(8,128)(2,1)}) %all-reduce.2.cloned.1.call-update) | async-done | bytes 2752528 | tf_op jit(solution)/shard_map/psum | solution.py:183
  223.9 5.3 %fusion.6 = (f32[768]{0:T(1024)S(1)}, bf16[768,1792]{1,0:T(8,128)(2,1)}) fusion(bf16[768,1792]{1,0:T(8,128)(2,1)} %all-reduce.2.cloned.1.call-done, bf16[768,1792]{1,0:T(8,128)(2,1)} %param.15), kind=kLoop, calls=%fused_computation.13 | loop fusion | flops 9633024 | bytes 8260608 | tf_op jit(solution)/shard_map/reduce_sum | solution.py:186
  229.3 14.1 %all-gather.2.cloned.1.call-done = bf16[3,1792,608]{2,1,0:T(8,128)(2,1)} async-done(((bf16[3,56,608]{2,1,0:T(8,128)(2,1)}), bf16[3,1792,608]{2,1,0:T(8,128)(2,1)}) %all-gather.2.cloned.1.call-update) | async-done | bytes 6537232 | tf_op jit(solution)/shard_map/all_gather | solution.py:189
  243.3 5.8 %fusion.16 = f32[768,608]{0,1:T(8,128)} fusion(bf16[3,1792,608]{2,1,0:T(8,128)(2,1)} %all-gather.2.cloned.1.call-done, bf16[768,1792]{1,0:T(8,128)(2,1)} %get-tuple-element.10, f32[1792]{0:T(1024)S(1)} %convert_element_type.118, f32[768]{0:T(1024)S(1)} %add_rsqrt_fusion), kind=kOutput, calls=%fused_computation.31 | convolution fusion | flops 1679032320 | bytes 6924288 | tf_op jit(solution)/shard_map/dot_general | solution.py:190
  249.2 10.5 %convolution_convert_fusion.1 = bf16[768,1792]{1,0:T(8,128)(2,1)} fusion(bf16[3,1792,608]{2,1,0:T(8,128)(2,1)} %all-gather.2.cloned.1.call-done, f32[768,608]{0,1:T(8,128)} %fusion.16, bf16[768,1792]{1,0:T(8,128)(2,1)} %get-tuple-element.10, f32[1792]{0:T(1024)S(1)} %convert_element_type.118, f32[768]{0:T(1024)S(1)} %add_rsqrt_fusion), kind=kOutput, calls=%fused_computation.19 | convolution fusion | flops 3356737536 | bytes 11970560 | tf_op jit(solution)/shard_map/tf,df->td/dot_general | solution.py:194
  259.8 36.0 %reduce-scatter.2.cloned.1.call-done = bf16[96,1792]{1,0:T(8,128)(2,1)} async-done(((bf16[768,1792]{1,0:T(8,128)(2,1)}), bf16[96,1792]{1,0:T(8,128)(2,1)}) %reduce-scatter.2.cloned.1.call-update) | async-done | bytes 344080 | tf_op jit(solution)/shard_map/reduce_scatter | solution.py:198
  295.7 1.9 add_convert_fusion.1
  (53 shorter events, 1.1 us)
Async XLA Ops:
  7.4 25.6 %copy-start = (bf16[3,224,1792]{2,1,0:T(8,128)(2,1)S(1)}, bf16[3,224,1792]{2,1,0:T(8,128)(2,1)}, u32[]{:S(2)}) copy-start(bf16[3,224,1792]{2,1,0:T(8,128)(2,1)} %param.16) | copy-start | bytes 7225348
  20.6 11.9 %copy-start.9 = (s32[1,24]{1,0:T(1,128)S(1)}, s32[1,24]{1,0:T(1,128)}, u32[]{:S(2)}) copy-start(s32[1,24]{1,0:T(1,128)} %param.25) | copy-start | bytes 292
  20.6 105.7 %all-to-all-start = ((bf16[32,2,64,448]{3,2,1,0:T(8,128)(2,1)}), bf16[32,2,64,448]{3,2,1,0:T(8,128)(2,1)}, u32[]{:S(2)}, u32[]{:S(2)}) async-start(bf16[32,2,64,448]{3,2,1,0:T(8,128)(2,1)} %bitcast.61), calls=%async_computation | async-start | bytes 8388608 | tf_op jit(solution)/shard_map/all_to_all | solution.py:141
  32.5 191.4 %all-reduce.2.cloned.1.call-start = ((), (), s32[]{:S(2)}) async-start(), calls=%async_computation.2 | async-start | bytes 5505024 | tf_op jit(solution)/shard_map/psum | solution.py:183
  33.0 5.4 %copy-start.7 = (s32[768]{0:T(1024)S(1)}, s32[768]{0:T(1024)}, u32[]{:S(2)}) copy-start(s32[768]{0:T(1024)} %param.24) | copy-start | bytes 9220
  33.0 5.4 %copy-start.4 = (bf16[8,1792,16]{1,2,0:T(8,128)(2,1)S(1)}, bf16[8,1792,16]{1,2,0:T(8,128)(2,1)}, u32[]{:S(2)}) copy-start(bf16[8,1792,16]{1,2,0:T(8,128)(2,1)} %param.18) | copy-start | bytes 1376260
  36.9 1.4 copy-start.2
  38.3 31.5 %copy-start.11 = (f32[4]{0:T(128)S(1)}, f32[4]{0:T(128)}, u32[]{:S(2)}) copy-start(f32[4]{0:T(128)} %param.20) | copy-start | bytes 52
  38.3 31.5 %copy-start.12 = (s32[24]{0:T(128)S(1)}, s32[24]{0:T(128)}, u32[]{:S(2)}) copy-start(s32[24]{0:T(128)} %param.26) | copy-start | bytes 292
  41.2 30.4 %copy-start.10 = (bf16[2,224,1024]{2,1,0:T(8,128)(2,1)S(1)}, bf16[2,224,1024]{2,1,0:T(8,128)(2,1)}, u32[]{:S(2)}) copy-start(bf16[2,224,1024]{2,1,0:T(8,128)(2,1)} %param.19) | copy-start | bytes 2752516
  130.0 1.6 copy-start.6
  131.6 9.6 %copy-start.5 = (bf16[768,2,112]{0,2,1:T(8,128)(2,1)S(1)}, bf16[768,2,112]{0,2,1:T(8,128)(2,1)}, u32[]{:S(2)}) copy-start(bf16[768,2,112]{0,2,1:T(8,128)(2,1)} %get-tuple-element.17) | copy-start | bytes 1032196
  141.2 7.6 %copy-start.3 = (bf16[224,1792]{1,0:T(8,128)(2,1)S(1)}, bf16[224,1792]{1,0:T(8,128)(2,1)}, u32[]{:S(2)}) copy-start(bf16[224,1792]{1,0:T(8,128)(2,1)} %param.17) | copy-start | bytes 2408452
  148.8 3.4 %copy-start.8 = (bf16[1792]{0:T(1024)(128)(2,1)S(1)}, bf16[1792]{0:T(1024)(128)(2,1)}, u32[]{:S(2)}) copy-start(bf16[1792]{0:T(1024)(128)(2,1)} %param.21) | copy-start | bytes 10756
  151.3 92.0 %all-gather.2.cloned.1.call-start = ((), (), s32[]{:S(2)}) async-start(), calls=%async_computation.3 | async-start | bytes 7096320 | tf_op jit(solution)/shard_map/all_gather | solution.py:189
  151.9 143.8 %reduce-scatter.2.cloned.1.call-start = ((), (), s32[]{:S(2)}) async-start(), calls=%async_computation.4 | async-start | bytes 3096576 | tf_op jit(solution)/shard_map/reduce_scatter | solution.py:198
  249.2 48.4 %copy-start.1 = (bf16[3,224,1792]{2,1,0:T(8,128)(2,1)S(1)}, bf16[3,224,1792]{2,1,0:T(8,128)(2,1)}, u32[]{:S(2)}) copy-start(bf16[3,224,1792]{2,1,0:T(8,128)(2,1)} %param.16) | copy-start | bytes 7225348
Sparse Core Ops, SparseCore 0:
  151.4 72.4 all-reduce.1
  259.9 35.7 reduce-scatter.1
Sparse Core Ops, SparseCore 1:
  154.8 88.5 all-gather.1

commit v14 on v13

--- a/solution.py
+++ b/solution.py
@@ -123,9 +123,10 @@
     picked = owned[:, None, :] * (
         owned_rank[:, None, :] == jnp.arange(cap_slots, dtype=jnp.int32)[None, :, None]
     ).astype(jnp.int32)
-    send_slot = jnp.sum(picked * slot_table[:, None, :], axis=2)
     fill_table = page_filled_rows.reshape(req_devices, req_per_dev)
-    send_fill = jnp.sum(picked * fill_table[:, None, :], axis=2)
+    send_both = jnp.sum(
+        picked[None] * jnp.stack([slot_table, fill_table])[:, :, None, :], axis=3
+    ).reshape(2, -1)
     my_owner = lax.dynamic_slice_in_dim(owner_column, req_index * req_per_dev, req_per_dev, 0)
     order_ids = jnp.arange(req_per_dev, dtype=jnp.int32)
     earlier = (my_owner[:, None] == my_owner[None, :]) & (order_ids[:, None] > order_ids[None, :])
@@ -134,8 +135,8 @@
     page_rows = prefix_cache_store.shape[3]
     source_pages = cut_windows(
         prefix_cache_store,
-        jnp.clip(send_slot.reshape(-1), 0, prefix_cache_store.shape[0] - 1),
-        send_fill.reshape(-1),
+        send_both[0],
+        send_both[1],
     )
     source_pages = source_pages.reshape((req_devices, cap_slots, WINDOW, 2 * head_column_set))
     arrived = lax.all_to_all(source_pages, "req", split_axis=0, concat_axis=0, tiled=True)

time: 305 us -> 305 us (level)
  no operation moved by 1% of the time
where the time goes in v14:
time: 305 us
  waiting for transfers between devices  172 us (56%)
  matrix products  43.6 us (14%)
  blocking collectives  26.8 us (9%)
  between operations  15.2 us (5%)
  other arithmetic  13.9 us (5%)
  local copies, waits for them, and re-layouts  12.4 us (4%)
  starting transfers between devices  12.2 us (4%)
  Pallas kernels  8.82 us (3%)
    psum x1, waiting for transfers between devices, per_device(): lax.psum(attn_part.astype(jnp.bfloat16), 'mdl').astype(jnp.float32)  71.7 us
    all_to_all x1, waiting for transfers between devices, per_device(): lax.all_to_all(source_pages, 'req', split_axis=0, concat_axis=0, tiled=True)  49.7 us
    reduce_scatter x1, waiting for transfers between devices, per_device(): lax.psum_scatter(mlp_part.astype(jnp.bfloat16), 'mdl', scatter_dimension=...  36 us
    psum x1, blocking collectives, per_device(): rank_feat = lax.psum(rank_part.astype(jnp.bfloat16), 'mdl')  26.8 us
    all_gather x1, waiting for transfers between devices, per_device(): full_mlp = lax.all_gather(feedforward_weight, 'req', axis=1, tiled=True)  14.1 us
    all_to_all x1, starting transfers between devices, per_device(): lax.all_to_all(source_pages, 'req', split_axis=0, concat_axis=0, tiled=True)  11.9 us
    dot_general x1, matrix products, per_device(): jnp.einsum('tf,df->td', hidden, full_mlp[2], preferred_element_type=jnp.f...  10.5 us
    sub x1, matrix products, per_device(): exp_scores = jnp.exp(masked - row_max)  9.55 us
  transfers between devices with their start and end apart: 4, of which 4 were waited for; matrix products, arithmetic and copies ran while one was open for 7% of the time, Pallas kernels for 0%

profile of v14, /device:TPU:8, one launch (start us, length us, event | category | flops | bytes accessed | tf_op | source)
XLA Modules:
  0.0 305.0 jit_solution(11714447552745411128)
XLA Ops:
  7.4 0.8 fusion.35
  8.4 0.2 reduce_window_sum.18
  8.6 0.8 stack_reshape.6
  9.4 0.8 stack_reshape.7
  10.3 0.1 copy.26
  10.4 0.6 squeeze.32.slot_ref
  11.0 0.1 copy.27
  11.1 0.6 squeeze.33.fill_ref
  11.7 8.8 %shard_map.145 = bf16[64,64,448]{2,1,0:T(8,128)(2,1)} custom-call(s32[64]{0:T(128)} %squeeze.32.slot_ref, s32[64]{0:T(128)} %squeeze.33.fill_ref, bf16[32,2,224,128]{3,2,1,0:T(8,128)(2,1)} %store_ref.1), custom_call_target="tpu_custom_call" | custom-call | tf_op jit(solution)/shard_map/pallas_call | solution.py:34
  20.6 11.9 %all-to-all-start = ((bf16[32,2,64,448]{3,2,1,0:T(8,128)(2,1)}), bf16[32,2,64,448]{3,2,1,0:T(8,128)(2,1)}, u32[]{:S(2)}, u32[]{:S(2)}) async-start(bf16[32,2,64,448]{3,2,1,0:T(8,128)(2,1)} %bitcast.61), calls=%async_computation | async-start | bytes 8388608 | tf_op jit(solution)/shard_map/all_to_all | solution.py:142
  32.5 0.1 copy.21
  32.7 0.1 reduce
  32.9 3.9 %fusion.17 = f32[3,768,224]{1,2,0:T(8,128)S(1)} fusion(bf16[3,224,1792]{2,1,0:T(8,128)(2,1)S(1)} %copy-done, bf16[768,1792]{1,0:T(8,128)(2,1)} %param.15), kind=kOutput, calls=%fused_computation.33 | convolution fusion | flops 1849688064 | bytes 7225344 | tf_op jit(solution)/shard_map/td,kcd->ktc/dot_general | solution.py:74
  36.9 1.4 copy-done.2
  38.4 2.8 fusion.52
  41.3 26.8 %psum.14 = bf16[768,16]{0,1:T(8,128)(2,1)S(1)} all-reduce(bf16[768,16]{0,1:T(8,128)(2,1)S(1)} %multiply_reduce_fusion), channel_id=1, replica_groups=mesh['req'=32,'mdl'=8] {'mdl'}, use_global_device_ids=true, to_apply=%region_4.5 | all-reduce | flops 12288 | bytes 49152 | tf_op jit(solution)/shard_map/psum | solution.py:89
  68.1 0.8 fusion.38
  68.8 0.2 convert_reduce_fusion
  69.0 0.8 fusion.37
  69.9 0.1 select_reduce_fusion.2
  70.0 0.1 select_reduce_fusion.1
  70.1 0.1 broadcast_multiply_fusion
  70.2 1.4 fusion.47
  71.6 0.9 fusion.53
  72.5 0.1 fusion.49
  72.6 0.3 fusion.14
  73.0 1.1 add_convert_fusion.3
  74.0 1.2 compare_and_fusion
  75.3 1.3 pad_add_fusion
  76.6 49.7 %all-to-all-done = bf16[32,2,64,448]{3,2,1,0:T(8,128)(2,1)} async-done(((bf16[32,2,64,448]{3,2,1,0:T(8,128)(2,1)}), bf16[32,2,64,448]{3,2,1,0:T(8,128)(2,1)}, u32[]{:S(2)}, u32[]{:S(2)}) %all-to-all-start) | async-done | bytes 3670048 | tf_op jit(solution)/shard_map/all_to_all | solution.py:142
  126.3 2.8 gather_fusion
  129.1 0.4 fusion.48
  129.5 0.4 concatenate.18
  129.9 0.6 copy.29
  130.5 0.4 concatenate.15
  130.9 0.6 copy.28
  131.6 9.6 %fusion.51 = (f32[2,768]{1,0:T(2,128)S(1)}, f32[2,768,2304]{2,1,0:T(8,128)}) fusion(pred[768,2304]{1,0:T(8,128)(4,1)} %pad_add_fusion, bf16[768,2,112]{0,2,1:T(8,128)(2,1)S(1)} %copy-done.6, bf16[1536,2,112]{0,2,1:T(8,128)(2,1)S(1)} %copy.29, bf16[768,2,112]{0,2,1:T(8,128)(2,1)S(1)} %bitcast.69), kind=kOutput, calls=%fused_computation.89 | convolution fusion | flops 808945920 | bytes 17307648 | tf_op jit(solution)/shard_map/sub | solution.py:171
  141.1 7.6 %fusion.22 = bf16[2,112,768]{2,1,0:T(8,128)(2,1)S(1)} fusion(f32[2,768,2304]{2,1,0:T(8,128)} %get-tuple-element.20, f32[2,768]{1,0:T(2,128)S(1)} %get-tuple-element.19, bf16[1536,2,112]{0,2,1:T(8,128)(2,1)S(1)} %copy.28, bf16[768,2,112]{0,2,1:T(8,128)(2,1)S(1)} %copy-done.5), kind=kOutput, calls=%fused_computation.35 | convolution fusion | flops 802037760 | bytes 15538176 | tf_op jit(solution)/shard_map/hts,shd->thd/dot_general | solution.py:174
  148.7 2.5 convolution_convert_fusion
  151.3 0.5 all-gather.2.cloned.1.call-update
  151.8 0.3 reduce-scatter.2.cloned.1.call-start
  152.1 71.7 %all-reduce.2.cloned.1.call-done = bf16[768,1792]{1,0:T(8,128)(2,1)} async-done(((bf16[768,1792]{1,0:T(8,128)(2,1)}), bf16[768,1792]{1,0:T(8,128)(2,1)}) %all-reduce.2.cloned.1.call-update) | async-done | bytes 2752528 | tf_op jit(solution)/shard_map/psum | solution.py:184
  223.8 5.3 %fusion.6 = (f32[768]{0:T(1024)S(1)}, bf16[768,1792]{1,0:T(8,128)(2,1)}) fusion(bf16[768,1792]{1,0:T(8,128)(2,1)} %all-reduce.2.cloned.1.call-done, bf16[768,1792]{1,0:T(8,128)(2,1)} %param.15), kind=kLoop, calls=%fused_computation.13 | loop fusion | flops 9633024 | bytes 8260608 | tf_op jit(solution)/shard_map/reduce_sum | solution.py:187
  229.2 14.1 %all-gather.2.cloned.1.call-done = bf16[3,1792,608]{2,1,0:T(8,128)(2,1)} async-done(((bf16[3,56,608]{2,1,0:T(8,128)(2,1)}), bf16[3,1792,608]{2,1,0:T(8,128)(2,1)}) %all-gather.2.cloned.1.call-update) | async-done | bytes 6537232 | tf_op jit(solution)/shard_map/all_gather | solution.py:190
  243.3 5.8 %fusion.16 = f32[768,608]{0,1:T(8,128)} fusion(bf16[3,1792,608]{2,1,0:T(8,128)(2,1)} %all-gather.2.cloned.1.call-done, bf16[768,1792]{1,0:T(8,128)(2,1)} %get-tuple-element.8, f32[1792]{0:T(1024)S(1)} %convert_element_type.118, f32[768]{0:T(1024)S(1)} %add_rsqrt_fusion), kind=kOutput, calls=%fused_computation.31 | convolution fusion | flops 1679032320 | bytes 6924288 | tf_op jit(solution)/shard_map/dot_general | solution.py:191
  249.1 10.5 %convolution_convert_fusion.1 = bf16[768,1792]{1,0:T(8,128)(2,1)} fusion(bf16[3,1792,608]{2,1,0:T(8,128)(2,1)} %all-gather.2.cloned.1.call-done, f32[768,608]{0,1:T(8,128)} %fusion.16, bf16[768,1792]{1,0:T(8,128)(2,1)} %get-tuple-element.8, f32[1792]{0:T(1024)S(1)} %convert_element_type.118, f32[768]{0:T(1024)S(1)} %add_rsqrt_fusion), kind=kOutput, calls=%fused_computation.19 | convolution fusion | flops 3356737536 | bytes 11970560 | tf_op jit(solution)/shard_map/tf,df->td/dot_general | solution.py:195
  259.7 36.0 %reduce-scatter.2.cloned.1.call-done = bf16[96,1792]{1,0:T(8,128)(2,1)} async-done(((bf16[768,1792]{1,0:T(8,128)(2,1)}), bf16[96,1792]{1,0:T(8,128)(2,1)}) %reduce-scatter.2.cloned.1.call-update) | async-done | bytes 344080 | tf_op jit(solution)/shard_map/reduce_scatter | solution.py:199
  295.6 1.9 add_convert_fusion.1
  (54 shorter events, 1.0 us)
Async XLA Ops:
  7.4 25.6 %copy-start = (bf16[3,224,1792]{2,1,0:T(8,128)(2,1)S(1)}, bf16[3,224,1792]{2,1,0:T(8,128)(2,1)}, u32[]{:S(2)}) copy-start(bf16[3,224,1792]{2,1,0:T(8,128)(2,1)} %param.16) | copy-start | bytes 7225348
  20.6 11.9 %copy-start.9 = (s32[1,24]{1,0:T(1,128)S(1)}, s32[1,24]{1,0:T(1,128)}, u32[]{:S(2)}) copy-start(s32[1,24]{1,0:T(1,128)} %param.25) | copy-start | bytes 292
  20.6 105.7 %all-to-all-start = ((bf16[32,2,64,448]{3,2,1,0:T(8,128)(2,1)}), bf16[32,2,64,448]{3,2,1,0:T(8,128)(2,1)}, u32[]{:S(2)}, u32[]{:S(2)}) async-start(bf16[32,2,64,448]{3,2,1,0:T(8,128)(2,1)} %bitcast.61), calls=%async_computation | async-start | bytes 8388608 | tf_op jit(solution)/shard_map/all_to_all | solution.py:142
  32.5 191.4 %all-reduce.2.cloned.1.call-start = ((), (), s32[]{:S(2)}) async-start(), calls=%async_computation.2 | async-start | bytes 5505024 | tf_op jit(solution)/shard_map/psum | solution.py:184
  32.9 5.4 %copy-start.7 = (s32[768]{0:T(1024)S(1)}, s32[768]{0:T(1024)}, u32[]{:S(2)}) copy-start(s32[768]{0:T(1024)} %param.24) | copy-start | bytes 9220
  32.9 5.4 %copy-start.4 = (bf16[8,1792,16]{1,2,0:T(8,128)(2,1)S(1)}, bf16[8,1792,16]{1,2,0:T(8,128)(2,1)}, u32[]{:S(2)}) copy-start(bf16[8,1792,16]{1,2,0:T(8,128)(2,1)} %param.18) | copy-start | bytes 1376260
  36.8 1.4 copy-start.2
  38.3 31.5 %copy-start.11 = (f32[4]{0:T(128)S(1)}, f32[4]{0:T(128)}, u32[]{:S(2)}) copy-start(f32[4]{0:T(128)} %param.20) | copy-start | bytes 52
  38.3 31.5 %copy-start.12 = (s32[24]{0:T(128)S(1)}, s32[24]{0:T(128)}, u32[]{:S(2)}) copy-start(s32[24]{0:T(128)} %param.26) | copy-start | bytes 292
  41.2 30.4 %copy-start.10 = (bf16[2,224,1024]{2,1,0:T(8,128)(2,1)S(1)}, bf16[2,224,1024]{2,1,0:T(8,128)(2,1)}, u32[]{:S(2)}) copy-start(bf16[2,224,1024]{2,1,0:T(8,128)(2,1)} %param.19) | copy-start | bytes 2752516
  129.9 1.6 copy-start.6
  131.5 9.6 %copy-start.5 = (bf16[768,2,112]{0,2,1:T(8,128)(2,1)S(1)}, bf16[768,2,112]{0,2,1:T(8,128)(2,1)}, u32[]{:S(2)}) copy-start(bf16[768,2,112]{0,2,1:T(8,128)(2,1)} %get-tuple-element.15) | copy-start | bytes 1032196
  141.1 7.6 %copy-start.3 = (bf16[224,1792]{1,0:T(8,128)(2,1)S(1)}, bf16[224,1792]{1,0:T(8,128)(2,1)}, u32[]{:S(2)}) copy-start(bf16[224,1792]{1,0:T(8,128)(2,1)} %param.17) | copy-start | bytes 2408452
  148.7 3.4 %copy-start.8 = (bf16[1792]{0:T(1024)(128)(2,1)S(1)}, bf16[1792]{0:T(1024)(128)(2,1)}, u32[]{:S(2)}) copy-start(bf16[1792]{0:T(1024)(128)(2,1)} %param.21) | copy-start | bytes 10756
  151.3 92.0 %all-gather.2.cloned.1.call-start = ((), (), s32[]{:S(2)}) async-start(), calls=%async_computation.3 | async-start | bytes 7096320 | tf_op jit(solution)/shard_map/all_gather | solution.py:190
  151.8 143.8 %reduce-scatter.2.cloned.1.call-start = ((), (), s32[]{:S(2)}) async-start(), calls=%async_computation.4 | async-start | bytes 3096576 | tf_op jit(solution)/shard_map/reduce_scatter | solution.py:199
  249.1 48.4 %copy-start.1 = (bf16[3,224,1792]{2,1,0:T(8,128)(2,1)S(1)}, bf16[3,224,1792]{2,1,0:T(8,128)(2,1)}, u32[]{:S(2)}) copy-start(bf16[3,224,1792]{2,1,0:T(8,128)(2,1)} %param.16) | copy-start | bytes 7225348
Sparse Core Ops, SparseCore 0:
  151.4 72.4 all-reduce.1
  259.8 35.7 reduce-scatter.1
Sparse Core Ops, SparseCore 1:
  154.8 88.5 all-gather.1

commit v15 on v13

--- a/solution.py
+++ b/solution.py
@@ -145,12 +145,8 @@
         axis=0,
         mode="clip",
     )
-    key_all = jnp.concatenate(
-        [key_rows, prefix[:, :, :head_column_set].reshape(req_per_dev * WINDOW, head_column_set)], axis=0
-    )
-    value_all = jnp.concatenate(
-        [value_row_block, prefix[:, :, head_column_set:].reshape(req_per_dev * WINDOW, head_column_set)], axis=0
-    )
+    prefix_keys = prefix[:, :, :head_column_set].reshape(req_per_dev * WINDOW, head_local, HEAD_SIZE)
+    prefix_values = prefix[:, :, head_column_set:].reshape(req_per_dev * WINDOW, head_local, HEAD_SIZE)
     distance = positions[:, None] - positions[None, :]
     local_ok = (request_of[:, None] == request_of[None, :]) & (distance >= 0) & (distance <= WINDOW)
     key_request = jnp.repeat(jnp.arange(req_per_dev, dtype=jnp.int32), WINDOW)
@@ -158,19 +154,35 @@
     prefix_ok = (request_of[:, None] == key_request[None, :]) & (
         key_offset[None, :] >= relative[:, None]
     )
-    allowed = jnp.concatenate([local_ok, prefix_ok], axis=1)
     query_heads = query_rows.reshape(tok_count, head_local, HEAD_SIZE)
-    key_heads = key_all.reshape(-1, head_local, HEAD_SIZE)
-    value_heads = value_all.reshape(-1, head_local, HEAD_SIZE)
-    scores = jnp.einsum(
-        "thd,shd->hts", query_heads, key_heads, preferred_element_type=jnp.float32
-    ) * (1.0 / math.sqrt(HEAD_SIZE))
-    masked = jnp.where(allowed[None], scores, -1e30)
-    row_max = jnp.max(masked, axis=-1, keepdims=True)
-    exp_scores = jnp.exp(masked - row_max)
-    weights = (exp_scores / jnp.sum(exp_scores, axis=-1, keepdims=True)).astype(jnp.bfloat16)
+    key_heads = key_rows.reshape(tok_count, head_local, HEAD_SIZE)
+    value_heads = value_row_block.reshape(tok_count, head_local, HEAD_SIZE)
+    scale = 1.0 / math.sqrt(HEAD_SIZE)
+    local_scores = jnp.where(
+        local_ok[None],
+        jnp.einsum("thd,shd->hts", query_heads, key_heads, preferred_element_type=jnp.float32) * scale,
+        -1e30,
+    )
+    prefix_scores = jnp.where(
+        prefix_ok[None],
+        jnp.einsum("thd,shd->hts", query_heads, prefix_keys, preferred_element_type=jnp.float32) * scale,
+        -1e30,
+    )
+    row_max = jnp.maximum(
+        jnp.max(local_scores, axis=-1, keepdims=True), jnp.max(prefix_scores, axis=-1, keepdims=True)
+    )
+    local_exp = jnp.exp(local_scores - row_max)
+    prefix_exp = jnp.exp(prefix_scores - row_max)
+    denom = jnp.sum(local_exp, axis=-1, keepdims=True) + jnp.sum(prefix_exp, axis=-1, keepdims=True)
+    local_weights = (local_exp / denom).astype(jnp.bfloat16)
+    prefix_weights = (prefix_exp / denom).astype(jnp.bfloat16)
     mixed = (
-        jnp.einsum("hts,shd->thd", weights, value_heads, preferred_element_type=jnp.float32)
+        (
+            jnp.einsum("hts,shd->thd", local_weights, value_heads, preferred_element_type=jnp.float32)
+            + jnp.einsum(
+                "hts,shd->thd", prefix_weights, prefix_values, preferred_element_type=jnp.float32
+            )
+        )
         .astype(jnp.bfloat16)
         .reshape(tok_count, head_column_set)
     )

time: 305 us -> 311 us (1.020)
  local copies, waits for them, and re-layouts: 12.5 us -> 20.3 us
  waiting for transfers between devices: 172 us -> 168 us
    sub x1 -> x0, matrix products: 9.55 us -> none  [per_device(): exp_scores = jnp.exp(masked - row_max)]
    dot_general x1 -> x4, matrix products: 7.56 us -> 16 us  [the longest x1 6.94 us: per_device(): jnp.einsum('hts,shd->thd', prefix_weights, prefix_values, preferred_eleme...]
    all_to_all x1, waiting for transfers between devices: 49.7 us -> 45.2 us  [per_device(): lax.all_to_all(source_pages, 'req', split_axis=0, concat_axis=0, tiled=True)]
    reshape x1 -> x3, local copies, waits for them, and re-layouts: 0.09 us -> 4.54 us  [the longest x1 3.18 us: per_device(): prefix[:, :, head_column_set:]]
    reduce_sum x1 -> x3, other arithmetic: 0.1 us -> 4.14 us  [the longest x1 2.92 us: per_device(): jnp.sum(prefix_exp, axis=-1, keepdims=True)]
  transfers between devices with their start and end apart: 4 -> 4, of which waited for: 4 -> 4; matrix products, arithmetic and copies ran while one was open for 7% -> 8% of each run, Pallas kernels for 0% -> 0%
where the time goes in v15:
time: 311 us
  waiting for transfers between devices  168 us (54%)
  matrix products  43.7 us (14%)
  blocking collectives  26.6 us (9%)
  local copies, waits for them, and re-layouts  20.3 us (7%)
  other arithmetic  16.5 us (5%)
  between operations  15.2 us (5%)
  starting transfers between devices  12 us (4%)
  Pallas kernels  8.82 us (3%)
    psum x1, waiting for transfers between devices, per_device(): lax.psum(attn_part.astype(jnp.bfloat16), 'mdl').astype(jnp.float32)  71.9 us
    all_to_all x1, waiting for transfers between devices, per_device(): lax.all_to_all(source_pages, 'req', split_axis=0, concat_axis=0, tiled=True)  45.2 us
    reduce_scatter x1, waiting for transfers between devices, per_device(): lax.psum_scatter(mlp_part.astype(jnp.bfloat16), 'mdl', scatter_dimension=...  36 us
    psum x1, blocking collectives, per_device(): rank_feat = lax.psum(rank_part.astype(jnp.bfloat16), 'mdl')  26.6 us
    all_gather x1, waiting for transfers between devices, per_device(): full_mlp = lax.all_gather(feedforward_weight, 'req', axis=1, tiled=True)  14.1 us
    all_to_all x1, starting transfers between devices, per_device(): lax.all_to_all(source_pages, 'req', split_axis=0, concat_axis=0, tiled=True)  11.9 us
    dot_general x1, matrix products, per_device(): jnp.einsum('tf,df->td', hidden, full_mlp[2], preferred_element_type=jnp.f...  10.5 us
    pallas_call x1, Pallas kernels, cut_windows(): pl.pallas_call(window_kernel, grid_spec=pltpu.PrefetchScalarGridSpec(num_...  8.82 us
  transfers between devices with their start and end apart: 4, of which 4 were waited for; matrix products, arithmetic and copies ran while one was open for 8% of the time, Pallas kernels for 0%

profile of v15, /device:TPU:8, one launch (start us, length us, event | category | flops | bytes accessed | tf_op | source)
XLA Modules:
  0.0 310.9 jit_solution(2881968611430084760)
XLA Ops:
  7.4 0.8 fusion.35
  8.4 0.2 reduce_window_sum.18
  8.6 0.8 mul.171
  9.5 0.8 mul.174
  10.4 0.1 copy.28
  10.5 0.6 min.12.slot_ref
  11.2 0.6 reshape.270.fill_ref
  11.8 8.8 %shard_map.145 = bf16[64,64,448]{2,1,0:T(8,128)(2,1)} custom-call(s32[64]{0:T(128)} %min.12.slot_ref, s32[64]{0:T(128)} %reshape.270.fill_ref, bf16[32,2,224,128]{3,2,1,0:T(8,128)(2,1)} %store_ref.1), custom_call_target="tpu_custom_call" | custom-call | tf_op jit(solution)/shard_map/pallas_call | solution.py:34
  20.6 11.9 %all-to-all-start = ((bf16[32,2,64,448]{3,2,1,0:T(8,128)(2,1)}), bf16[32,2,64,448]{3,2,1,0:T(8,128)(2,1)}, u32[]{:S(2)}, u32[]{:S(2)}) async-start(bf16[32,2,64,448]{3,2,1,0:T(8,128)(2,1)} %bitcast.66), calls=%async_computation | async-start | bytes 8388608 | tf_op jit(solution)/shard_map/all_to_all | solution.py:141
  32.7 0.1 reduce
  33.0 3.9 %fusion.17 = f32[3,768,224]{1,2,0:T(8,128)S(1)} fusion(bf16[3,224,1792]{2,1,0:T(8,128)(2,1)S(1)} %copy-done, bf16[768,1792]{1,0:T(8,128)(2,1)} %param.15), kind=kOutput, calls=%fused_computation.35 | convolution fusion | flops 1849688064 | bytes 7225344 | tf_op jit(solution)/shard_map/td,kcd->ktc/dot_general | solution.py:74
  36.9 1.4 copy-done.4
  38.4 2.8 fusion.47
  41.3 26.6 %psum.14 = bf16[768,16]{0,1:T(8,128)(2,1)S(1)} all-reduce(bf16[768,16]{0,1:T(8,128)(2,1)S(1)} %multiply_reduce_fusion), channel_id=1, replica_groups=mesh['req'=32,'mdl'=8] {'mdl'}, use_global_device_ids=true, to_apply=%region_4.5 | all-reduce | flops 12288 | bytes 49152 | tf_op jit(solution)/shard_map/psum | solution.py:89
  67.9 0.8 fusion.38
  68.6 0.2 convert_reduce_fusion
  68.8 0.8 fusion.37
  69.7 0.1 select_reduce_fusion.2
  69.8 0.1 select_reduce_fusion
  69.9 0.1 broadcast_multiply_fusion
  70.1 2.3 fusion.44
  72.3 2.1 fusion.48
  74.4 0.9 fusion.46
  75.4 0.3 fusion.13
  75.7 3.3 %fusion.6 = (f32[2,768]{1,0:T(2,128)S(1)}, f32[2,768,768]{1,2,0:T(8,128)}) fusion(pred[768,768]{0,1:T(8,128)(4,1)S(1)} %fusion.13, bf16[768,2,112]{0,2,1:T(8,128)(2,1)S(1)} %add_convert_fusion.2, bf16[768,2,112]{0,2,1:T(8,128)(2,1)S(1)} %bitcast.71), kind=kOutput, calls=%fused_computation.17 | convolution fusion | flops 267778560 | bytes 6002688 | tf_op jit(solution)/shard_map/thd,shd->hts/dot_general | solution.py:163
  79.0 2.1 compare_and_fusion
  81.1 45.2 %all-to-all-done = bf16[32,2,64,448]{3,2,1,0:T(8,128)(2,1)} async-done(((bf16[32,2,64,448]{3,2,1,0:T(8,128)(2,1)}), bf16[32,2,64,448]{3,2,1,0:T(8,128)(2,1)}, u32[]{:S(2)}, u32[]{:S(2)}) %all-to-all-start) | async-done | bytes 3670048 | tf_op jit(solution)/shard_map/all_to_all | solution.py:141
  126.3 2.8 gather_fusion
  129.2 1.3 fusion.45
  130.5 1.3 reshape.273
  131.7 4.1 %fusion = (f32[2,768]{1,0:T(2,128)S(1)}, f32[2,768,1536]{2,1,0:T(8,128)S(1)}) fusion(pred[768,1536]{1,0:T(8,128)(4,1)} %compare_and_fusion, bf16[768,2,112]{0,2,1:T(8,128)(2,1)S(1)} %add_convert_fusion.2, bf16[1536,2,112]{2,1,0:T(2,128)(2,1)} %reshape.273), kind=kOutput, calls=%fused_computation.4 | convolution fusion | flops 535558656 | bytes 11655168 | tf_op jit(solution)/shard_map/thd,shd->hts/dot_general | solution.py:168
  135.9 2.9 fusion.1
  138.9 1.8 copy-done.2
  140.7 0.6 slice-done
  141.3 0.3 slice-done.1
  141.6 1.1 fusion.7
  142.8 3.2 %reshape.274 = bf16[1536,2,112]{2,1,0:T(2,128)(2,1)} reshape(bf16[24,64,224]{2,1,0:T(8,128)(2,1)} %get-tuple-element.13) | data formatting | bytes 1376256 | tf_op jit(solution)/shard_map/reshape | solution.py:149
  146.0 6.9 %fusion.5 = f32[2,112,768]{2,1,0:T(8,128)S(1)} fusion(f32[2,768,1536]{2,1,0:T(8,128)} %copy-done.2, f32[2,768]{1,0:T(2,128)S(1)} %add.82, f32[2,768]{1,0:T(2,128)S(1)} %max.15, pred[768,1536]{1,0:T(8,128)(4,1)S(1)} %copy-done.3, bf16[1536,2,112]{2,1,0:T(2,128)(2,1)} %reshape.274), kind=kOutput, calls=%fused_computation.16 | convolution fusion | flops 540278784 | bytes 12005376 | tf_op jit(solution)/shard_map/hts,shd->thd/dot_general | solution.py:182
  153.0 1.7 fusion.21
  154.7 2.5 convolution_convert_fusion
  157.3 0.5 all-gather.2.cloned.1.call-update
  157.9 71.9 %all-reduce.2.cloned.1.call-done = bf16[768,1792]{1,0:T(8,128)(2,1)} async-done(((bf16[768,1792]{1,0:T(8,128)(2,1)}), bf16[768,1792]{1,0:T(8,128)(2,1)}) %all-reduce.2.cloned.1.call-update) | async-done | bytes 2752528 | tf_op jit(solution)/shard_map/psum | solution.py:195
  229.8 5.3 %fusion.2 = (f32[768]{0:T(1024)S(1)}, bf16[768,1792]{1,0:T(8,128)(2,1)}) fusion(bf16[768,1792]{1,0:T(8,128)(2,1)} %all-reduce.2.cloned.1.call-done, bf16[768,1792]{1,0:T(8,128)(2,1)} %param.15), kind=kLoop, calls=%fused_computation.8 | loop fusion | flops 9633024 | bytes 8260608 | tf_op jit(solution)/shard_map/reduce_sum | solution.py:198
  235.1 14.1 %all-gather.2.cloned.1.call-done = bf16[3,1792,608]{2,1,0:T(8,128)(2,1)} async-done(((bf16[3,56,608]{2,1,0:T(8,128)(2,1)}), bf16[3,1792,608]{2,1,0:T(8,128)(2,1)}) %all-gather.2.cloned.1.call-update) | async-done | bytes 6537232 | tf_op jit(solution)/shard_map/all_gather | solution.py:201
  249.2 5.8 %fusion.16 = f32[768,608]{0,1:T(8,128)} fusion(bf16[3,1792,608]{2,1,0:T(8,128)(2,1)} %all-gather.2.cloned.1.call-done, bf16[768,1792]{1,0:T(8,128)(2,1)} %get-tuple-element.10, f32[1792]{0:T(1024)S(1)} %convert_element_type.122, f32[768]{0:T(1024)S(1)} %add_rsqrt_fusion), kind=kOutput, calls=%fused_computation.33 | convolution fusion | flops 1679032320 | bytes 6924288 | tf_op jit(solution)/shard_map/dot_general | solution.py:202
  255.1 10.5 %convolution_convert_fusion.1 = bf16[768,1792]{1,0:T(8,128)(2,1)} fusion(bf16[3,1792,608]{2,1,0:T(8,128)(2,1)} %all-gather.2.cloned.1.call-done, f32[768,608]{0,1:T(8,128)} %fusion.16, bf16[768,1792]{1,0:T(8,128)(2,1)} %get-tuple-element.10, f32[1792]{0:T(1024)S(1)} %convert_element_type.122, f32[768]{0:T(1024)S(1)} %add_rsqrt_fusion), kind=kOutput, calls=%fused_computation.20 | convolution fusion | flops 3356737536 | bytes 11970560 | tf_op jit(solution)/shard_map/tf,df->td/dot_general | solution.py:206
  265.6 36.0 %reduce-scatter.2.cloned.1.call-done = bf16[96,1792]{1,0:T(8,128)(2,1)} async-done(((bf16[768,1792]{1,0:T(8,128)(2,1)}), bf16[96,1792]{1,0:T(8,128)(2,1)}) %reduce-scatter.2.cloned.1.call-update) | async-done | bytes 344080 | tf_op jit(solution)/shard_map/reduce_scatter | solution.py:210
  301.6 1.9 add_convert_fusion.1
  (68 shorter events, 1.4 us)
Async XLA Ops:
  7.4 25.6 %copy-start = (bf16[3,224,1792]{2,1,0:T(8,128)(2,1)S(1)}, bf16[3,224,1792]{2,1,0:T(8,128)(2,1)}, u32[]{:S(2)}) copy-start(bf16[3,224,1792]{2,1,0:T(8,128)(2,1)} %param.16) | copy-start | bytes 7225348
  20.6 11.9 %copy-start.11 = (s32[1,24]{1,0:T(1,128)S(1)}, s32[1,24]{1,0:T(1,128)}, u32[]{:S(2)}) copy-start(s32[1,24]{1,0:T(1,128)} %param.25) | copy-start | bytes 292
  20.6 105.7 %all-to-all-start = ((bf16[32,2,64,448]{3,2,1,0:T(8,128)(2,1)}), bf16[32,2,64,448]{3,2,1,0:T(8,128)(2,1)}, u32[]{:S(2)}, u32[]{:S(2)}) async-start(bf16[32,2,64,448]{3,2,1,0:T(8,128)(2,1)} %bitcast.66), calls=%async_computation | async-start | bytes 8388608 | tf_op jit(solution)/shard_map/all_to_all | solution.py:141
  32.5 197.3 %all-reduce.2.cloned.1.call-start = ((), (), s32[]{:S(2)}) async-start(), calls=%async_computation.2 | async-start | bytes 5505024 | tf_op jit(solution)/shard_map/psum | solution.py:195
  33.0 5.4 %copy-start.9 = (s32[768]{0:T(1024)S(1)}, s32[768]{0:T(1024)}, u32[]{:S(2)}) copy-start(s32[768]{0:T(1024)} %param.24) | copy-start | bytes 9220
  33.0 5.4 %copy-start.8 = (bf16[8,1792,16]{1,2,0:T(8,128)(2,1)S(1)}, bf16[8,1792,16]{1,2,0:T(8,128)(2,1)}, u32[]{:S(2)}) copy-start(bf16[8,1792,16]{1,2,0:T(8,128)(2,1)} %param.18) | copy-start | bytes 1376260
  36.9 1.4 copy-start.4
  38.3 31.3 %copy-start.12 = (f32[4]{0:T(128)S(1)}, f32[4]{0:T(128)}, u32[]{:S(2)}) copy-start(f32[4]{0:T(128)} %param.20) | copy-start | bytes 52
  38.3 31.3 %copy-start.13 = (s32[24]{0:T(128)S(1)}, s32[24]{0:T(128)}, u32[]{:S(2)}) copy-start(s32[24]{0:T(128)} %param.26) | copy-start | bytes 292
  131.7 4.2 %copy-start.3 = (pred[768,1536]{1,0:T(8,128)(4,1)S(1)}, pred[768,1536]{1,0:T(8,128)(4,1)}, u32[]{:S(2)}) copy-start(pred[768,1536]{1,0:T(8,128)(4,1)} %compare_and_fusion) | copy-start | bytes 3538948
  135.9 4.8 %copy-start.2 = (f32[2,768,1536]{2,1,0:T(8,128)}, f32[2,768,1536]{2,1,0:T(8,128)S(1)}, u32[]{:S(2)}) copy-start(f32[2,768,1536]{2,1,0:T(8,128)S(1)} %get-tuple-element.20) | copy-start | bytes 28311556
  135.9 5.4 %slice-start = ((s8[4718592]{0:T(1024)(128)(4,1)}), s8[4194304]{0:T(1024)(128)(4,1)S(1)}, s32[]{:S(2)}) async-start(s8[4718592]{0:T(1024)(128)(4,1)} %bitcast.62), calls=%async_computation.5 | async-start | bytes 8388608
  135.9 5.7 %slice-start.1 = ((s8[4718592]{0:T(1024)(128)(4,1)}), s8[524288]{0:T(1024)(128)(4,1)S(1)}, s32[]{:S(2)}) async-start(s8[4718592]{0:T(1024)(128)(4,1)} %bitcast.62), calls=%async_computation.6 | async-start | bytes 1048576
  142.8 10.2 %slice-start.2 = ((s8[4718592]{0:T(1024)(128)(4,1)}), s8[524288]{0:T(1024)(128)(4,1)S(1)}, s32[]{:S(2)}) async-start(s8[4718592]{0:T(1024)(128)(4,1)} %bitcast.64), calls=%async_computation.7 | async-start | bytes 1048576
  145.9 7.0 %slice-start.3 = ((s8[4718592]{0:T(1024)(128)(4,1)}), s8[4194304]{0:T(1024)(128)(4,1)S(1)}, s32[]{:S(2)}) async-start(s8[4718592]{0:T(1024)(128)(4,1)} %bitcast.64), calls=%async_computation.8 | async-start | bytes 8388608
  145.9 7.0 %copy-start.6 = (f32[1,768,224]{1,2,0:T(8,128)S(1)}, f32[1,768,224]{1,2,0:T(8,128)}, u32[]{:S(2)}) copy-start(f32[1,768,224]{1,2,0:T(8,128)} %get-tuple-element.11) | copy-start | bytes 2064388
  146.0 7.0 %copy-start.7 = (f32[768,1,224]{0,2,1:T(8,128)S(1)}, f32[768,1,224]{0,2,1:T(8,128)}, u32[]{:S(2)}) copy-start(f32[768,1,224]{0,2,1:T(8,128)} %get-tuple-element.15) | copy-start | bytes 2064388
  153.0 1.7 copy-start.5
  154.6 3.2 %copy-start.10 = (bf16[1792]{0:T(1024)(128)(2,1)S(1)}, bf16[1792]{0:T(1024)(128)(2,1)}, u32[]{:S(2)}) copy-start(bf16[1792]{0:T(1024)(128)(2,1)} %param.21) | copy-start | bytes 10756
  157.2 92.0 %all-gather.2.cloned.1.call-start = ((), (), s32[]{:S(2)}) async-start(), calls=%async_computation.3 | async-start | bytes 7096320 | tf_op jit(solution)/shard_map/all_gather | solution.py:201
  157.8 143.8 %reduce-scatter.2.cloned.1.call-start = ((), (), s32[]{:S(2)}) async-start(), calls=%async_computation.4 | async-start | bytes 3096576 | tf_op jit(solution)/shard_map/reduce_scatter | solution.py:210
  255.1 48.4 %copy-start.1 = (bf16[3,224,1792]{2,1,0:T(8,128)(2,1)S(1)}, bf16[3,224,1792]{2,1,0:T(8,128)(2,1)}, u32[]{:S(2)}) copy-start(bf16[3,224,1792]{2,1,0:T(8,128)(2,1)} %param.16) | copy-start | bytes 7225348
Sparse Core Ops, SparseCore 0:
  157.3 72.4 all-reduce.1
  265.8 35.7 reduce-scatter.1
Sparse Core Ops, SparseCore 1:
  160.7 88.5 all-gather.1

commit v16 on v13

--- a/solution.py
+++ b/solution.py
@@ -25,7 +25,7 @@
         ).astype(out_ref.dtype)
         return carry
 
-    lax.fori_loop(0, count, pick_rows, 0, unroll=8)
+    lax.fori_loop(0, count, pick_rows, 0, unroll=16)
 
 
 def cut_windows(store, slots, fills):

time: 305 us -> 305 us (level)
  no operation moved by 1% of the time
where the time goes in v16:
time: 305 us; the launch traced here: 304 us
  waiting for transfers between devices  172 us (56%)
  matrix products  43.6 us (14%)
  blocking collectives  26.8 us (9%)
  between operations  15.2 us (5%)
  other arithmetic  13.9 us (5%)
  local copies, waits for them, and re-layouts  12.5 us (4%)
  starting transfers between devices  12.2 us (4%)
  Pallas kernels  8.27 us (3%)
    psum x1, waiting for transfers between devices, per_device(): lax.psum(attn_part.astype(jnp.bfloat16), 'mdl').astype(jnp.float32)  71.8 us
    all_to_all x1, waiting for transfers between devices, per_device(): lax.all_to_all(source_pages, 'req', split_axis=0, concat_axis=0, tiled=True)  49.7 us
    reduce_scatter x1, waiting for transfers between devices, per_device(): lax.psum_scatter(mlp_part.astype(jnp.bfloat16), 'mdl', scatter_dimension=...  36 us
    psum x1, blocking collectives, per_device(): rank_feat = lax.psum(rank_part.astype(jnp.bfloat16), 'mdl')  26.8 us
    all_gather x1, waiting for transfers between devices, per_device(): full_mlp = lax.all_gather(feedforward_weight, 'req', axis=1, tiled=True)  14.1 us
    all_to_all x1, starting transfers between devices, per_device(): lax.all_to_all(source_pages, 'req', split_axis=0, concat_axis=0, tiled=True)  11.9 us
    dot_general x1, matrix products, per_device(): jnp.einsum('tf,df->td', hidden, full_mlp[2], preferred_element_type=jnp.f...  10.5 us
    sub x1, matrix products, per_device(): exp_scores = jnp.exp(masked - row_max)  9.55 us
  transfers between devices with their start and end apart: 4, of which 4 were waited for; matrix products, arithmetic and copies ran while one was open for 7% of the time, Pallas kernels for 0%

profile of v16, /device:TPU:8, one launch (start us, length us, event | category | flops | bytes accessed | tf_op | source)
XLA Modules:
  0.0 304.5 jit_solution(14150400913935117457)
XLA Ops:
  7.4 0.8 fusion.36
  8.4 0.2 reduce_window_sum.18
  8.6 0.8 mul.159
  9.5 0.8 mul.162
  10.4 0.1 copy.26
  10.5 0.6 min.12.slot_ref
  11.1 0.1 copy.28
  11.2 0.6 reshape.164.fill_ref
  11.8 8.3 %shard_map.145 = bf16[64,64,448]{2,1,0:T(8,128)(2,1)} custom-call(s32[64]{0:T(128)} %min.12.slot_ref, s32[64]{0:T(128)} %reshape.164.fill_ref, bf16[32,2,224,128]{3,2,1,0:T(8,128)(2,1)} %store_ref.1), custom_call_target="tpu_custom_call" | custom-call | tf_op jit(solution)/shard_map/pallas_call | solution.py:34
  20.1 11.9 %all-to-all-start = ((bf16[32,2,64,448]{3,2,1,0:T(8,128)(2,1)}), bf16[32,2,64,448]{3,2,1,0:T(8,128)(2,1)}, u32[]{:S(2)}, u32[]{:S(2)}) async-start(bf16[32,2,64,448]{3,2,1,0:T(8,128)(2,1)} %bitcast.61), calls=%async_computation | async-start | bytes 8388608 | tf_op jit(solution)/shard_map/all_to_all | solution.py:141
  32.0 0.1 copy.21
  32.2 0.1 reduce
  32.4 3.9 %fusion.17 = f32[3,768,224]{1,2,0:T(8,128)S(1)} fusion(bf16[3,224,1792]{2,1,0:T(8,128)(2,1)S(1)} %copy-done, bf16[768,1792]{1,0:T(8,128)(2,1)} %param.15), kind=kOutput, calls=%fused_computation.33 | convolution fusion | flops 1849688064 | bytes 7225344 | tf_op jit(solution)/shard_map/td,kcd->ktc/dot_general | solution.py:74
  36.4 1.4 copy-done.2
  37.9 2.8 fusion.52
  40.7 26.8 %psum.14 = bf16[768,16]{0,1:T(8,128)(2,1)S(1)} all-reduce(bf16[768,16]{0,1:T(8,128)(2,1)S(1)} %multiply_reduce_fusion), channel_id=1, replica_groups=mesh['req'=32,'mdl'=8] {'mdl'}, use_global_device_ids=true, to_apply=%region_4.5 | all-reduce | flops 12288 | bytes 49152 | tf_op jit(solution)/shard_map/psum | solution.py:89
  67.5 0.8 fusion.39
  68.3 0.2 convert_reduce_fusion
  68.5 0.8 fusion.38
  69.3 0.1 select_reduce_fusion.2
  69.4 0.1 select_reduce_fusion.1
  69.6 0.1 broadcast_multiply_fusion
  69.7 1.4 fusion.48
  71.1 0.9 fusion.53
  72.0 0.1 fusion.50
  72.1 0.3 fusion.14
  72.5 1.1 add_convert_fusion.3
  73.5 1.2 compare_and_fusion
  74.8 1.3 pad_add_fusion
  76.1 49.7 %all-to-all-done = bf16[32,2,64,448]{3,2,1,0:T(8,128)(2,1)} async-done(((bf16[32,2,64,448]{3,2,1,0:T(8,128)(2,1)}), bf16[32,2,64,448]{3,2,1,0:T(8,128)(2,1)}, u32[]{:S(2)}, u32[]{:S(2)}) %all-to-all-start) | async-done | bytes 3670048 | tf_op jit(solution)/shard_map/all_to_all | solution.py:141
  125.7 2.8 gather_fusion
  128.6 0.4 fusion.49
  129.0 0.4 concatenate.18
  129.4 0.6 copy.30
  130.0 0.4 concatenate.15
  130.4 0.6 copy.29
  131.0 9.5 %fusion.51 = (f32[2,768]{1,0:T(2,128)S(1)}, f32[2,768,2304]{2,1,0:T(8,128)}) fusion(pred[768,2304]{1,0:T(8,128)(4,1)} %pad_add_fusion, bf16[768,2,112]{0,2,1:T(8,128)(2,1)S(1)} %copy-done.6, bf16[1536,2,112]{0,2,1:T(8,128)(2,1)S(1)} %copy.30, bf16[768,2,112]{0,2,1:T(8,128)(2,1)S(1)} %bitcast.69), kind=kOutput, calls=%fused_computation.90 | convolution fusion | flops 808945920 | bytes 17307648 | tf_op jit(solution)/shard_map/sub | solution.py:170
  140.6 7.6 %fusion.22 = bf16[2,112,768]{2,1,0:T(8,128)(2,1)S(1)} fusion(f32[2,768,2304]{2,1,0:T(8,128)} %get-tuple-element.20, f32[2,768]{1,0:T(2,128)S(1)} %get-tuple-element.19, bf16[1536,2,112]{0,2,1:T(8,128)(2,1)S(1)} %copy.29, bf16[768,2,112]{0,2,1:T(8,128)(2,1)S(1)} %copy-done.5), kind=kOutput, calls=%fused_computation.35 | convolution fusion | flops 802037760 | bytes 15538176 | tf_op jit(solution)/shard_map/hts,shd->thd/dot_general | solution.py:173
  148.2 2.5 convolution_convert_fusion
  150.8 0.5 all-gather.2.cloned.1.call-update
  151.3 0.3 reduce-scatter.2.cloned.1.call-start
  151.6 71.8 %all-reduce.2.cloned.1.call-done = bf16[768,1792]{1,0:T(8,128)(2,1)} async-done(((bf16[768,1792]{1,0:T(8,128)(2,1)}), bf16[768,1792]{1,0:T(8,128)(2,1)}) %all-reduce.2.cloned.1.call-update) | async-done | bytes 2752528 | tf_op jit(solution)/shard_map/psum | solution.py:183
  223.4 5.3 %fusion.6 = (f32[768]{0:T(1024)S(1)}, bf16[768,1792]{1,0:T(8,128)(2,1)}) fusion(bf16[768,1792]{1,0:T(8,128)(2,1)} %all-reduce.2.cloned.1.call-done, bf16[768,1792]{1,0:T(8,128)(2,1)} %param.15), kind=kLoop, calls=%fused_computation.13 | loop fusion | flops 9633024 | bytes 8260608 | tf_op jit(solution)/shard_map/reduce_sum | solution.py:186
  228.7 14.1 %all-gather.2.cloned.1.call-done = bf16[3,1792,608]{2,1,0:T(8,128)(2,1)} async-done(((bf16[3,56,608]{2,1,0:T(8,128)(2,1)}), bf16[3,1792,608]{2,1,0:T(8,128)(2,1)}) %all-gather.2.cloned.1.call-update) | async-done | bytes 6537232 | tf_op jit(solution)/shard_map/all_gather | solution.py:189
  242.8 5.8 %fusion.16 = f32[768,608]{0,1:T(8,128)} fusion(bf16[3,1792,608]{2,1,0:T(8,128)(2,1)} %all-gather.2.cloned.1.call-done, bf16[768,1792]{1,0:T(8,128)(2,1)} %get-tuple-element.10, f32[1792]{0:T(1024)S(1)} %convert_element_type.118, f32[768]{0:T(1024)S(1)} %add_rsqrt_fusion), kind=kOutput, calls=%fused_computation.31 | convolution fusion | flops 1679032320 | bytes 6924288 | tf_op jit(solution)/shard_map/dot_general | solution.py:190
  248.6 10.5 %convolution_convert_fusion.1 = bf16[768,1792]{1,0:T(8,128)(2,1)} fusion(bf16[3,1792,608]{2,1,0:T(8,128)(2,1)} %all-gather.2.cloned.1.call-done, f32[768,608]{0,1:T(8,128)} %fusion.16, bf16[768,1792]{1,0:T(8,128)(2,1)} %get-tuple-element.10, f32[1792]{0:T(1024)S(1)} %convert_element_type.118, f32[768]{0:T(1024)S(1)} %add_rsqrt_fusion), kind=kOutput, calls=%fused_computation.19 | convolution fusion | flops 3356737536 | bytes 11970560 | tf_op jit(solution)/shard_map/tf,df->td/dot_general | solution.py:194
  259.2 36.0 %reduce-scatter.2.cloned.1.call-done = bf16[96,1792]{1,0:T(8,128)(2,1)} async-done(((bf16[768,1792]{1,0:T(8,128)(2,1)}), bf16[96,1792]{1,0:T(8,128)(2,1)}) %reduce-scatter.2.cloned.1.call-update) | async-done | bytes 344080 | tf_op jit(solution)/shard_map/reduce_scatter | solution.py:198
  295.2 1.9 add_convert_fusion.1
  (53 shorter events, 1.1 us)
Async XLA Ops:
  7.4 25.1 %copy-start = (bf16[3,224,1792]{2,1,0:T(8,128)(2,1)S(1)}, bf16[3,224,1792]{2,1,0:T(8,128)(2,1)}, u32[]{:S(2)}) copy-start(bf16[3,224,1792]{2,1,0:T(8,128)(2,1)} %param.16) | copy-start | bytes 7225348
  20.1 11.9 %copy-start.9 = (s32[1,24]{1,0:T(1,128)S(1)}, s32[1,24]{1,0:T(1,128)}, u32[]{:S(2)}) copy-start(s32[1,24]{1,0:T(1,128)} %param.25) | copy-start | bytes 292
  20.1 105.7 %all-to-all-start = ((bf16[32,2,64,448]{3,2,1,0:T(8,128)(2,1)}), bf16[32,2,64,448]{3,2,1,0:T(8,128)(2,1)}, u32[]{:S(2)}, u32[]{:S(2)}) async-start(bf16[32,2,64,448]{3,2,1,0:T(8,128)(2,1)} %bitcast.61), calls=%async_computation | async-start | bytes 8388608 | tf_op jit(solution)/shard_map/all_to_all | solution.py:141
  32.0 191.4 %all-reduce.2.cloned.1.call-start = ((), (), s32[]{:S(2)}) async-start(), calls=%async_computation.2 | async-start | bytes 5505024 | tf_op jit(solution)/shard_map/psum | solution.py:183
  32.4 5.4 %copy-start.7 = (s32[768]{0:T(1024)S(1)}, s32[768]{0:T(1024)}, u32[]{:S(2)}) copy-start(s32[768]{0:T(1024)} %param.24) | copy-start | bytes 9220
  32.4 5.4 %copy-start.4 = (bf16[8,1792,16]{1,2,0:T(8,128)(2,1)S(1)}, bf16[8,1792,16]{1,2,0:T(8,128)(2,1)}, u32[]{:S(2)}) copy-start(bf16[8,1792,16]{1,2,0:T(8,128)(2,1)} %param.18) | copy-start | bytes 1376260
  36.3 1.4 copy-start.2
  37.8 31.5 %copy-start.11 = (f32[4]{0:T(128)S(1)}, f32[4]{0:T(128)}, u32[]{:S(2)}) copy-start(f32[4]{0:T(128)} %param.20) | copy-start | bytes 52
  37.8 31.5 %copy-start.12 = (s32[24]{0:T(128)S(1)}, s32[24]{0:T(128)}, u32[]{:S(2)}) copy-start(s32[24]{0:T(128)} %param.26) | copy-start | bytes 292
  40.7 30.4 %copy-start.10 = (bf16[2,224,1024]{2,1,0:T(8,128)(2,1)S(1)}, bf16[2,224,1024]{2,1,0:T(8,128)(2,1)}, u32[]{:S(2)}) copy-start(bf16[2,224,1024]{2,1,0:T(8,128)(2,1)} %param.19) | copy-start | bytes 2752516
  129.4 1.6 copy-start.6
  131.0 9.6 %copy-start.5 = (bf16[768,2,112]{0,2,1:T(8,128)(2,1)S(1)}, bf16[768,2,112]{0,2,1:T(8,128)(2,1)}, u32[]{:S(2)}) copy-start(bf16[768,2,112]{0,2,1:T(8,128)(2,1)} %get-tuple-element.17) | copy-start | bytes 1032196
  140.6 7.6 %copy-start.3 = (bf16[224,1792]{1,0:T(8,128)(2,1)S(1)}, bf16[224,1792]{1,0:T(8,128)(2,1)}, u32[]{:S(2)}) copy-start(bf16[224,1792]{1,0:T(8,128)(2,1)} %param.17) | copy-start | bytes 2408452
  148.2 3.4 %copy-start.8 = (bf16[1792]{0:T(1024)(128)(2,1)S(1)}, bf16[1792]{0:T(1024)(128)(2,1)}, u32[]{:S(2)}) copy-start(bf16[1792]{0:T(1024)(128)(2,1)} %param.21) | copy-start | bytes 10756
  150.7 92.1 %all-gather.2.cloned.1.call-start = ((), (), s32[]{:S(2)}) async-start(), calls=%async_computation.3 | async-start | bytes 7096320 | tf_op jit(solution)/shard_map/all_gather | solution.py:189
  151.3 143.8 %reduce-scatter.2.cloned.1.call-start = ((), (), s32[]{:S(2)}) async-start(), calls=%async_computation.4 | async-start | bytes 3096576 | tf_op jit(solution)/shard_map/reduce_scatter | solution.py:198
  248.6 48.4 %copy-start.1 = (bf16[3,224,1792]{2,1,0:T(8,128)(2,1)S(1)}, bf16[3,224,1792]{2,1,0:T(8,128)(2,1)}, u32[]{:S(2)}) copy-start(bf16[3,224,1792]{2,1,0:T(8,128)(2,1)} %param.16) | copy-start | bytes 7225348
Sparse Core Ops, SparseCore 0:
  150.9 72.4 all-reduce.1
  259.3 35.7 reduce-scatter.1
Sparse Core Ops, SparseCore 1:
  154.2 88.5 all-gather.1

commit v17 on v16

--- a/solution.py
+++ b/solution.py
@@ -25,7 +25,7 @@
         ).astype(out_ref.dtype)
         return carry
 
-    lax.fori_loop(0, count, pick_rows, 0, unroll=16)
+    lax.fori_loop(0, count, pick_rows, 0, unroll=32)
 
 
 def cut_windows(store, slots, fills):

time: 305 us -> 305 us (level)
  no operation moved by 1% of the time
where the time goes in v17:
time: 305 us; the launch traced here: 304 us
  waiting for transfers between devices  172 us (56%)
  matrix products  43.6 us (14%)
  blocking collectives  26.8 us (9%)
  between operations  15.2 us (5%)
  other arithmetic  13.9 us (5%)
  local copies, waits for them, and re-layouts  12.5 us (4%)
  starting transfers between devices  12.2 us (4%)
  Pallas kernels  7.99 us (3%)
    psum x1, waiting for transfers between devices, per_device(): lax.psum(attn_part.astype(jnp.bfloat16), 'mdl').astype(jnp.float32)  71.7 us
    all_to_all x1, waiting for transfers between devices, per_device(): lax.all_to_all(source_pages, 'req', split_axis=0, concat_axis=0, tiled=True)  49.7 us
    reduce_scatter x1, waiting for transfers between devices, per_device(): lax.psum_scatter(mlp_part.astype(jnp.bfloat16), 'mdl', scatter_dimension=...  36 us
    psum x1, blocking collectives, per_device(): rank_feat = lax.psum(rank_part.astype(jnp.bfloat16), 'mdl')  26.8 us
    all_gather x1, waiting for transfers between devices, per_device(): full_mlp = lax.all_gather(feedforward_weight, 'req', axis=1, tiled=True)  14.1 us
    all_to_all x1, starting transfers between devices, per_device(): lax.all_to_all(source_pages, 'req', split_axis=0, concat_axis=0, tiled=True)  11.9 us
    dot_general x1, matrix products, per_device(): jnp.einsum('tf,df->td', hidden, full_mlp[2], preferred_element_type=jnp.f...  10.5 us
    sub x1, matrix products, per_device(): exp_scores = jnp.exp(masked - row_max)  9.55 us
  transfers between devices with their start and end apart: 4, of which 4 were waited for; matrix products, arithmetic and copies ran while one was open for 7% of the time, Pallas kernels for 0%

profile of v17, /device:TPU:8, one launch (start us, length us, event | category | flops | bytes accessed | tf_op | source)
XLA Modules:
  0.0 304.2 jit_solution(14797715221058181212)
XLA Ops:
  7.4 0.8 fusion.36
  8.4 0.2 reduce_window_sum.18
  8.6 0.8 mul.159
  9.5 0.8 mul.162
  10.4 0.1 copy.26
  10.5 0.6 min.12.slot_ref
  11.1 0.1 copy.28
  11.2 0.6 reshape.164.fill_ref
  11.8 8.0 %shard_map.145 = bf16[64,64,448]{2,1,0:T(8,128)(2,1)} custom-call(s32[64]{0:T(128)} %min.12.slot_ref, s32[64]{0:T(128)} %reshape.164.fill_ref, bf16[32,2,224,128]{3,2,1,0:T(8,128)(2,1)} %store_ref.1), custom_call_target="tpu_custom_call" | custom-call | tf_op jit(solution)/shard_map/pallas_call | solution.py:34
  19.8 11.9 %all-to-all-start = ((bf16[32,2,64,448]{3,2,1,0:T(8,128)(2,1)}), bf16[32,2,64,448]{3,2,1,0:T(8,128)(2,1)}, u32[]{:S(2)}, u32[]{:S(2)}) async-start(bf16[32,2,64,448]{3,2,1,0:T(8,128)(2,1)} %bitcast.61), calls=%async_computation | async-start | bytes 8388608 | tf_op jit(solution)/shard_map/all_to_all | solution.py:141
  31.7 0.1 copy.21
  31.9 0.1 reduce
  32.2 3.9 %fusion.17 = f32[3,768,224]{1,2,0:T(8,128)S(1)} fusion(bf16[3,224,1792]{2,1,0:T(8,128)(2,1)S(1)} %copy-done, bf16[768,1792]{1,0:T(8,128)(2,1)} %param.15), kind=kOutput, calls=%fused_computation.33 | convolution fusion | flops 1849688064 | bytes 7225344 | tf_op jit(solution)/shard_map/td,kcd->ktc/dot_general | solution.py:74
  36.1 1.4 copy-done.2
  37.6 2.8 fusion.52
  40.5 26.8 %psum.14 = bf16[768,16]{0,1:T(8,128)(2,1)S(1)} all-reduce(bf16[768,16]{0,1:T(8,128)(2,1)S(1)} %multiply_reduce_fusion), channel_id=1, replica_groups=mesh['req'=32,'mdl'=8] {'mdl'}, use_global_device_ids=true, to_apply=%region_4.5 | all-reduce | flops 12288 | bytes 49152 | tf_op jit(solution)/shard_map/psum | solution.py:89
  67.3 0.8 fusion.39
  68.0 0.2 convert_reduce_fusion
  68.2 0.8 fusion.38
  69.1 0.1 select_reduce_fusion.2
  69.2 0.1 select_reduce_fusion.1
  69.3 0.1 broadcast_multiply_fusion
  69.4 1.4 fusion.48
  70.9 0.9 fusion.53
  71.8 0.1 fusion.50
  71.9 0.3 fusion.14
  72.2 1.1 add_convert_fusion.3
  73.2 1.2 compare_and_fusion
  74.5 1.3 pad_add_fusion
  75.8 49.7 %all-to-all-done = bf16[32,2,64,448]{3,2,1,0:T(8,128)(2,1)} async-done(((bf16[32,2,64,448]{3,2,1,0:T(8,128)(2,1)}), bf16[32,2,64,448]{3,2,1,0:T(8,128)(2,1)}, u32[]{:S(2)}, u32[]{:S(2)}) %all-to-all-start) | async-done | bytes 3670048 | tf_op jit(solution)/shard_map/all_to_all | solution.py:141
  125.5 2.8 gather_fusion
  128.3 0.4 fusion.49
  128.7 0.4 concatenate.18
  129.1 0.6 copy.30
  129.8 0.4 concatenate.15
  130.2 0.6 copy.29
  130.8 9.6 %fusion.51 = (f32[2,768]{1,0:T(2,128)S(1)}, f32[2,768,2304]{2,1,0:T(8,128)}) fusion(pred[768,2304]{1,0:T(8,128)(4,1)} %pad_add_fusion, bf16[768,2,112]{0,2,1:T(8,128)(2,1)S(1)} %copy-done.6, bf16[1536,2,112]{0,2,1:T(8,128)(2,1)S(1)} %copy.30, bf16[768,2,112]{0,2,1:T(8,128)(2,1)S(1)} %bitcast.69), kind=kOutput, calls=%fused_computation.90 | convolution fusion | flops 808945920 | bytes 17307648 | tf_op jit(solution)/shard_map/sub | solution.py:170
  140.3 7.6 %fusion.22 = bf16[2,112,768]{2,1,0:T(8,128)(2,1)S(1)} fusion(f32[2,768,2304]{2,1,0:T(8,128)} %get-tuple-element.20, f32[2,768]{1,0:T(2,128)S(1)} %get-tuple-element.19, bf16[1536,2,112]{0,2,1:T(8,128)(2,1)S(1)} %copy.29, bf16[768,2,112]{0,2,1:T(8,128)(2,1)S(1)} %copy-done.5), kind=kOutput, calls=%fused_computation.35 | convolution fusion | flops 802037760 | bytes 15538176 | tf_op jit(solution)/shard_map/hts,shd->thd/dot_general | solution.py:173
  147.9 2.5 convolution_convert_fusion
  150.5 0.5 all-gather.2.cloned.1.call-update
  151.1 0.3 reduce-scatter.2.cloned.1.call-start
  151.4 71.7 %all-reduce.2.cloned.1.call-done = bf16[768,1792]{1,0:T(8,128)(2,1)} async-done(((bf16[768,1792]{1,0:T(8,128)(2,1)}), bf16[768,1792]{1,0:T(8,128)(2,1)}) %all-reduce.2.cloned.1.call-update) | async-done | bytes 2752528 | tf_op jit(solution)/shard_map/psum | solution.py:183
  223.1 5.3 %fusion.6 = (f32[768]{0:T(1024)S(1)}, bf16[768,1792]{1,0:T(8,128)(2,1)}) fusion(bf16[768,1792]{1,0:T(8,128)(2,1)} %all-reduce.2.cloned.1.call-done, bf16[768,1792]{1,0:T(8,128)(2,1)} %param.15), kind=kLoop, calls=%fused_computation.13 | loop fusion | flops 9633024 | bytes 8260608 | tf_op jit(solution)/shard_map/reduce_sum | solution.py:186
  228.4 14.1 %all-gather.2.cloned.1.call-done = bf16[3,1792,608]{2,1,0:T(8,128)(2,1)} async-done(((bf16[3,56,608]{2,1,0:T(8,128)(2,1)}), bf16[3,1792,608]{2,1,0:T(8,128)(2,1)}) %all-gather.2.cloned.1.call-update) | async-done | bytes 6537232 | tf_op jit(solution)/shard_map/all_gather | solution.py:189
  242.5 5.8 %fusion.16 = f32[768,608]{0,1:T(8,128)} fusion(bf16[3,1792,608]{2,1,0:T(8,128)(2,1)} %all-gather.2.cloned.1.call-done, bf16[768,1792]{1,0:T(8,128)(2,1)} %get-tuple-element.10, f32[1792]{0:T(1024)S(1)} %convert_element_type.118, f32[768]{0:T(1024)S(1)} %add_rsqrt_fusion), kind=kOutput, calls=%fused_computation.31 | convolution fusion | flops 1679032320 | bytes 6924288 | tf_op jit(solution)/shard_map/dot_general | solution.py:190
  248.4 10.5 %convolution_convert_fusion.1 = bf16[768,1792]{1,0:T(8,128)(2,1)} fusion(bf16[3,1792,608]{2,1,0:T(8,128)(2,1)} %all-gather.2.cloned.1.call-done, f32[768,608]{0,1:T(8,128)} %fusion.16, bf16[768,1792]{1,0:T(8,128)(2,1)} %get-tuple-element.10, f32[1792]{0:T(1024)S(1)} %convert_element_type.118, f32[768]{0:T(1024)S(1)} %add_rsqrt_fusion), kind=kOutput, calls=%fused_computation.19 | convolution fusion | flops 3356737536 | bytes 11970560 | tf_op jit(solution)/shard_map/tf,df->td/dot_general | solution.py:194
  258.9 36.0 %reduce-scatter.2.cloned.1.call-done = bf16[96,1792]{1,0:T(8,128)(2,1)} async-done(((bf16[768,1792]{1,0:T(8,128)(2,1)}), bf16[96,1792]{1,0:T(8,128)(2,1)}) %reduce-scatter.2.cloned.1.call-update) | async-done | bytes 344080 | tf_op jit(solution)/shard_map/reduce_scatter | solution.py:198
  294.9 1.9 add_convert_fusion.1
  (53 shorter events, 1.1 us)
Async XLA Ops:
  7.4 24.8 %copy-start = (bf16[3,224,1792]{2,1,0:T(8,128)(2,1)S(1)}, bf16[3,224,1792]{2,1,0:T(8,128)(2,1)}, u32[]{:S(2)}) copy-start(bf16[3,224,1792]{2,1,0:T(8,128)(2,1)} %param.16) | copy-start | bytes 7225348
  19.8 11.9 %copy-start.9 = (s32[1,24]{1,0:T(1,128)S(1)}, s32[1,24]{1,0:T(1,128)}, u32[]{:S(2)}) copy-start(s32[1,24]{1,0:T(1,128)} %param.25) | copy-start | bytes 292
  19.8 105.7 %all-to-all-start = ((bf16[32,2,64,448]{3,2,1,0:T(8,128)(2,1)}), bf16[32,2,64,448]{3,2,1,0:T(8,128)(2,1)}, u32[]{:S(2)}, u32[]{:S(2)}) async-start(bf16[32,2,64,448]{3,2,1,0:T(8,128)(2,1)} %bitcast.61), calls=%async_computation | async-start | bytes 8388608 | tf_op jit(solution)/shard_map/all_to_all | solution.py:141
  31.7 191.4 %all-reduce.2.cloned.1.call-start = ((), (), s32[]{:S(2)}) async-start(), calls=%async_computation.2 | async-start | bytes 5505024 | tf_op jit(solution)/shard_map/psum | solution.py:183
  32.2 5.4 %copy-start.7 = (s32[768]{0:T(1024)S(1)}, s32[768]{0:T(1024)}, u32[]{:S(2)}) copy-start(s32[768]{0:T(1024)} %param.24) | copy-start | bytes 9220
  32.2 5.4 %copy-start.4 = (bf16[8,1792,16]{1,2,0:T(8,128)(2,1)S(1)}, bf16[8,1792,16]{1,2,0:T(8,128)(2,1)}, u32[]{:S(2)}) copy-start(bf16[8,1792,16]{1,2,0:T(8,128)(2,1)} %param.18) | copy-start | bytes 1376260
  36.1 1.4 copy-start.2
  37.5 31.5 %copy-start.11 = (f32[4]{0:T(128)S(1)}, f32[4]{0:T(128)}, u32[]{:S(2)}) copy-start(f32[4]{0:T(128)} %param.20) | copy-start | bytes 52
  37.5 31.5 %copy-start.12 = (s32[24]{0:T(128)S(1)}, s32[24]{0:T(128)}, u32[]{:S(2)}) copy-start(s32[24]{0:T(128)} %param.26) | copy-start | bytes 292
  40.4 30.4 %copy-start.10 = (bf16[2,224,1024]{2,1,0:T(8,128)(2,1)S(1)}, bf16[2,224,1024]{2,1,0:T(8,128)(2,1)}, u32[]{:S(2)}) copy-start(bf16[2,224,1024]{2,1,0:T(8,128)(2,1)} %param.19) | copy-start | bytes 2752516
  129.1 1.6 copy-start.6
  130.8 9.6 %copy-start.5 = (bf16[768,2,112]{0,2,1:T(8,128)(2,1)S(1)}, bf16[768,2,112]{0,2,1:T(8,128)(2,1)}, u32[]{:S(2)}) copy-start(bf16[768,2,112]{0,2,1:T(8,128)(2,1)} %get-tuple-element.17) | copy-start | bytes 1032196
  140.3 7.6 %copy-start.3 = (bf16[224,1792]{1,0:T(8,128)(2,1)S(1)}, bf16[224,1792]{1,0:T(8,128)(2,1)}, u32[]{:S(2)}) copy-start(bf16[224,1792]{1,0:T(8,128)(2,1)} %param.17) | copy-start | bytes 2408452
  147.9 3.4 %copy-start.8 = (bf16[1792]{0:T(1024)(128)(2,1)S(1)}, bf16[1792]{0:T(1024)(128)(2,1)}, u32[]{:S(2)}) copy-start(bf16[1792]{0:T(1024)(128)(2,1)} %param.21) | copy-start | bytes 10756
  150.5 92.0 %all-gather.2.cloned.1.call-start = ((), (), s32[]{:S(2)}) async-start(), calls=%async_computation.3 | async-start | bytes 7096320 | tf_op jit(solution)/shard_map/all_gather | solution.py:189
  151.1 143.8 %reduce-scatter.2.cloned.1.call-start = ((), (), s32[]{:S(2)}) async-start(), calls=%async_computation.4 | async-start | bytes 3096576 | tf_op jit(solution)/shard_map/reduce_scatter | solution.py:198
  248.4 48.4 %copy-start.1 = (bf16[3,224,1792]{2,1,0:T(8,128)(2,1)S(1)}, bf16[3,224,1792]{2,1,0:T(8,128)(2,1)}, u32[]{:S(2)}) copy-start(bf16[3,224,1792]{2,1,0:T(8,128)(2,1)} %param.16) | copy-start | bytes 7225348
Sparse Core Ops, SparseCore 0:
  150.6 72.4 all-reduce.1
  259.0 35.7 reduce-scatter.1
Sparse Core Ops, SparseCore 1:
  154.0 88.5 all-gather.1
